TPU v7x, 128 devices: a whole 4x4x4 slice. The times are simulated.
128 devices in a mesh: rows: 32 (over x, y, core), grp: 4 (over z).
Axes of the slice: x: 4, y: 4, z: 4, core: 2. Of those that a mesh axis runs over, the one named last changes fastest.
Arguments:
- embeddings: bfloat16 [262144, 1024], P('rows', 'grp'), may hold values from -6 to 6
- fine_local: int32 [262144], P('rows'), may hold values from 0 to 2047
- send_counts: int32 [32, 32], P('rows'), may hold values from 0 to 512, as said below
- old_fine: bfloat16 [65536, 1024], P('rows', 'grp'), may hold values from -6 to 6
- coarse_ids: int32 [65536], P('rows'), may hold values from 0 to 8191, as said below
- old_coarse: bfloat16 [8192, 1024], P('rows', 'grp'), may hold values from -6 to 6
Outputs:
- new_fine: bfloat16 [65536, 1024], P('rows', 'grp')
- coarse_dirs: bfloat16 [8192, 1024], P('rows')
Inputs may be any that keep to these rules, and one draw needn't show every extreme that they name: Row d of send_counts splits the 8192 rows of block d, in order, into segments for owners 0, 1, ...; each row of send_counts sums to 8192; one owner receives exactly 512 rows from every block. `coarse_ids`: within each block of 2048 consecutive level-1 clusters, at most 128 have a level-2 cluster in any one block of 256 consecutive level-2 clusters; one such block reaches that from every block.
All inputs are finite; a program needn't handle non-finite values.
Results may differ from a plain program's by a relative error of at most 0.006.
Values may be sent and summed in bfloat16 or wider, within the bound.
No kernel may reach another device: no remote copies, remote signals or barrier semaphores. Data moves between devices by JAX's collectives and lax.ppermute only.
A program may use at most 64 MiB of HBM per device.

v0:
```python
import functools

import jax
import jax.numpy as jnp
from jax import lax
from jax.experimental import pallas as pl
from jax.experimental.pallas import tpu as pltpu
from jax.sharding import PartitionSpec as P


F32 = jnp.float32
BF16 = jnp.bfloat16
LANES = 128
TAIL = 8
SIDE = 4


def iota(shape, axis):
    return lax.broadcasted_iota(jnp.int32, shape, axis)


def device(x, y, core):
    return (x % SIDE) * 2 * SIDE + (y % SIDE) * 2 + core


CHIPS = [(x, y) for x in range(SIDE) for y in range(SIDE)]


def line_pairs(step, same_class):
    pairs = []
    for x, y in CHIPS:
        for core in range(2):
            kind = core if same_class else 1 - core
            to = device(x + step, y, 0) if kind == 0 else device(x, y + step, 1)
            pairs.append((device(x, y, core), to))
    return pairs


def cross_pairs(step):
    pairs = []
    for x, y in CHIPS:
        pairs.append((device(x, y, 0), device(x, y + step, 0)))
        pairs.append((device(x, y, 1), device(x + step, y, 1)))
    return pairs


def pack_body(slots, capacity, counts, emb, local, *rest):
    outs, (rows, labels, starts, done) = rest[: len(slots)], rest[len(slots) :]
    per_dev, width = emb.shape
    label_rows = local.shape[0]
    owners = counts.shape[1]
    at_step = pl.program_id(0)

    @pl.when(at_step == 0)
    def _():
        fetch = pltpu.make_async_copy(emb, rows.at[:per_dev, :], done)
        fetch.start()

        def add(o, total):
            starts[o] = total
            return total + counts[0, o]

        lax.fori_loop(0, owners, add, 0)
        labels[:label_rows, :] = local[...]
        labels[label_rows:, :] = jnp.zeros((16, LANES), jnp.int32)
        rows[per_dev:, :] = jnp.zeros((capacity + 16, width), BF16)
        fetch.wait()

    here = lax.axis_index("rows")
    x, y, core = here // (2 * SIDE), lax.rem(here // 2, SIDE), lax.rem(here, 2)
    line = iota((TAIL, LANES), 0) * LANES + iota((TAIL, LANES), 1)
    lane = iota((TAIL, LANES), 1)
    for (same_class, step, crosses), out in zip(slots, outs):

        @pl.when(at_step < len(crosses))
        def _():
            cross = at_step + crosses[0]
            kind = core if same_class else 1 - core
            along = lax.rem(x + jnp.where(kind == 0, step, cross), SIDE)
            over = lax.rem(y + jnp.where(kind == 0, cross, step), SIDE)
            owner = along * 2 * SIDE + over * 2 + kind
            first = starts[owner]
            count = counts[0, owner]
            aligned = first // 16
            turn = first - aligned * 16
            far = turn >= 8
            small = jnp.where(far, turn - 8, turn)
            turn_back = lax.rem(8 - small, 8)
            kept = iota((9, 8, width), 1) < 8 - small
            for at in range(0, capacity, 64):
                window = rows[pl.ds(pl.multiple_of(aligned * 16 + at, 16), 80), :]
                window = window.astype(F32).reshape(10, 8, width)
                window = pltpu.roll(window, turn_back, 1)
                moved = jnp.where(kept, window[:9], window[1:])
                moved = jnp.where(far, moved[1:], moved[:8])
                out[0, at : at + 64, :] = moved.reshape(64, width).astype(BF16)
            base = first // LANES
            shift = first - base * LANES
            got = [labels[pl.ds(base + i, 1), :] for i in range(TAIL + 1)]
            low_part = jnp.concatenate(got[:TAIL], axis=0)
            high_part = jnp.concatenate(got[1:], axis=0)
            back = lax.rem(LANES - shift, LANES)
            low_part = pltpu.roll(low_part, back, 1)
            high_part = pltpu.roll(high_part, back, 1)
            value = jnp.where(lane < LANES - shift, low_part, high_part)
            live = line < count
            high = jnp.where(live, lax.shift_right_logical(value, 7), 64).astype(F32)
            low = jnp.where(live, value & 127, 0).astype(F32)
            out[0, capacity:, :] = jnp.concatenate([high, low], axis=1).astype(BF16)


def pack(slots, send_counts, embeddings, local, capacity):
    per_dev, width = embeddings.shape
    tall = capacity + TAIL
    longest = max(len(c) for _, _, c in slots)

    def spec(length):
        return pl.BlockSpec((1, tall, width), lambda q: (jnp.minimum(q, length - 1), 0, 0))

    many = sum(len(c) for _, _, c in slots)
    return pl.pallas_call(
        functools.partial(pack_body, slots, capacity),
        grid=(longest,),
        out_shape=[jax.ShapeDtypeStruct((len(c), tall, width), BF16) for _, _, c in slots],
        in_specs=[
            pl.BlockSpec(memory_space=pltpu.SMEM),
            pl.BlockSpec(memory_space=pl.ANY),
            pl.BlockSpec(local.shape, lambda q: (0, 0)),
        ],
        out_specs=[spec(len(c)) for _, _, c in slots],
        scratch_shapes=[
            pltpu.VMEM((per_dev + capacity + 16, width), BF16),
            pltpu.VMEM((local.shape[0] + 16, LANES), jnp.int32),
            pltpu.SMEM((send_counts.shape[1],), jnp.int32),
            pltpu.SemaphoreType.DMA,
        ],
        cost_estimate=pl.CostEstimate(
            flops=0,
            bytes_accessed=per_dev * width * 2 + many * tall * width * 2,
            transcendentals=0,
        ),
        name="pack_rows",
    )(send_counts, embeddings, local)


def sums_body(sources, capacity, blocks, had, sent, *refs):
    arrived, refs = refs[:sources], refs[sources:]
    had_acc, had_counts = None, None
    if had:
        had_acc, had_counts, refs = refs[0], refs[1], refs[2:]
    if sent:
        out, low_hot, high_hot, onehot, data = refs
        out_counts = None
    else:
        out, out_counts, low_hot, high_hot, onehot, data = refs
    digits = high_hot.shape[0]
    depth = sources * capacity
    part = pl.program_id(1)
    size = onehot.shape[0]

    @pl.when(part == 0)
    def _():
        for s in range(sources):
            tail = arrived[s][0, capacity:, :].astype(F32)
            data[s * capacity : (s + 1) * capacity, :] = arrived[s][0, :capacity, :]
            for i in range(capacity // LANES):
                at = s * capacity + i * LANES
                high = tail[i : i + 1, :LANES]
                low = tail[i : i + 1, LANES : 2 * LANES]
                low_hot[:, at : at + LANES] = jnp.where(
                    iota((LANES, LANES), 0).astype(F32) == low, 1.0, 0.0
                ).astype(BF16)
                high_hot[:, at : at + LANES] = jnp.where(
                    iota((digits, LANES), 0).astype(F32) == high, 1.0, 0.0
                )
        counts = lax.dot_general(
            high_hot[...].astype(BF16),
            low_hot[...],
            (((1,), (1,)), ((), ())),
            preferred_element_type=F32,
        )
        if had_counts is not None:
            counts = counts + had_counts[0]
        if sent:
            tens = jnp.floor(counts / 64.0)
            out[blocks * size :, :] = jnp.concatenate(
                [tens, counts - 64.0 * tens], axis=1
            ).astype(BF16)
        else:
            out_counts[0] = counts

    group = size // LANES
    for h in range(group):
        row = high_hot[pl.ds(pl.multiple_of(part * group, group), group), :][h : h + 1, :]
        row = jnp.broadcast_to(row, (16, depth)).astype(BF16)
        for at in range(0, LANES, 16):
            onehot[h * LANES + at : h * LANES + at + 16, :] = low_hot[at : at + 16, :] * row
    total = jnp.dot(onehot[...], data[...], preferred_element_type=F32)
    if had_acc is not None:
        total = total + had_acc[0]
    if sent:
        out[pl.ds(pl.multiple_of(part * size, size), size), :] = total.astype(BF16)
    else:
        out[0] = total


def line_sums(arrived, capacity, fine_dev, crosses, had=None, send=False):
    width = arrived[0][0].shape[2]
    tall = capacity + TAIL
    sources = len(arrived)
    digits = fine_dev // LANES
    size = fine_dev // 2
    blocks = fine_dev // size
    many = len(crosses)

    def source(lowest):
        at = crosses[0] - lowest
        return pl.BlockSpec((1, tall, width), lambda q, m: (at + q, 0, 0))

    operands = [a for a, _ in arrived]
    in_specs = [source(lowest) for _, lowest in arrived]
    if had is not None:
        acc, counts, lowest = had
        at = crosses[0] - lowest
        operands += [acc, counts]
        in_specs += [
            pl.BlockSpec((1, size, width), lambda q, m: (at + q, m, 0)),
            pl.BlockSpec((1, digits, LANES), lambda q, m: (at + q, 0, 0)),
        ]
    if send:
        out_shape = jax.ShapeDtypeStruct((fine_dev + 16, width), BF16)
        out_specs = pl.BlockSpec((fine_dev + 16, width), lambda q, m: (0, 0))
    else:
        out_shape = (
            jax.ShapeDtypeStruct((many, fine_dev, width), F32),
            jax.ShapeDtypeStruct((many, digits, LANES), F32),
        )
        out_specs = (
            pl.BlockSpec((1, size, width), lambda q, m: (q, m, 0)),
            pl.BlockSpec((1, digits, LANES), lambda q, m: (q, 0, 0)),
        )
    return pl.pallas_call(
        functools.partial(sums_body, sources, capacity, blocks, had is not None, send),
        grid=(many, blocks),
        out_shape=out_shape,
        in_specs=in_specs,
        out_specs=out_specs,
        scratch_shapes=[
            pltpu.VMEM((LANES, sources * capacity), BF16),
            pltpu.VMEM((digits, sources * capacity), F32),
            pltpu.VMEM((size, sources * capacity), BF16),
            pltpu.VMEM((sources * capacity, width), BF16),
        ],
        cost_estimate=pl.CostEstimate(
            flops=2 * many * sources * capacity * fine_dev * width,
            bytes_accessed=many * (sources * tall * width * 2 + fine_dev * width * 8),
            transcendentals=0,
        ),
        name="line_sums",
    )(*operands)


def update_body(acc, counts, old, *refs):
    steps = SIDE - 1
    got, tails, new, column = refs[:steps], refs[steps : 2 * steps], refs[-2], refs[-1]
    digits = counts.shape[1]
    part = pl.program_id(0)
    group = old.shape[0] // LANES

    @pl.when(part == 0)
    def _():
        count = counts[0]
        for tail in tails:
            value = tail[...].astype(F32)
            count = count + value[:, :LANES] * 64.0 + value[:, LANES : 2 * LANES]
        tens = jnp.floor(count / 64.0)
        eye = jnp.where(iota((LANES, LANES), 0) == iota((LANES, LANES), 1), 1.0, 0.0)
        turn = lambda a: lax.dot_general(
            eye.astype(BF16), a.astype(BF16), (((1,), (1,)), ((), ())), preferred_element_type=F32
        )
        column[...] = turn(tens) * 64.0 + turn(count - 64.0 * tens)

    for p in range(digits // group):

        @pl.when(part == p)
        def _():
            for h in range(group):
                at = slice(h * LANES, (h + 1) * LANES)
                total = acc[0, at, :] + old[at, :].astype(F32)
                for g in got:
                    total = total + g[at, :].astype(F32)
                count = column[:, p * group + h : p * group + h + 1]
                new[at, :] = (total / (count + 1.0)).astype(BF16)


def update(acc, counts, old_fine, got):
    fine_dev, width = old_fine.shape
    digits = fine_dev // LANES
    size = fine_dev // 4
    return pl.pallas_call(
        update_body,
        grid=(fine_dev // size,),
        out_shape=jax.ShapeDtypeStruct((fine_dev, width), BF16),
        in_specs=[
            pl.BlockSpec((1, size, width), lambda m: (0, m, 0)),
            pl.BlockSpec((1, digits, LANES), lambda m: (0, 0, 0)),
            pl.BlockSpec((size, width), lambda m: (m, 0)),
        ]
        + [pl.BlockSpec((size, width), lambda m: (m, 0))] * len(got)
        + [pl.BlockSpec((16, width), lambda m: (fine_dev // 16, 0))] * len(got),
        out_specs=pl.BlockSpec((size, width), lambda m: (m, 0)),
        scratch_shapes=[pltpu.VMEM((LANES, digits), F32)],
        name="new_fine",
    )(acc, counts, old_fine, *got, *got)


def plan_body(coarse_dev, ids, owner_hot, rank_hot, labels):
    peers, fine_dev = owner_hot.shape
    value = ids[...]
    owner = value // coarse_dev
    local = (value - owner * coarse_dev).astype(F32)
    member = jnp.where(iota((peers, fine_dev), 0) == owner, 1.0, 0.0)
    owner_hot[...] = member
    step = 256
    before = jnp.where(iota((step, step), 0) < iota((step, step), 1), 1.0, 0.0).astype(BF16)
    carry = jnp.zeros((peers, 1), F32)
    for at in range(0, fine_dev, step):
        piece = member[:, at : at + step]
        prefix = jnp.dot(piece.astype(BF16), before, preferred_element_type=F32) + carry
        rank = jnp.sum(prefix * piece, axis=0, keepdims=True)
        carry = carry + jnp.sum(piece, axis=1, keepdims=True)
        hot = jnp.where(iota((rank_hot.shape[0], step), 0).astype(F32) == rank, 1.0, 0.0)
        rank_hot[:, at : at + step] = hot.astype(BF16)
    tagged = (member * (local + 1.0)).astype(BF16)
    labels[...] = lax.dot_general(
        tagged, rank_hot[...], (((1,), (1,)), ((), ())), preferred_element_type=F32
    )


def plan(coarse_ids, peers, capacity, coarse_dev):
    fine_dev = coarse_ids.shape[1]
    return pl.pallas_call(
        functools.partial(plan_body, coarse_dev),
        out_shape=(
            jax.ShapeDtypeStruct((peers, fine_dev), F32),
            jax.ShapeDtypeStruct((capacity, fine_dev), BF16),
            jax.ShapeDtypeStruct((peers, capacity), F32),
        ),
        name="plan_clusters",
    )(coarse_ids)


def place_body(group, owner_hot, rank_hot, tags, new, out, placement):
    capacity, fine_dev = rank_hot.shape
    for g in range(group):
        row = jnp.broadcast_to(owner_hot[g : g + 1, :], (16, fine_dev)).astype(BF16)
        for at in range(0, capacity, 16):
            top = g * capacity + at
            placement[top : top + 16, :] = rank_hot[at : at + 16, :] * row
    sent = jnp.dot(placement[...], new[...], preferred_element_type=F32).astype(BF16)
    for g in range(group):
        out[g, :capacity, :] = sent[g * capacity : (g + 1) * capacity, :]
        tag = jnp.broadcast_to(tags[g : g + 1, :], (TAIL, capacity))
        out[g, capacity:, :] = jnp.concatenate([tag, tag], axis=1).astype(BF16)


def place(owner_hot, rank_hot, tags, new_fine, group):
    peers, fine_dev = owner_hot.shape
    capacity = rank_hot.shape[0]
    width = new_fine.shape[1]
    whole = lambda a: pl.BlockSpec(a.shape, lambda i: (0, 0))
    return pl.pallas_call(
        functools.partial(place_body, group),
        grid=(peers // group,),
        out_shape=jax.ShapeDtypeStruct((peers, capacity + TAIL, width), BF16),
        in_specs=[
            pl.BlockSpec((group, fine_dev), lambda i: (i, 0)),
            whole(rank_hot),
            pl.BlockSpec((group, capacity), lambda i: (i, 0)),
            whole(new_fine),
        ],
        out_specs=pl.BlockSpec((group, capacity + TAIL, width), lambda i: (i, 0, 0)),
        scratch_shapes=[pltpu.VMEM((group * capacity, fine_dev), BF16)],
        name="place_clusters",
    )(owner_hot, rank_hot, tags, new_fine)


def coarse_body(received, old, means, onehot, data):
    peers, tall, _ = received.shape
    capacity = tall - TAIL
    coarse_dev = old.shape[0]
    total = jnp.zeros((coarse_dev, capacity), F32)
    row = iota((coarse_dev, capacity), 0).astype(F32) + 1.0
    for p in range(peers):
        tag = received[p, capacity:, :].astype(F32)[:1, :capacity]
        hot = jnp.where(row == tag, 1.0, 0.0)
        total = total + hot
        onehot[:, p * capacity : (p + 1) * capacity] = hot.astype(BF16)
        data[p * capacity : (p + 1) * capacity, :] = received[p, :capacity, :]
    sums = jnp.dot(onehot[...], data[...], preferred_element_type=F32)
    count = jnp.sum(total, axis=1, keepdims=True)
    means[...] = ((sums + old[...].astype(F32)) / (count + 1.0)).astype(BF16)


def coarse(received, old_coarse):
    peers, tall, width = received.shape
    deep = peers * (tall - TAIL)
    return pl.pallas_call(
        coarse_body,
        out_shape=jax.ShapeDtypeStruct(old_coarse.shape, BF16),
        scratch_shapes=[
            pltpu.VMEM((old_coarse.shape[0], deep), BF16),
            pltpu.VMEM((deep, width), BF16),
        ],
        name="coarse_means",
    )(received, old_coarse)


def finish_body(groups, at, *refs):
    pieces, out, full = refs[:groups], refs[groups], refs[groups + 1]
    width = pieces[0].shape[1]
    for step in range(groups):
        place = lax.rem(at[0] + step, groups) * width
        full[:, pl.ds(pl.multiple_of(place, width), width)] = pieces[step][...].astype(F32)
    whole = full[...]
    scale = lax.rsqrt(jnp.mean(whole * whole, axis=1, keepdims=True) + 1e-06)
    out[...] = (whole * scale).astype(BF16)


def finish(at, pieces):
    groups = len(pieces)
    rows, width = pieces[0].shape
    return pl.pallas_call(
        functools.partial(finish_body, groups),
        out_shape=jax.ShapeDtypeStruct((rows, groups * width), BF16),
        in_specs=[pl.BlockSpec(memory_space=pltpu.SMEM)]
        + [pl.BlockSpec(memory_space=pltpu.VMEM)] * groups,
        scratch_shapes=[pltpu.VMEM((rows, groups * width), F32)],
        name="coarse_dirs",
    )(at, *pieces)


def exchange(slots):
    return lax.all_to_all(slots, "rows", split_axis=0, concat_axis=0, tiled=True)


def level_step(embeddings, fine_local, send_counts, old_fine, coarse_ids, old_coarse):
    peers = lax.axis_size("rows")
    groups = lax.axis_size("grp")
    per_dev = embeddings.shape[0]
    fine_dev = old_fine.shape[0]
    coarse_dev = old_coarse.shape[0]
    capacity = 2 * per_dev // peers
    capacity_two = 2 * fine_dev // peers
    local = fine_local.reshape(-1, LANES)
    steps = range(1, SIDE)

    def along(slots, step, same_class):
        return lax.ppermute(slots, "rows", line_pairs(step, same_class))

    rows = (send_counts, embeddings, local, capacity)
    sent, own = tuple(steps), (0,)
    order = (2, 1, 3)

    keep = pack([(True, s, sent) for s in order], *rows)
    kept = [along(a, s, True) for s, a in zip(order, keep)]
    more = pack(
        [(False, s, sent) for s in order]
        + [(False, 0, own + sent), (True, 0, own + sent)]
        + [(k, s, own) for k in (True, False) for s in order],
        *rows,
    )
    swapped = along(more[3], 0, False)
    given = [along(a, s, False) for s, a in zip(order, more[:3])]
    kept_own = [along(a, s, True) for s, a in zip(order, more[5:8])]
    given_own = [along(a, s, False) for s, a in zip(order, more[8:])]
    owner_hot, rank_hot, tags = plan(
        coarse_ids.reshape(1, -1), peers, capacity_two, coarse_dev
    )
    near = [(more[4], 0), (swapped, 0)]
    had = line_sums(near + [(a, 1) for a in kept], capacity, fine_dev, sent)
    got = {}
    for cross in order:
        part = line_sums(
            [(a, 1) for a in given], capacity, fine_dev, (cross,), (*had, 1), send=True
        )
        got[cross] = lax.ppermute(part, "rows", cross_pairs(cross))
    acc, counts = line_sums(
        near + [(a, 0) for a in kept_own + given_own], capacity, fine_dev, own
    )
    new_fine = update(acc, counts, old_fine, [got[c] for c in steps])

    received = exchange(place(owner_hot, rank_hot, tags, new_fine, 8))
    means = coarse(received, old_coarse)
    pieces = [means]
    for step in range(1, groups):
        back = [((g + step) % groups, g) for g in range(groups)]
        pieces.append(lax.ppermute(means, "grp", back))
    at = lax.axis_index("grp").astype(jnp.int32).reshape(1)
    return (new_fine, finish(at, pieces))


def solution(mesh):
    in_specs = (
        P("rows", "grp"),
        P("rows"),
        P("rows", None),
        P("rows", "grp"),
        P("rows"),
        P("rows", "grp"),
    )
    out_specs = (P("rows", "grp"), P("rows", None))
    return jax.shard_map(
        level_step, mesh=mesh, in_specs=in_specs, out_specs=out_specs, check_vma=False
    )
```

profile of v0, /device:TPU:0, one launch (start us, length us, event | category | flops | bytes accessed | tf_op | source)
XLA Modules:
  0.0 198.5 jit_solution(6703072208002613872)
XLA Ops:
  0.6 7.8 %pack_rows.2 = (bf16[3,520,256]{2,1,0:T(8,128)(2,1)}, bf16[3,520,256]{2,1,0:T(8,128)(2,1)}, bf16[3,520,256]{2,1,0:T(8,128)(2,1)}, bf16[4,520,256]{2,1,0:T(8,128)...) custom-call(s32[1,32]{1,0:T(1,128)} %counts.3, ...), custom_call_target="tpu_custom_call" | custom-call | bytes 10317824 | tf_op jit(solution)/shard_map/pack_rows/pallas_call | solution.py:121
  8.5 5.5 %pack_rows.3 = (bf16[3,520,256]{2,1,0:T(8,128)(2,1)}, bf16[3,520,256]{2,1,0:T(8,128)(2,1)}, bf16[3,520,256]{2,1,0:T(8,128)(2,1)}) custom-call(s32[1,32]{1,0:T(1,128)} %counts.3, bf16[8192,256]{1,0:T(8,128)(2,1)} %emb.3, s32[64,128]{1,0:T(8,128)} %bitcast.4), custom_call_target="tpu_custom_call" | custom-call | bytes 6590464 | tf_op jit(solution)/shard_map/pack_rows/pallas_call | solution.py:121
  14.0 3.2 %collective-permute-start.10 = (bf16[3,520,256]{2,1,0:T(8,128)(2,1)}, bf16[3,520,256]{2,1,0:T(8,128)(2,1)S(1)}, u32[]{:S(2)}, u32[]{:S(2)}) collective-permute-start(bf16[3,520,256]{2,1,0:T(8,128)(2,1)} %get-tuple-element.36), channel_id=1, source_target_pairs={{0,64},{4,20},{8,72},{12,28},{16,80},{20,4},{24,88},{28,12},{32,96... | collective-permute-start | bytes 2396168 | tf_op jit(solution)/shard_map/ppermute | solution.py:459
  17.8 2.6 %collective-permute-start.12 = (bf16[3,520,256]{2,1,0:T(8,128)(2,1)}, bf16[3,520,256]{2,1,0:T(8,128)(2,1)S(1)}, u32[]{:S(2)}, u32[]{:S(2)}) collective-permute-start(bf16[3,520,256]{2,1,0:T(8,128)(2,1)} %get-tuple-element.38), channel_id=1, source_target_pairs={{0,96},{4,28},{8,104},{12,4},{16,112},{20,12},{24,120},{28,20},{32... | collective-permute-start | bytes 2396168 | tf_op jit(solution)/shard_map/ppermute | solution.py:459
  20.5 13.0 %collective-permute-done.10.refs_2_ = bf16[3,520,256]{2,1,0:T(8,128)(2,1)S(1)} collective-permute-done((bf16[3,520,256]{2,1,0:T(8,128)(2,1)}, bf16[3,520,256]{2,1,0:T(8,128)(2,1)S(1)}, u32[]{:S(2)}, u32[]{:S(2)}) %collective-permute-start.10) | collective-permute-done | bytes 798752 | tf_op jit(solution)/shard_map/ppermute | solution.py:459
  34.4 16.2 %collective-permute-done.11.refs_3_ = bf16[3,520,256]{2,1,0:T(8,128)(2,1)S(1)} collective-permute-done((bf16[3,520,256]{2,1,0:T(8,128)(2,1)}, bf16[3,520,256]{2,1,0:T(8,128)(2,1)S(1)}, u32[]{:S(2)}, u32[]{:S(2)}) %collective-permute-start.11) | collective-permute-done | bytes 798752 | tf_op jit(solution)/shard_map/ppermute | solution.py:459
  51.5 2.3 %collective-permute-start.1 = (bf16[1,520,256]{2,1,0:T(8,128)(2,1)}, bf16[1,520,256]{2,1,0:T(8,128)(2,1)}, u32[]{:S(2)}, u32[]{:S(2)}) collective-permute-start(bf16[1,520,256]{2,1,0:T(8,128)(2,1)} %get-tuple-element.25), channel_id=1, source_target_pairs={{0,64},{4,20},{8,72},{12,28},{16,80},{20,4},{24,88},{28,12},{32,96... | collective-permute-start | bytes 798728 | tf_op jit(solution)/shard_map/ppermute | solution.py:459
  55.0 12.9 %line_sums.6 = (f32[3,2048,256]{2,1,0:T(8,128)}, f32[3,16,128]{2,1,0:T(8,128)}) custom-call(bf16[4,520,256]{2,1,0:T(8,128)(2,1)} %get-tuple-element.23.refs_0_, bf16[4,520,256]{2,1,0:T(8,128)(2,1)} %copy-done.9, bf16[3,520,256]{2,1,0:T(8,128)(2,1)} %copy-done.10, bf16[3,520,256]{2,1,0:T(8,128)(2,1)} %copy-done.11, bf16[3,520,256]{2,1,0:T(8,128)(2,1)} %copy-done.12), custom_call_target="tpu_custom_call" | custom-call | flops 8053063680 | bytes 16576512 | tf_op jit(solution)/shard_map/line_sums/pallas_call | solution.py:242
  69.4 4.7 %line_sums.7 = bf16[2064,256]{1,0:T(8,128)(2,1)} custom-call(bf16[3,520,256]{2,1,0:T(8,128)(2,1)} %copy-done, bf16[3,520,256]{2,1,0:T(8,128)(2,1)} %copy-done.1, bf16[3,520,256]{2,1,0:T(8,128)(2,1)} %copy-done.2, f32[3,2048,256]{2,1,0:T(8,128)} %get-tuple-element.39.refs_3_, f32[3,16,128]{2,1,0:T(8,128)} %get-tuple-element.40.refs_4_), custom_call_target="tpu_custom_call" | custom-call | flops 1610612736 | bytes 4993024 | tf_op jit(solution)/shard_map/line_sums/pallas_call | solution.py:242
  75.8 4.7 %line_sums.8 = bf16[2064,256]{1,0:T(8,128)(2,1)} custom-call(bf16[3,520,256]{2,1,0:T(8,128)(2,1)} %copy-done, bf16[3,520,256]{2,1,0:T(8,128)(2,1)} %copy-done.1, bf16[3,520,256]{2,1,0:T(8,128)(2,1)} %copy-done.2, f32[3,2048,256]{2,1,0:T(8,128)} %get-tuple-element.39.refs_3_, f32[3,16,128]{2,1,0:T(8,128)} %get-tuple-element.40.refs_4_), custom_call_target="tpu_custom_call" | custom-call | flops 1610612736 | bytes 4993024 | tf_op jit(solution)/shard_map/line_sums/pallas_call | solution.py:242
  80.5 2.9 %collective-permute-start.14 = (bf16[2064,256]{1,0:T(8,128)(2,1)}, bf16[2064,256]{1,0:T(8,128)(2,1)S(1)}, u32[]{:S(2)}, u32[]{:S(2)}) collective-permute-start(bf16[2064,256]{1,0:T(8,128)(2,1)} %line_sums.8), channel_id=1, source_target_pairs={{0,16},{4,68},{8,24},{12,76},{16,0},{20,84},{24,8},{28,92},{32,48}... | collective-permute-start | bytes 3170312 | tf_op jit(solution)/shard_map/ppermute | solution.py:487
  83.4 4.7 %line_sums.9 = bf16[2064,256]{1,0:T(8,128)(2,1)} custom-call(bf16[3,520,256]{2,1,0:T(8,128)(2,1)} %copy-done, bf16[3,520,256]{2,1,0:T(8,128)(2,1)} %copy-done.1, bf16[3,520,256]{2,1,0:T(8,128)(2,1)} %copy-done.2, f32[3,2048,256]{2,1,0:T(8,128)} %get-tuple-element.39.refs_3_, f32[3,16,128]{2,1,0:T(8,128)} %get-tuple-element.40.refs_4_), custom_call_target="tpu_custom_call" | custom-call | flops 1610612736 | bytes 4993024 | tf_op jit(solution)/shard_map/line_sums/pallas_call | solution.py:242
  90.2 2.2 %collective-permute-start.3 = (bf16[1,520,256]{2,1,0:T(8,128)(2,1)}, bf16[1,520,256]{2,1,0:T(8,128)(2,1)S(1)}, u32[]{:S(2)}, u32[]{:S(2)}) collective-permute-start(bf16[1,520,256]{2,1,0:T(8,128)(2,1)} %get-tuple-element.27), channel_id=1, source_target_pairs={{0,96},{4,28},{8,104},{12,4},{16,112},{20,12},{24,120},{28,20},{32... | collective-permute-start | bytes 798728 | tf_op jit(solution)/shard_map/ppermute | solution.py:459
  92.7 8.7 %collective-permute-done.3.refs_4_ = bf16[1,520,256]{2,1,0:T(8,128)(2,1)S(1)} collective-permute-done((bf16[1,520,256]{2,1,0:T(8,128)(2,1)}, bf16[1,520,256]{2,1,0:T(8,128)(2,1)S(1)}, u32[]{:S(2)}, u32[]{:S(2)}) %collective-permute-start.3) | collective-permute-done | bytes 266272 | tf_op jit(solution)/shard_map/ppermute | solution.py:459
  101.4 3.5 %collective-permute-start.5 = (bf16[1,520,256]{2,1,0:T(8,128)(2,1)}, bf16[1,520,256]{2,1,0:T(8,128)(2,1)}, u32[]{:S(2)}, u32[]{:S(2)}) collective-permute-start(bf16[1,520,256]{2,1,0:T(8,128)(2,1)} %get-tuple-element.29), channel_id=1, source_target_pairs={{0,12},{4,32},{8,20},{12,40},{16,28},{20,48},{24,4},{28,56},{32,44... | collective-permute-start | bytes 798728 | tf_op jit(solution)/shard_map/ppermute | solution.py:459
  106.0 9.1 %collective-permute-start.6 = (bf16[1,520,256]{2,1,0:T(8,128)(2,1)S(1)}, bf16[1,520,256]{2,1,0:T(8,128)(2,1)}, u32[]{:S(2)}, u32[]{:S(2)}) collective-permute-start(bf16[1,520,256]{2,1,0:T(8,128)(2,1)S(1)} %copy-done.13), channel_id=1, source_target_pairs={{0,28},{4,96},{8,4},{12,104},{16,12},{20,112},{24,20},{28,120},{32... | collective-permute-start | bytes 798728 | tf_op jit(solution)/shard_map/ppermute | solution.py:459
  119.0 7.8 %line_sums.5 = (f32[1,2048,256]{2,1,0:T(8,128)}, f32[1,16,128]{2,1,0:T(8,128)}) custom-call(bf16[4,520,256]{2,1,0:T(8,128)(2,1)} %get-tuple-element.23.refs_0_, bf16[4,520,256]{2,1,0:T(8,128)(2,1)} %copy-done.9, bf16[1,520,256]{2,1,0:T(8,128)(2,1)} %collective-permute-done.1.refs_2_, bf16[1,520,256]{2,1,0:T(8,128)(2,1)} %collective-permute-done.2.refs_3_, ...), custom_call_target="tpu_custom_call" | custom-call | flops 4294967296 | bytes 6324224 | tf_op jit(solution)/shard_map/line_sums/pallas_call | solution.py:242
  128.5 4.7 %new_fine.1.new = bf16[2048,256]{1,0:T(8,128)(2,1)} custom-call(f32[1,2048,256]{2,1,0:T(8,128)} %get-tuple-element.31.acc, f32[1,16,128]{2,1,0:T(8,128)} %get-tuple-element.32.counts, bf16[2048,256]{1,0:T(8,128)(2,1)} %old.2, bf16[2064,256]{1,0:T(8,128)(2,1)} %copy-done.3, bf16[2064,256]{1,0:T(8,128)(2,1)} %copy-done.4, bf16[2064,256]{1,0:T(8,128)(2,1)} %copy-done.5, ...), custom_call_target="tpu_custom_call" | custom-call | tf_op jit(solution)/shard_map/new_fine/pallas_call | solution.py:300
  133.2 7.3 %place_clusters.1 = bf16[32,136,256]{2,1,0:T(8,128)(2,1)} custom-call(f32[32,2048]{1,0:T(8,128)} %get-tuple-element.41.owner_hot, bf16[128,2048]{1,0:T(8,128)(2,1)} %get-tuple-element.42.rank_hot, f32[32,128]{1,0:T(8,128)} %get-tuple-element.43.tags, bf16[2048,256]{1,0:T(8,128)(2,1)} %new_fine.1.new), custom_call_target="tpu_custom_call" | custom-call | tf_op jit(solution)/shard_map/place_clusters/pallas_call | solution.py:372
  140.6 38.2 %all_to_all.5.received = bf16[32,136,256]{2,1,0:T(8,128)(2,1)} all-to-all(bf16[32,136,256]{2,1,0:T(8,128)(2,1)} %place_clusters.1), channel_id=1, replica_groups=mesh['rows'=32,'grp'=4] {'rows'}, dimensions={0} | all-to-all | bytes 4456448 | tf_op jit(solution)/shard_map/all_to_all | solution.py:444
  178.7 3.5 %coarse_means.1.refs_0_ = bf16[256,256]{1,0:T(8,128)(2,1)} custom-call(bf16[32,136,256]{2,1,0:T(8,128)(2,1)} %all_to_all.5.received, bf16[256,256]{1,0:T(8,128)(2,1)} %old.3), custom_call_target="tpu_custom_call" | custom-call | tf_op jit(solution)/shard_map/coarse_means/pallas_call | solution.py:408
  182.2 4.0 %collective-permute-start.16 = (bf16[256,256]{1,0:T(8,128)(2,1)}, bf16[256,256]{1,0:T(8,128)(2,1)S(1)}, u32[]{:S(2)}, u32[]{:S(2)}) collective-permute-start(bf16[256,256]{1,0:T(8,128)(2,1)} %coarse_means.1.refs_0_), channel_id=1, source_target_pairs={{1,0},{2,1},{3,2},{0,3},{5,4},{6,5},{7,6},{4,7},{9,8},{10,9},{11,1... | collective-permute-start | bytes 393224 | tf_op jit(solution)/shard_map/ppermute | solution.py:498
  187.5 4.9 %collective-permute-done.16.refs_1_ = bf16[256,256]{1,0:T(8,128)(2,1)S(1)} collective-permute-done((bf16[256,256]{1,0:T(8,128)(2,1)}, bf16[256,256]{1,0:T(8,128)(2,1)S(1)}, u32[]{:S(2)}, u32[]{:S(2)}) %collective-permute-start.16) | collective-permute-done | bytes 131104 | tf_op jit(solution)/shard_map/ppermute | solution.py:498
  196.3 2.2 %coarse_dirs.1 = bf16[256,1024]{1,0:T(8,128)(2,1)} custom-call(s32[1]{0:T(128)} %bitcast.1.at, bf16[256,256]{1,0:T(8,128)(2,1)} %coarse_means.1.refs_0_, bf16[256,256]{1,0:T(8,128)(2,1)} %copy-done.6, bf16[256,256]{1,0:T(8,128)(2,1)} %copy-done.7, bf16[256,256]{1,0:T(8,128)(2,1)} %copy-done.8), custom_call_target="tpu_custom_call" | custom-call | tf_op jit(solution)/shard_map/coarse_dirs/pallas_call | solution.py:433
  (59 shorter events, 21.0 us)
Async XLA Ops:
  8.4 45.5 %collective-permute-start = (bf16[4,520,256]{2,1,0:T(8,128)(2,1)}, bf16[4,520,256]{2,1,0:T(8,128)(2,1)S(1)}, u32[]{:S(2)}, u32[]{:S(2)}) collective-permute-start(bf16[4,520,256]{2,1,0:T(8,128)(2,1)} %get-tuple-element.24), channel_id=1, source_target_pairs={{0,4},{4,0},{8,12},{12,8},{16,20},{20,16},{24,28},{28,24},{32,36},... | collective-permute-start | bytes 3194888 | tf_op jit(solution)/shard_map/ppermute | solution.py:459
  14.0 19.5 %collective-permute-start.10 = (bf16[3,520,256]{2,1,0:T(8,128)(2,1)}, bf16[3,520,256]{2,1,0:T(8,128)(2,1)S(1)}, u32[]{:S(2)}, u32[]{:S(2)}) collective-permute-start(bf16[3,520,256]{2,1,0:T(8,128)(2,1)} %get-tuple-element.36), channel_id=1, source_target_pairs={{0,64},{4,20},{8,72},{12,28},{16,80},{20,4},{24,88},{28,12},{32,96... | collective-permute-start | bytes 2396168 | tf_op jit(solution)/shard_map/ppermute | solution.py:459
  17.2 33.4 %collective-permute-start.11 = (bf16[3,520,256]{2,1,0:T(8,128)(2,1)}, bf16[3,520,256]{2,1,0:T(8,128)(2,1)S(1)}, u32[]{:S(2)}, u32[]{:S(2)}) collective-permute-start(bf16[3,520,256]{2,1,0:T(8,128)(2,1)} %get-tuple-element.37), channel_id=1, source_target_pairs={{0,32},{4,12},{8,40},{12,20},{16,48},{20,28},{24,56},{28,4},{32,64... | collective-permute-start | bytes 2396168 | tf_op jit(solution)/shard_map/ppermute | solution.py:459
  17.8 33.7 %collective-permute-start.12 = (bf16[3,520,256]{2,1,0:T(8,128)(2,1)}, bf16[3,520,256]{2,1,0:T(8,128)(2,1)S(1)}, u32[]{:S(2)}, u32[]{:S(2)}) collective-permute-start(bf16[3,520,256]{2,1,0:T(8,128)(2,1)} %get-tuple-element.38), channel_id=1, source_target_pairs={{0,96},{4,28},{8,104},{12,4},{16,112},{20,12},{24,120},{28,20},{32... | collective-permute-start | bytes 2396168 | tf_op jit(solution)/shard_map/ppermute | solution.py:459
  20.5 47.5 %collective-permute-start.7 = (bf16[3,520,256]{2,1,0:T(8,128)(2,1)}, bf16[3,520,256]{2,1,0:T(8,128)(2,1)S(1)}, u32[]{:S(2)}, u32[]{:S(2)}) collective-permute-start(bf16[3,520,256]{2,1,0:T(8,128)(2,1)} %get-tuple-element.33), channel_id=1, source_target_pairs={{0,20},{4,64},{8,28},{12,72},{16,4},{20,80},{24,12},{28,88},{32,52... | collective-permute-start | bytes 2396168 | tf_op jit(solution)/shard_map/ppermute | solution.py:459
  34.4 33.5 %collective-permute-start.8 = (bf16[3,520,256]{2,1,0:T(8,128)(2,1)}, bf16[3,520,256]{2,1,0:T(8,128)(2,1)S(1)}, u32[]{:S(2)}, u32[]{:S(2)}) collective-permute-start(bf16[3,520,256]{2,1,0:T(8,128)(2,1)} %get-tuple-element.34), channel_id=1, source_target_pairs={{0,12},{4,32},{8,20},{12,40},{16,28},{20,48},{24,4},{28,56},{32,44... | collective-permute-start | bytes 2396168 | tf_op jit(solution)/shard_map/ppermute | solution.py:459
  51.5 16.4 %collective-permute-start.9 = (bf16[3,520,256]{2,1,0:T(8,128)(2,1)}, bf16[3,520,256]{2,1,0:T(8,128)(2,1)S(1)}, u32[]{:S(2)}, u32[]{:S(2)}) collective-permute-start(bf16[3,520,256]{2,1,0:T(8,128)(2,1)} %get-tuple-element.35), channel_id=1, source_target_pairs={{0,28},{4,96},{8,4},{12,104},{16,12},{20,112},{24,20},{28,120},{32... | collective-permute-start | bytes 2396168 | tf_op jit(solution)/shard_map/ppermute | solution.py:459
  51.5 2.3 %copy-start.12 = (bf16[3,520,256]{2,1,0:T(8,128)(2,1)}, bf16[3,520,256]{2,1,0:T(8,128)(2,1)S(1)}, u32[]{:S(2)}) copy-start(bf16[3,520,256]{2,1,0:T(8,128)(2,1)S(1)} %collective-permute-done.12.refs_4_) | copy-start | bytes 2396164
  51.5 38.7 %collective-permute-start.1 = (bf16[1,520,256]{2,1,0:T(8,128)(2,1)}, bf16[1,520,256]{2,1,0:T(8,128)(2,1)}, u32[]{:S(2)}, u32[]{:S(2)}) collective-permute-start(bf16[1,520,256]{2,1,0:T(8,128)(2,1)} %get-tuple-element.25), channel_id=1, source_target_pairs={{0,64},{4,20},{8,72},{12,28},{16,80},{20,4},{24,88},{28,12},{32,96... | collective-permute-start | bytes 798728 | tf_op jit(solution)/shard_map/ppermute | solution.py:459
  53.9 38.5 %collective-permute-start.2 = (bf16[1,520,256]{2,1,0:T(8,128)(2,1)}, bf16[1,520,256]{2,1,0:T(8,128)(2,1)}, u32[]{:S(2)}, u32[]{:S(2)}) collective-permute-start(bf16[1,520,256]{2,1,0:T(8,128)(2,1)} %get-tuple-element.26), channel_id=1, source_target_pairs={{0,32},{4,12},{8,40},{12,20},{16,48},{20,28},{24,56},{28,4},{32,64... | collective-permute-start | bytes 798728 | tf_op jit(solution)/shard_map/ppermute | solution.py:459
  74.1 52.7 %collective-permute-start.13 = (bf16[2064,256]{1,0:T(8,128)(2,1)}, bf16[2064,256]{1,0:T(8,128)(2,1)S(1)}, u32[]{:S(2)}, u32[]{:S(2)}) collective-permute-start(bf16[2064,256]{1,0:T(8,128)(2,1)} %line_sums.7), channel_id=1, source_target_pairs={{0,8},{4,36},{8,16},{12,44},{16,24},{20,52},{24,0},{28,60},{32,40}... | collective-permute-start | bytes 3170312 | tf_op jit(solution)/shard_map/ppermute | solution.py:487
  80.5 25.6 %copy-start.13 = (bf16[1,520,256]{2,1,0:T(8,128)(2,1)S(1)}, bf16[1,520,256]{2,1,0:T(8,128)(2,1)}, u32[]{:S(2)}) copy-start(bf16[1,520,256]{2,1,0:T(8,128)(2,1)} %get-tuple-element.30) | copy-start | bytes 798724
  80.5 46.3 %collective-permute-start.14 = (bf16[2064,256]{1,0:T(8,128)(2,1)}, bf16[2064,256]{1,0:T(8,128)(2,1)S(1)}, u32[]{:S(2)}, u32[]{:S(2)}) collective-permute-start(bf16[2064,256]{1,0:T(8,128)(2,1)} %line_sums.8), channel_id=1, source_target_pairs={{0,16},{4,68},{8,24},{12,76},{16,0},{20,84},{24,8},{28,92},{32,48}... | collective-permute-start | bytes 3170312 | tf_op jit(solution)/shard_map/ppermute | solution.py:487
  88.1 38.7 %collective-permute-start.15 = (bf16[2064,256]{1,0:T(8,128)(2,1)}, bf16[2064,256]{1,0:T(8,128)(2,1)S(1)}, u32[]{:S(2)}, u32[]{:S(2)}) collective-permute-start(bf16[2064,256]{1,0:T(8,128)(2,1)} %line_sums.9), channel_id=1, source_target_pairs={{0,24},{4,100},{8,0},{12,108},{16,8},{20,116},{24,16},{28,124},{32... | collective-permute-start | bytes 3170312 | tf_op jit(solution)/shard_map/ppermute | solution.py:487
  90.2 11.2 %collective-permute-start.3 = (bf16[1,520,256]{2,1,0:T(8,128)(2,1)}, bf16[1,520,256]{2,1,0:T(8,128)(2,1)S(1)}, u32[]{:S(2)}, u32[]{:S(2)}) collective-permute-start(bf16[1,520,256]{2,1,0:T(8,128)(2,1)} %get-tuple-element.27), channel_id=1, source_target_pairs={{0,96},{4,28},{8,104},{12,4},{16,112},{20,12},{24,120},{28,20},{32... | collective-permute-start | bytes 798728 | tf_op jit(solution)/shard_map/ppermute | solution.py:459
  92.4 13.6 %collective-permute-start.4 = (bf16[1,520,256]{2,1,0:T(8,128)(2,1)}, bf16[1,520,256]{2,1,0:T(8,128)(2,1)S(1)}, u32[]{:S(2)}, u32[]{:S(2)}) collective-permute-start(bf16[1,520,256]{2,1,0:T(8,128)(2,1)} %get-tuple-element.28), channel_id=1, source_target_pairs={{0,20},{4,64},{8,28},{12,72},{16,4},{20,80},{24,12},{28,88},{32,52... | collective-permute-start | bytes 798728 | tf_op jit(solution)/shard_map/ppermute | solution.py:459
  101.4 13.7 %copy-start.14 = (bf16[1,520,256]{2,1,0:T(8,128)(2,1)}, bf16[1,520,256]{2,1,0:T(8,128)(2,1)S(1)}, u32[]{:S(2)}) copy-start(bf16[1,520,256]{2,1,0:T(8,128)(2,1)S(1)} %collective-permute-done.3.refs_4_) | copy-start | bytes 798724
  101.4 15.6 %collective-permute-start.5 = (bf16[1,520,256]{2,1,0:T(8,128)(2,1)}, bf16[1,520,256]{2,1,0:T(8,128)(2,1)}, u32[]{:S(2)}, u32[]{:S(2)}) collective-permute-start(bf16[1,520,256]{2,1,0:T(8,128)(2,1)} %get-tuple-element.29), channel_id=1, source_target_pairs={{0,12},{4,32},{8,20},{12,40},{16,28},{20,48},{24,4},{28,56},{32,44... | collective-permute-start | bytes 798728 | tf_op jit(solution)/shard_map/ppermute | solution.py:459
  106.0 9.1 %copy-start.15 = (bf16[1,520,256]{2,1,0:T(8,128)(2,1)}, bf16[1,520,256]{2,1,0:T(8,128)(2,1)S(1)}, u32[]{:S(2)}) copy-start(bf16[1,520,256]{2,1,0:T(8,128)(2,1)S(1)} %collective-permute-done.4.refs_5_) | copy-start | bytes 798724
  106.0 13.0 %collective-permute-start.6 = (bf16[1,520,256]{2,1,0:T(8,128)(2,1)S(1)}, bf16[1,520,256]{2,1,0:T(8,128)(2,1)}, u32[]{:S(2)}, u32[]{:S(2)}) collective-permute-start(bf16[1,520,256]{2,1,0:T(8,128)(2,1)S(1)} %copy-done.13), channel_id=1, source_target_pairs={{0,28},{4,96},{8,4},{12,104},{16,12},{20,112},{24,20},{28,120},{32... | collective-permute-start | bytes 798728 | tf_op jit(solution)/shard_map/ppermute | solution.py:459
  182.2 10.2 %collective-permute-start.16 = (bf16[256,256]{1,0:T(8,128)(2,1)}, bf16[256,256]{1,0:T(8,128)(2,1)S(1)}, u32[]{:S(2)}, u32[]{:S(2)}) collective-permute-start(bf16[256,256]{1,0:T(8,128)(2,1)} %coarse_means.1.refs_0_), channel_id=1, source_target_pairs={{1,0},{2,1},{3,2},{0,3},{5,4},{6,5},{7,6},{4,7},{9,8},{10,9},{11,1... | collective-permute-start | bytes 393224 | tf_op jit(solution)/shard_map/ppermute | solution.py:498
  186.2 8.1 %collective-permute-start.17 = (bf16[256,256]{1,0:T(8,128)(2,1)}, bf16[256,256]{1,0:T(8,128)(2,1)S(1)}, u32[]{:S(2)}, u32[]{:S(2)}) collective-permute-start(bf16[256,256]{1,0:T(8,128)(2,1)} %coarse_means.1.refs_0_), channel_id=1, source_target_pairs={{2,0},{3,1},{0,2},{1,3},{6,4},{7,5},{4,6},{5,7},{10,8},{11,9},{8,1... | collective-permute-start | bytes 393224 | tf_op jit(solution)/shard_map/ppermute | solution.py:498
  186.2 9.5 %collective-permute-start.18 = (bf16[256,256]{1,0:T(8,128)(2,1)}, bf16[256,256]{1,0:T(8,128)(2,1)S(1)}, u32[]{:S(2)}, u32[]{:S(2)}) collective-permute-start(bf16[256,256]{1,0:T(8,128)(2,1)} %coarse_means.1.refs_0_), channel_id=1, source_target_pairs={{3,0},{0,1},{1,2},{2,3},{7,4},{4,5},{5,6},{6,7},{11,8},{8,9},{9,10... | collective-permute-start | bytes 393224 | tf_op jit(solution)/shard_map/ppermute | solution.py:498
  192.4 3.3 %copy-start.6 = (bf16[256,256]{1,0:T(8,128)(2,1)}, bf16[256,256]{1,0:T(8,128)(2,1)S(1)}, u32[]{:S(2)}) copy-start(bf16[256,256]{1,0:T(8,128)(2,1)S(1)} %collective-permute-done.16.refs_1_) | copy-start | bytes 393220
  (11 other events, 12.4 us)
where the time goes:
time: 200 us; the launch traced here: 199 us
  Pallas kernels  67.7 us (34%)
  waiting for transfers between devices  49.3 us (25%)
  blocking collectives  38.2 us (19%)
  starting transfers between devices  36.9 us (18%)
  local copies, waits for them, and re-layouts  5.69 us (3%)
    ppermute x13, waiting for transfers between devices, along(): return lax.ppermute(slots, 'rows', line_pairs(step, same_class))  41 us
    all_to_all x1, blocking collectives, exchange(): lax.all_to_all(slots, 'rows', split_axis=0, concat_axis=0, tiled=True)  38.2 us
    pallas_call x5, Pallas kernels, line_sums(): pl.pallas_call(functools.partial(sums_body, sources, capacity, blocks, ha...  34.8 us
    ppermute x13, starting transfers between devices, along(): return lax.ppermute(slots, 'rows', line_pairs(step, same_class))  24.9 us
    pallas_call x2, Pallas kernels, pack(): pl.pallas_call(functools.partial(pack_body, slots, capacity), grid=(longe...  13.3 us
    ppermute x3, waiting for transfers between devices, level_step(): pieces.append(lax.ppermute(means, 'grp', back))  8.21 us
    pallas_call x1, Pallas kernels, place(): pl.pallas_call(functools.partial(place_body, group), grid=(peers // group...  7.32 us
    ppermute x3, starting transfers between devices, level_step(): got[cross] = lax.ppermute(part, 'rows', cross_pairs(cross))  6.69 us
  transfers between devices with their start and end apart: 19, of which 8 were waited for; matrix products, arithmetic and copies ran while one was open for 0% of the time, Pallas kernels for 21%

commit v1 on v0

--- a/solution.py
+++ b/solution.py
@@ -11,6 +11,7 @@
 F32 = jnp.float32
 BF16 = jnp.bfloat16
 LANES = 128
+MIB = 1024 * 1024
 TAIL = 8
 SIDE = 4
 
@@ -139,6 +140,7 @@
             bytes_accessed=per_dev * width * 2 + many * tall * width * 2,
             transcendentals=0,
         ),
+        compiler_params=pltpu.CompilerParams(vmem_limit_bytes=60 * MIB),
         name="pack_rows",
     )(send_counts, embeddings, local)
 
@@ -256,6 +258,7 @@
             bytes_accessed=many * (sources * tall * width * 2 + fine_dev * width * 8),
             transcendentals=0,
         ),
+        compiler_params=pltpu.CompilerParams(vmem_limit_bytes=32 * MIB),
         name="line_sums",
     )(*operands)
 
@@ -310,6 +313,7 @@
         + [pl.BlockSpec((16, width), lambda m: (fine_dev // 16, 0))] * len(got),
         out_specs=pl.BlockSpec((size, width), lambda m: (m, 0)),
         scratch_shapes=[pltpu.VMEM((LANES, digits), F32)],
+        compiler_params=pltpu.CompilerParams(vmem_limit_bytes=24 * MIB),
         name="new_fine",
     )(acc, counts, old_fine, *got, *got)
 
@@ -346,6 +350,7 @@
             jax.ShapeDtypeStruct((capacity, fine_dev), BF16),
             jax.ShapeDtypeStruct((peers, capacity), F32),
         ),
+        compiler_params=pltpu.CompilerParams(vmem_limit_bytes=24 * MIB),
         name="plan_clusters",
     )(coarse_ids)
 
@@ -381,6 +386,7 @@
         ],
         out_specs=pl.BlockSpec((group, capacity + TAIL, width), lambda i: (i, 0, 0)),
         scratch_shapes=[pltpu.VMEM((group * capacity, fine_dev), BF16)],
+        compiler_params=pltpu.CompilerParams(vmem_limit_bytes=24 * MIB),
         name="place_clusters",
     )(owner_hot, rank_hot, tags, new_fine)
 
@@ -412,6 +418,7 @@
             pltpu.VMEM((old_coarse.shape[0], deep), BF16),
             pltpu.VMEM((deep, width), BF16),
         ],
+        compiler_params=pltpu.CompilerParams(vmem_limit_bytes=24 * MIB),
         name="coarse_means",
     )(received, old_coarse)
 
@@ -436,6 +443,7 @@
         in_specs=[pl.BlockSpec(memory_space=pltpu.SMEM)]
         + [pl.BlockSpec(memory_space=pltpu.VMEM)] * groups,
         scratch_shapes=[pltpu.VMEM((rows, groups * width), F32)],
+        compiler_params=pltpu.CompilerParams(vmem_limit_bytes=24 * MIB),
         name="coarse_dirs",
     )(at, *pieces)
 
@@ -463,7 +471,9 @@
     order = (2, 1, 3)
 
     keep = pack([(True, s, sent) for s in order], *rows)
-    kept = [along(a, s, True) for s, a in zip(order, keep)]
+    kept = []
+    for s, a in zip(order, keep):
+        kept.append(along(a, s, True))
     more = pack(
         [(False, s, sent) for s in order]
         + [(False, 0, own + sent), (True, 0, own + sent)]
@@ -472,22 +482,21 @@
     )
     swapped = along(more[3], 0, False)
     given = [along(a, s, False) for s, a in zip(order, more[:3])]
-    kept_own = [along(a, s, True) for s, a in zip(order, more[5:8])]
-    given_own = [along(a, s, False) for s, a in zip(order, more[8:])]
     owner_hot, rank_hot, tags = plan(
         coarse_ids.reshape(1, -1), peers, capacity_two, coarse_dev
     )
     near = [(more[4], 0), (swapped, 0)]
-    had = line_sums(near + [(a, 1) for a in kept], capacity, fine_dev, sent)
+    had = line_sums(near + [(kept[0], 1)], capacity, fine_dev, sent)
+    had = line_sums([(a, 1) for a in kept[1:]], capacity, fine_dev, sent, (*had, 1))
+    kept_own = [along(a, s, True) for s, a in zip(order, more[5:8])]
+    given_own = [along(a, s, False) for s, a in zip(order, more[8:])]
     got = {}
     for cross in order:
         part = line_sums(
             [(a, 1) for a in given], capacity, fine_dev, (cross,), (*had, 1), send=True
         )
         got[cross] = lax.ppermute(part, "rows", cross_pairs(cross))
-    acc, counts = line_sums(
-        near + [(a, 0) for a in kept_own + given_own], capacity, fine_dev, own
-    )
+    acc, counts = line_sums(near + [(a, 0) for a in kept_own + given_own], capacity, fine_dev, own)
     new_fine = update(acc, counts, old_fine, [got[c] for c in steps])
 
     received = exchange(place(owner_hot, rank_hot, tags, new_fine, 8))

time: 200 us -> 172 us (0.86)
  Pallas kernels: 67.7 us -> 47.5 us
  waiting for transfers between devices: 49.3 us -> 42.7 us
  local copies, waits for them, and re-layouts: 5.69 us -> 1.28 us
  starting transfers between devices: 36.9 us -> 40.8 us
    pallas_call x5 -> x6, Pallas kernels: 34.8 us -> 24.1 us  [line_sums(): pl.pallas_call(functools.partial(sums_body, sources, capacity, blocks, ha...]
    ppermute x13, waiting for transfers between devices: 41 us -> 34.7 us  [along(): return lax.ppermute(slots, 'rows', line_pairs(step, same_class))]
    ppermute x13, starting transfers between devices: 24.9 us -> 29.4 us  [along(): return lax.ppermute(slots, 'rows', line_pairs(step, same_class))]
    unnamed x32 -> x26, local copies, waits for them, and re-layouts: 5.69 us -> 1.28 us
    pallas_call x1, Pallas kernels: 4.74 us -> 2.22 us  [update(): pl.pallas_call(update_body, grid=(fine_dev // size,), out_shape=jax.Shape...]
    pallas_call x1, Pallas kernels: 7.32 us -> 5.03 us  [place(): pl.pallas_call(functools.partial(place_body, group), grid=(peers // group...]
    pallas_call x1, Pallas kernels: 3.45 us -> 1.17 us  [coarse(): pl.pallas_call(coarse_body, out_shape=jax.ShapeDtypeStruct(old_coarse.sha...]
  transfers between devices with their start and end apart: 19 -> 19, of which waited for: 8 -> 8; matrix products, arithmetic and copies ran while one was open for 0% -> 0% of each run, Pallas kernels for 21% -> 18%
where the time goes in v1:
time: 172 us; the launch traced here: 171 us
  Pallas kernels  47.5 us (28%)
  waiting for transfers between devices  42.7 us (25%)
  starting transfers between devices  40.8 us (24%)
  blocking collectives  38.3 us (22%)
    all_to_all x1, blocking collectives, exchange(): lax.all_to_all(slots, 'rows', split_axis=0, concat_axis=0, tiled=True)  38.3 us
    ppermute x13, waiting for transfers between devices, along(): return lax.ppermute(slots, 'rows', line_pairs(step, same_class))  34.7 us
    ppermute x13, starting transfers between devices, along(): return lax.ppermute(slots, 'rows', line_pairs(step, same_class))  29.4 us
    pallas_call x6, Pallas kernels, line_sums(): pl.pallas_call(functools.partial(sums_body, sources, capacity, blocks, ha...  24.1 us
    pallas_call x2, Pallas kernels, pack(): pl.pallas_call(functools.partial(pack_body, slots, capacity), grid=(longe...  13.4 us
    ppermute x3, waiting for transfers between devices, level_step(): pieces.append(lax.ppermute(means, 'grp', back))  8 us
    ppermute x3, starting transfers between devices, level_step(): got[cross] = lax.ppermute(part, 'rows', cross_pairs(cross))  6.04 us
    ppermute x3, starting transfers between devices, level_step(): pieces.append(lax.ppermute(means, 'grp', back))  5.37 us
  transfers between devices with their start and end apart: 19, of which 8 were waited for; matrix products, arithmetic and copies ran while one was open for 0% of the time, Pallas kernels for 18%

profile of v1, /device:TPU:0, one launch (start us, length us, event | category | flops | bytes accessed | tf_op | source)
XLA Modules:
  0.0 171.4 jit_solution(15350684992225114075)
XLA Ops:
  0.6 7.8 %pack_rows.2 = (bf16[3,520,256]{2,1,0:T(8,128)(2,1)}, bf16[3,520,256]{2,1,0:T(8,128)(2,1)}, bf16[3,520,256]{2,1,0:T(8,128)(2,1)}, bf16[4,520,256]{2,1,0:T(8,128)...) custom-call(s32[1,32]{1,0:T(1,128)} %counts.3, ...), custom_call_target="tpu_custom_call" | custom-call | bytes 10317824 | tf_op jit(solution)/shard_map/pack_rows/pallas_call | solution.py:122
  8.5 5.6 %pack_rows.3 = (bf16[3,520,256]{2,1,0:T(8,128)(2,1)}, bf16[3,520,256]{2,1,0:T(8,128)(2,1)}, bf16[3,520,256]{2,1,0:T(8,128)(2,1)}) custom-call(s32[1,32]{1,0:T(1,128)} %counts.3, bf16[8192,256]{1,0:T(8,128)(2,1)} %emb.3, s32[64,128]{1,0:T(8,128)} %bitcast.5), custom_call_target="tpu_custom_call" | custom-call | bytes 6590464 | tf_op jit(solution)/shard_map/pack_rows/pallas_call | solution.py:122
  14.2 3.2 %collective-permute-start.12 = (bf16[3,520,256]{2,1,0:T(8,128)(2,1)}, bf16[3,520,256]{2,1,0:T(8,128)(2,1)S(1)}, u32[]{:S(2)}, u32[]{:S(2)}) collective-permute-start(bf16[3,520,256]{2,1,0:T(8,128)(2,1)} %get-tuple-element.40), channel_id=1, source_target_pairs={{0,64},{4,20},{8,72},{12,28},{16,80},{20,4},{24,88},{28,12},{32,96... | collective-permute-start | bytes 2396168 | tf_op jit(solution)/shard_map/ppermute | solution.py:467
  18.0 2.6 %collective-permute-start.11 = (bf16[3,520,256]{2,1,0:T(8,128)(2,1)}, bf16[3,520,256]{2,1,0:T(8,128)(2,1)S(1)}, u32[]{:S(2)}, u32[]{:S(2)}) collective-permute-start(bf16[3,520,256]{2,1,0:T(8,128)(2,1)} %get-tuple-element.39), channel_id=1, source_target_pairs={{0,96},{4,28},{8,104},{12,4},{16,112},{20,12},{24,120},{28,20},{32... | collective-permute-start | bytes 2396168 | tf_op jit(solution)/shard_map/ppermute | solution.py:467
  20.6 13.2 %collective-permute-done.12.refs_2_ = bf16[3,520,256]{2,1,0:T(8,128)(2,1)S(1)} collective-permute-done((bf16[3,520,256]{2,1,0:T(8,128)(2,1)}, bf16[3,520,256]{2,1,0:T(8,128)(2,1)S(1)}, u32[]{:S(2)}, u32[]{:S(2)}) %collective-permute-start.12) | collective-permute-done | bytes 798752 | tf_op jit(solution)/shard_map/ppermute | solution.py:467
  33.8 3.7 %collective-permute-start.9 = (bf16[3,520,256]{2,1,0:T(8,128)(2,1)S(1)}, bf16[3,520,256]{2,1,0:T(8,128)(2,1)S(1)}, u32[]{:S(2)}, u32[]{:S(2)}) collective-permute-start(bf16[3,520,256]{2,1,0:T(8,128)(2,1)S(1)} %copy-done.5), channel_id=1, source_target_pairs={{0,28},{4,96},{8,4},{12,104},{16,12},{20,112},{24,20},{28,120},{32... | collective-permute-start | bytes 2396168 | tf_op jit(solution)/shard_map/ppermute | solution.py:467
  37.6 6.8 %line_sums.7 = (f32[3,2048,256]{2,1,0:T(8,128)S(1)}, f32[3,16,128]{2,1,0:T(8,128)S(1)}) custom-call(bf16[4,520,256]{2,1,0:T(8,128)(2,1)S(1)} %copy-done.4, bf16[4,520,256]{2,1,0:T(8,128)(2,1)S(1)} %collective-permute-done.refs_1_, bf16[3,520,256]{2,1,0:T(8,128)(2,1)S(1)} %collective-permute-done.12.refs_2_), custom_call_target="tpu_custom_call" | custom-call | flops 4831838208 | bytes 14979072 | tf_op jit(solution)/shard_map/line_sums/pallas_call | solution.py:244
  44.4 6.5 %collective-permute-done.10.refs_0_ = bf16[3,520,256]{2,1,0:T(8,128)(2,1)S(1)} collective-permute-done((bf16[3,520,256]{2,1,0:T(8,128)(2,1)}, bf16[3,520,256]{2,1,0:T(8,128)(2,1)S(1)}, u32[]{:S(2)}, u32[]{:S(2)}) %collective-permute-start.10) | collective-permute-done | bytes 798752 | tf_op jit(solution)/shard_map/ppermute | solution.py:467
  50.9 2.7 %collective-permute-start.1 = (bf16[1,520,256]{2,1,0:T(8,128)(2,1)S(1)}, bf16[1,520,256]{2,1,0:T(8,128)(2,1)S(1)}, u32[]{:S(2)}, u32[]{:S(2)}) collective-permute-start(bf16[1,520,256]{2,1,0:T(8,128)(2,1)S(1)} %copy-done.12), channel_id=1, source_target_pairs={{0,64},{4,20},{8,72},{12,28},{16,80},{20,4},{24,88},{28,12},{32,96... | collective-permute-start | bytes 798728 | tf_op jit(solution)/shard_map/ppermute | solution.py:467
  53.6 5.1 %line_sums.8 = (f32[3,2048,256]{2,1,0:T(8,128)S(1)}, f32[3,16,128]{2,1,0:T(8,128)S(1)}) custom-call(bf16[3,520,256]{2,1,0:T(8,128)(2,1)S(1)} %collective-permute-done.10.refs_0_, bf16[3,520,256]{2,1,0:T(8,128)(2,1)S(1)} %collective-permute-done.11.refs_1_, f32[3,2048,256]{2,1,0:T(8,128)S(1)} %get-tuple-element.41.refs_2_, ...), custom_call_target="tpu_custom_call" | custom-call | flops 3221225472 | bytes 14180352 | tf_op jit(solution)/shard_map/line_sums/pallas_call | solution.py:244
  58.7 2.3 %line_sums.9 = bf16[2064,256]{1,0:T(8,128)(2,1)S(1)} custom-call(bf16[3,520,256]{2,1,0:T(8,128)(2,1)S(1)} %collective-permute-done.7.refs_0_, bf16[3,520,256]{2,1,0:T(8,128)(2,1)S(1)} %collective-permute-done.8.refs_1_, bf16[3,520,256]{2,1,0:T(8,128)(2,1)S(1)} %collective-permute-done.9.refs_2_, f32[3,2048,256]{2,1,0:T(8,128)S(1)} %get-tuple-element.43.refs_3_, ...), custom_call_target="tpu_custom_call" | custom-call | flops 1610612736 | bytes 4993024 | tf_op jit(solution)/shard_map/line_sums/pallas_call | solution.py:244
  65.0 3.0 %collective-permute-start.14 = (bf16[2064,256]{1,0:T(8,128)(2,1)S(1)}, bf16[2064,256]{1,0:T(8,128)(2,1)S(1)}, u32[]{:S(2)}, u32[]{:S(2)}) collective-permute-start(bf16[2064,256]{1,0:T(8,128)(2,1)S(1)} %line_sums.10), channel_id=1, source_target_pairs={{0,16},{4,68},{8,24},{12,76},{16,0},{20,84},{24,8},{28,92},{32,48}... | collective-permute-start | bytes 3170312 | tf_op jit(solution)/shard_map/ppermute | solution.py:498
  68.0 2.3 %line_sums.11 = bf16[2064,256]{1,0:T(8,128)(2,1)S(1)} custom-call(bf16[3,520,256]{2,1,0:T(8,128)(2,1)S(1)} %collective-permute-done.7.refs_0_, bf16[3,520,256]{2,1,0:T(8,128)(2,1)S(1)} %collective-permute-done.8.refs_1_, bf16[3,520,256]{2,1,0:T(8,128)(2,1)S(1)} %collective-permute-done.9.refs_2_, f32[3,2048,256]{2,1,0:T(8,128)S(1)} %get-tuple-element.43.refs_3_, ...), custom_call_target="tpu_custom_call" | custom-call | flops 1610612736 | bytes 4993024 | tf_op jit(solution)/shard_map/line_sums/pallas_call | solution.py:244
  71.7 3.2 %collective-permute-start.3 = (bf16[1,520,256]{2,1,0:T(8,128)(2,1)S(1)}, bf16[1,520,256]{2,1,0:T(8,128)(2,1)S(1)}, u32[]{:S(2)}, u32[]{:S(2)}) collective-permute-start(bf16[1,520,256]{2,1,0:T(8,128)(2,1)S(1)} %copy-done.10), channel_id=1, source_target_pairs={{0,96},{4,28},{8,104},{12,4},{16,112},{20,12},{24,120},{28,20},{32... | collective-permute-start | bytes 798728 | tf_op jit(solution)/shard_map/ppermute | solution.py:467
  75.0 9.3 %collective-permute-done.3.refs_4_ = bf16[1,520,256]{2,1,0:T(8,128)(2,1)S(1)} collective-permute-done((bf16[1,520,256]{2,1,0:T(8,128)(2,1)S(1)}, bf16[1,520,256]{2,1,0:T(8,128)(2,1)S(1)}, u32[]{:S(2)}, u32[]{:S(2)}) %collective-permute-start.3) | collective-permute-done | bytes 266272 | tf_op jit(solution)/shard_map/ppermute | solution.py:467
  84.2 4.3 %collective-permute-start.5 = (bf16[1,520,256]{2,1,0:T(8,128)(2,1)S(1)}, bf16[1,520,256]{2,1,0:T(8,128)(2,1)S(1)}, u32[]{:S(2)}, u32[]{:S(2)}) collective-permute-start(bf16[1,520,256]{2,1,0:T(8,128)(2,1)S(1)} %copy-done.8), channel_id=1, source_target_pairs={{0,12},{4,32},{8,20},{12,40},{16,28},{20,48},{24,4},{28,56},{32,44... | collective-permute-start | bytes 798728 | tf_op jit(solution)/shard_map/ppermute | solution.py:467
  88.5 2.4 %collective-permute-done.4.refs_5_ = bf16[1,520,256]{2,1,0:T(8,128)(2,1)S(1)} collective-permute-done((bf16[1,520,256]{2,1,0:T(8,128)(2,1)S(1)}, bf16[1,520,256]{2,1,0:T(8,128)(2,1)S(1)}, u32[]{:S(2)}, u32[]{:S(2)}) %collective-permute-start.4) | collective-permute-done | bytes 266272 | tf_op jit(solution)/shard_map/ppermute | solution.py:467
  90.9 8.8 %collective-permute-start.6 = (bf16[1,520,256]{2,1,0:T(8,128)(2,1)S(1)}, bf16[1,520,256]{2,1,0:T(8,128)(2,1)S(1)}, u32[]{:S(2)}, u32[]{:S(2)}) collective-permute-start(bf16[1,520,256]{2,1,0:T(8,128)(2,1)S(1)} %copy-done.7), channel_id=1, source_target_pairs={{0,28},{4,96},{8,4},{12,104},{16,12},{20,112},{24,20},{28,120},{32... | collective-permute-start | bytes 798728 | tf_op jit(solution)/shard_map/ppermute | solution.py:467
  100.4 3.3 %collective-permute-done.6.refs_7_ = bf16[1,520,256]{2,1,0:T(8,128)(2,1)S(1)} collective-permute-done((bf16[1,520,256]{2,1,0:T(8,128)(2,1)S(1)}, bf16[1,520,256]{2,1,0:T(8,128)(2,1)S(1)}, u32[]{:S(2)}, u32[]{:S(2)}) %collective-permute-start.6) | collective-permute-done | bytes 266272 | tf_op jit(solution)/shard_map/ppermute | solution.py:467
  103.7 5.3 %line_sums.6 = (f32[1,2048,256]{2,1,0:T(8,128)S(1)}, f32[1,16,128]{2,1,0:T(8,128)S(1)}) custom-call(bf16[4,520,256]{2,1,0:T(8,128)(2,1)S(1)} %copy-done.4, bf16[4,520,256]{2,1,0:T(8,128)(2,1)S(1)} %collective-permute-done.refs_1_, bf16[1,520,256]{2,1,0:T(8,128)(2,1)S(1)} %collective-permute-done.1.refs_2_, ...), custom_call_target="tpu_custom_call" | custom-call | flops 4294967296 | bytes 6324224 | tf_op jit(solution)/shard_map/line_sums/pallas_call | solution.py:244
  112.5 5.0 %place_clusters.1 = bf16[32,136,256]{2,1,0:T(8,128)(2,1)S(1)} custom-call(f32[32,2048]{1,0:T(8,128)S(1)} %get-tuple-element.45.owner_hot, bf16[128,2048]{1,0:T(8,128)(2,1)S(1)} %get-tuple-element.46.rank_hot, f32[32,128]{1,0:T(8,128)S(1)} %get-tuple-element.47.tags, bf16[2048,256]{1,0:T(8,128)(2,1)S(1)} %copy-done), custom_call_target="tpu_custom_call" | custom-call | tf_op jit(solution)/shard_map/place_clusters/pallas_call | solution.py:377
  117.5 38.3 %all_to_all.5.received = bf16[32,136,256]{2,1,0:T(8,128)(2,1)S(1)} all-to-all(bf16[32,136,256]{2,1,0:T(8,128)(2,1)S(1)} %place_clusters.1), channel_id=1, replica_groups=mesh['rows'=32,'grp'=4] {'rows'}, dimensions={0} | all-to-all | bytes 4456448 | tf_op jit(solution)/shard_map/all_to_all | solution.py:452
  156.9 4.1 %collective-permute-start.16 = (bf16[256,256]{1,0:T(8,128)(2,1)S(1)}, bf16[256,256]{1,0:T(8,128)(2,1)S(1)}, u32[]{:S(2)}, u32[]{:S(2)}) collective-permute-start(bf16[256,256]{1,0:T(8,128)(2,1)S(1)} %coarse_means.1.refs_0_), channel_id=1, source_target_pairs={{1,0},{2,1},{3,2},{0,3},{5,4},{6,5},{7,6},{4,7},{9,8},{10,9},{11,1... | collective-permute-start | bytes 393224 | tf_op jit(solution)/shard_map/ppermute | solution.py:507
  162.3 4.6 %collective-permute-done.16.refs_1_ = bf16[256,256]{1,0:T(8,128)(2,1)S(1)} collective-permute-done((bf16[256,256]{1,0:T(8,128)(2,1)S(1)}, bf16[256,256]{1,0:T(8,128)(2,1)S(1)}, u32[]{:S(2)}, u32[]{:S(2)}) %collective-permute-start.16) | collective-permute-done | bytes 131104 | tf_op jit(solution)/shard_map/ppermute | solution.py:507
  (54 shorter events, 17.1 us)
Async XLA Ops:
  8.4 25.4 %copy-start.5 = (bf16[3,520,256]{2,1,0:T(8,128)(2,1)S(1)}, bf16[3,520,256]{2,1,0:T(8,128)(2,1)}, u32[]{:S(2)}) copy-start(bf16[3,520,256]{2,1,0:T(8,128)(2,1)} %get-tuple-element.37) | copy-start | bytes 2396164
  8.4 29.1 %copy-start.4 = (bf16[4,520,256]{2,1,0:T(8,128)(2,1)S(1)}, bf16[4,520,256]{2,1,0:T(8,128)(2,1)}, u32[]{:S(2)}) copy-start(bf16[4,520,256]{2,1,0:T(8,128)(2,1)} %get-tuple-element.25.refs_0_) | copy-start | bytes 3194884
  8.4 25.3 %collective-permute-start = (bf16[4,520,256]{2,1,0:T(8,128)(2,1)}, bf16[4,520,256]{2,1,0:T(8,128)(2,1)S(1)}, u32[]{:S(2)}, u32[]{:S(2)}) collective-permute-start(bf16[4,520,256]{2,1,0:T(8,128)(2,1)} %get-tuple-element.26), channel_id=1, source_target_pairs={{0,4},{4,0},{8,12},{12,8},{16,20},{20,16},{24,28},{28,24},{32,36},... | collective-permute-start | bytes 3194888 | tf_op jit(solution)/shard_map/ppermute | solution.py:467
  14.2 19.6 %collective-permute-start.12 = (bf16[3,520,256]{2,1,0:T(8,128)(2,1)}, bf16[3,520,256]{2,1,0:T(8,128)(2,1)S(1)}, u32[]{:S(2)}, u32[]{:S(2)}) collective-permute-start(bf16[3,520,256]{2,1,0:T(8,128)(2,1)} %get-tuple-element.40), channel_id=1, source_target_pairs={{0,64},{4,20},{8,72},{12,28},{16,80},{20,4},{24,88},{28,12},{32,96... | collective-permute-start | bytes 2396168 | tf_op jit(solution)/shard_map/ppermute | solution.py:467
  17.4 33.5 %collective-permute-start.10 = (bf16[3,520,256]{2,1,0:T(8,128)(2,1)}, bf16[3,520,256]{2,1,0:T(8,128)(2,1)S(1)}, u32[]{:S(2)}, u32[]{:S(2)}) collective-permute-start(bf16[3,520,256]{2,1,0:T(8,128)(2,1)} %get-tuple-element.38), channel_id=1, source_target_pairs={{0,32},{4,12},{8,40},{12,20},{16,48},{20,28},{24,56},{28,4},{32,64... | collective-permute-start | bytes 2396168 | tf_op jit(solution)/shard_map/ppermute | solution.py:467
  18.0 35.6 %collective-permute-start.11 = (bf16[3,520,256]{2,1,0:T(8,128)(2,1)}, bf16[3,520,256]{2,1,0:T(8,128)(2,1)S(1)}, u32[]{:S(2)}, u32[]{:S(2)}) collective-permute-start(bf16[3,520,256]{2,1,0:T(8,128)(2,1)} %get-tuple-element.39), channel_id=1, source_target_pairs={{0,96},{4,28},{8,104},{12,4},{16,112},{20,12},{24,120},{28,20},{32... | collective-permute-start | bytes 2396168 | tf_op jit(solution)/shard_map/ppermute | solution.py:467
  20.6 38.1 %collective-permute-start.7 = (bf16[3,520,256]{2,1,0:T(8,128)(2,1)}, bf16[3,520,256]{2,1,0:T(8,128)(2,1)S(1)}, u32[]{:S(2)}, u32[]{:S(2)}) collective-permute-start(bf16[3,520,256]{2,1,0:T(8,128)(2,1)} %get-tuple-element.35), channel_id=1, source_target_pairs={{0,20},{4,64},{8,28},{12,72},{16,4},{20,80},{24,12},{28,88},{32,52... | collective-permute-start | bytes 2396168 | tf_op jit(solution)/shard_map/ppermute | solution.py:467
  33.8 24.9 %collective-permute-start.8 = (bf16[3,520,256]{2,1,0:T(8,128)(2,1)S(1)}, bf16[3,520,256]{2,1,0:T(8,128)(2,1)S(1)}, u32[]{:S(2)}, u32[]{:S(2)}) collective-permute-start(bf16[3,520,256]{2,1,0:T(8,128)(2,1)S(1)} %copy-done.6), channel_id=1, source_target_pairs={{0,12},{4,32},{8,20},{12,40},{16,28},{20,48},{24,4},{28,56},{32,44... | collective-permute-start | bytes 2396168 | tf_op jit(solution)/shard_map/ppermute | solution.py:467
  33.8 24.9 %collective-permute-start.9 = (bf16[3,520,256]{2,1,0:T(8,128)(2,1)S(1)}, bf16[3,520,256]{2,1,0:T(8,128)(2,1)S(1)}, u32[]{:S(2)}, u32[]{:S(2)}) collective-permute-start(bf16[3,520,256]{2,1,0:T(8,128)(2,1)S(1)} %copy-done.5), channel_id=1, source_target_pairs={{0,28},{4,96},{8,4},{12,104},{16,12},{20,112},{24,20},{28,120},{32... | collective-permute-start | bytes 2396168 | tf_op jit(solution)/shard_map/ppermute | solution.py:467
  50.9 20.8 %collective-permute-start.1 = (bf16[1,520,256]{2,1,0:T(8,128)(2,1)S(1)}, bf16[1,520,256]{2,1,0:T(8,128)(2,1)S(1)}, u32[]{:S(2)}, u32[]{:S(2)}) collective-permute-start(bf16[1,520,256]{2,1,0:T(8,128)(2,1)S(1)} %copy-done.12), channel_id=1, source_target_pairs={{0,64},{4,20},{8,72},{12,28},{16,80},{20,4},{24,88},{28,12},{32,96... | collective-permute-start | bytes 798728 | tf_op jit(solution)/shard_map/ppermute | solution.py:467
  53.6 21.4 %collective-permute-start.2 = (bf16[1,520,256]{2,1,0:T(8,128)(2,1)S(1)}, bf16[1,520,256]{2,1,0:T(8,128)(2,1)S(1)}, u32[]{:S(2)}, u32[]{:S(2)}) collective-permute-start(bf16[1,520,256]{2,1,0:T(8,128)(2,1)S(1)} %copy-done.11), channel_id=1, source_target_pairs={{0,32},{4,12},{8,40},{12,20},{16,48},{20,28},{24,56},{28,4},{32,64... | collective-permute-start | bytes 798728 | tf_op jit(solution)/shard_map/ppermute | solution.py:467
  61.1 47.9 %collective-permute-start.13 = (bf16[2064,256]{1,0:T(8,128)(2,1)S(1)}, bf16[2064,256]{1,0:T(8,128)(2,1)S(1)}, u32[]{:S(2)}, u32[]{:S(2)}) collective-permute-start(bf16[2064,256]{1,0:T(8,128)(2,1)S(1)} %line_sums.9), channel_id=1, source_target_pairs={{0,8},{4,36},{8,16},{12,44},{16,24},{20,52},{24,0},{28,60},{32,40}... | collective-permute-start | bytes 3170312 | tf_op jit(solution)/shard_map/ppermute | solution.py:498
  65.0 25.9 %copy-start.7 = (bf16[1,520,256]{2,1,0:T(8,128)(2,1)S(1)}, bf16[1,520,256]{2,1,0:T(8,128)(2,1)}, u32[]{:S(2)}) copy-start(bf16[1,520,256]{2,1,0:T(8,128)(2,1)} %get-tuple-element.32) | copy-start | bytes 798724
  65.0 34.7 %copy-start.3 = (s32[2048]{0:T(1024)S(1)}, s32[2048]{0:T(1024)}, u32[]{:S(2)}) copy-start(s32[2048]{0:T(1024)} %param.10) | copy-start | bytes 24580
  65.0 43.9 %collective-permute-start.14 = (bf16[2064,256]{1,0:T(8,128)(2,1)S(1)}, bf16[2064,256]{1,0:T(8,128)(2,1)S(1)}, u32[]{:S(2)}, u32[]{:S(2)}) collective-permute-start(bf16[2064,256]{1,0:T(8,128)(2,1)S(1)} %line_sums.10), channel_id=1, source_target_pairs={{0,16},{4,68},{8,24},{12,76},{16,0},{20,84},{24,8},{28,92},{32,48}... | collective-permute-start | bytes 3170312 | tf_op jit(solution)/shard_map/ppermute | solution.py:498
  70.3 38.7 %collective-permute-start.15 = (bf16[2064,256]{1,0:T(8,128)(2,1)S(1)}, bf16[2064,256]{1,0:T(8,128)(2,1)S(1)}, u32[]{:S(2)}, u32[]{:S(2)}) collective-permute-start(bf16[2064,256]{1,0:T(8,128)(2,1)S(1)} %line_sums.11), channel_id=1, source_target_pairs={{0,24},{4,100},{8,0},{12,108},{16,8},{20,116},{24,16},{28,124},{32... | collective-permute-start | bytes 3170312 | tf_op jit(solution)/shard_map/ppermute | solution.py:498
  71.7 12.5 %collective-permute-start.3 = (bf16[1,520,256]{2,1,0:T(8,128)(2,1)S(1)}, bf16[1,520,256]{2,1,0:T(8,128)(2,1)S(1)}, u32[]{:S(2)}, u32[]{:S(2)}) collective-permute-start(bf16[1,520,256]{2,1,0:T(8,128)(2,1)S(1)} %copy-done.10), channel_id=1, source_target_pairs={{0,96},{4,28},{8,104},{12,4},{16,112},{20,12},{24,120},{28,20},{32... | collective-permute-start | bytes 798728 | tf_op jit(solution)/shard_map/ppermute | solution.py:467
  75.0 16.0 %collective-permute-start.4 = (bf16[1,520,256]{2,1,0:T(8,128)(2,1)S(1)}, bf16[1,520,256]{2,1,0:T(8,128)(2,1)S(1)}, u32[]{:S(2)}, u32[]{:S(2)}) collective-permute-start(bf16[1,520,256]{2,1,0:T(8,128)(2,1)S(1)} %copy-done.9), channel_id=1, source_target_pairs={{0,20},{4,64},{8,28},{12,72},{16,4},{20,80},{24,12},{28,88},{32,52... | collective-permute-start | bytes 798728 | tf_op jit(solution)/shard_map/ppermute | solution.py:467
  84.2 16.1 %collective-permute-start.5 = (bf16[1,520,256]{2,1,0:T(8,128)(2,1)S(1)}, bf16[1,520,256]{2,1,0:T(8,128)(2,1)S(1)}, u32[]{:S(2)}, u32[]{:S(2)}) collective-permute-start(bf16[1,520,256]{2,1,0:T(8,128)(2,1)S(1)} %copy-done.8), channel_id=1, source_target_pairs={{0,12},{4,32},{8,20},{12,40},{16,28},{20,48},{24,4},{28,56},{32,44... | collective-permute-start | bytes 798728 | tf_op jit(solution)/shard_map/ppermute | solution.py:467
  90.9 12.8 %collective-permute-start.6 = (bf16[1,520,256]{2,1,0:T(8,128)(2,1)S(1)}, bf16[1,520,256]{2,1,0:T(8,128)(2,1)S(1)}, u32[]{:S(2)}, u32[]{:S(2)}) collective-permute-start(bf16[1,520,256]{2,1,0:T(8,128)(2,1)S(1)} %copy-done.7), channel_id=1, source_target_pairs={{0,28},{4,96},{8,4},{12,104},{16,12},{20,112},{24,20},{28,120},{32... | collective-permute-start | bytes 798728 | tf_op jit(solution)/shard_map/ppermute | solution.py:467
  117.5 38.3 %copy-start.2 = (bf16[256,256]{1,0:T(8,128)(2,1)S(1)}, bf16[256,256]{1,0:T(8,128)(2,1)}, u32[]{:S(2)}) copy-start(bf16[256,256]{1,0:T(8,128)(2,1)} %old.3) | copy-start | bytes 393220
  156.9 10.0 %collective-permute-start.16 = (bf16[256,256]{1,0:T(8,128)(2,1)S(1)}, bf16[256,256]{1,0:T(8,128)(2,1)S(1)}, u32[]{:S(2)}, u32[]{:S(2)}) collective-permute-start(bf16[256,256]{1,0:T(8,128)(2,1)S(1)} %coarse_means.1.refs_0_), channel_id=1, source_target_pairs={{1,0},{2,1},{3,2},{0,3},{5,4},{6,5},{7,6},{4,7},{9,8},{10,9},{11,1... | collective-permute-start | bytes 393224 | tf_op jit(solution)/shard_map/ppermute | solution.py:507
  161.1 7.9 %collective-permute-start.17 = (bf16[256,256]{1,0:T(8,128)(2,1)S(1)}, bf16[256,256]{1,0:T(8,128)(2,1)S(1)}, u32[]{:S(2)}, u32[]{:S(2)}) collective-permute-start(bf16[256,256]{1,0:T(8,128)(2,1)S(1)} %coarse_means.1.refs_0_), channel_id=1, source_target_pairs={{2,0},{3,1},{0,2},{1,3},{6,4},{7,5},{4,6},{5,7},{10,8},{11,9},{8,1... | collective-permute-start | bytes 393224 | tf_op jit(solution)/shard_map/ppermute | solution.py:507
  161.1 9.3 %collective-permute-start.18 = (bf16[256,256]{1,0:T(8,128)(2,1)S(1)}, bf16[256,256]{1,0:T(8,128)(2,1)S(1)}, u32[]{:S(2)}, u32[]{:S(2)}) collective-permute-start(bf16[256,256]{1,0:T(8,128)(2,1)S(1)} %coarse_means.1.refs_0_), channel_id=1, source_target_pairs={{3,0},{0,1},{1,2},{2,3},{7,4},{4,5},{5,6},{6,7},{11,8},{8,9},{9,10... | collective-permute-start | bytes 393224 | tf_op jit(solution)/shard_map/ppermute | solution.py:507
  (8 other events, 100.5 us)

commit v2 on v1

--- a/solution.py
+++ b/solution.py
@@ -45,7 +45,16 @@
     return pairs
 
 
-def pack_body(slots, capacity, counts, emb, local, *rest):
+def owner_of(kind, step, cross):
+    here = lax.axis_index("rows")
+    along = lax.rem(here // (2 * SIDE) + jnp.where(kind == 0, step, cross), SIDE)
+    over = lax.rem(lax.rem(here // 2, SIDE) + jnp.where(kind == 0, cross, step), SIDE)
+    return along * 2 * SIDE + over * 2 + kind
+
+
+def pack_body(slots, capacity, tagged, counts, emb, local, *rest):
+    tags = rest[0] if tagged else None
+    rest = rest[1:] if tagged else rest
     outs, (rows, labels, starts, done) = rest[: len(slots)], rest[len(slots) :]
     per_dev, width = emb.shape
     label_rows = local.shape[0]
@@ -67,8 +76,7 @@
         rows[per_dev:, :] = jnp.zeros((capacity + 16, width), BF16)
         fetch.wait()
 
-    here = lax.axis_index("rows")
-    x, y, core = here // (2 * SIDE), lax.rem(here // 2, SIDE), lax.rem(here, 2)
+    core = lax.rem(lax.axis_index("rows"), 2)
     line = iota((TAIL, LANES), 0) * LANES + iota((TAIL, LANES), 1)
     lane = iota((TAIL, LANES), 1)
     for (same_class, step, crosses), out in zip(slots, outs):
@@ -77,9 +85,7 @@
         def _():
             cross = at_step + crosses[0]
             kind = core if same_class else 1 - core
-            along = lax.rem(x + jnp.where(kind == 0, step, cross), SIDE)
-            over = lax.rem(y + jnp.where(kind == 0, cross, step), SIDE)
-            owner = along * 2 * SIDE + over * 2 + kind
+            owner = owner_of(kind, step, cross)
             first = starts[owner]
             count = counts[0, owner]
             aligned = first // 16
@@ -107,10 +113,13 @@
             live = line < count
             high = jnp.where(live, lax.shift_right_logical(value, 7), 64).astype(F32)
             low = jnp.where(live, value & 127, 0).astype(F32)
+            if crosses[0] == 0:
+                own_tags = [tags[pl.ds(owner_of(kind, step, c), 1), :] for c in range(SIDE)]
+                high = jnp.concatenate([high[: TAIL - SIDE]] + own_tags, axis=0)
             out[0, capacity:, :] = jnp.concatenate([high, low], axis=1).astype(BF16)
 
 
-def pack(slots, send_counts, embeddings, local, capacity):
+def pack(slots, send_counts, embeddings, local, capacity, tags=None):
     per_dev, width = embeddings.shape
     tall = capacity + TAIL
     longest = max(len(c) for _, _, c in slots)
@@ -120,14 +129,15 @@
 
     many = sum(len(c) for _, _, c in slots)
     return pl.pallas_call(
-        functools.partial(pack_body, slots, capacity),
+        functools.partial(pack_body, slots, capacity, tags is not None),
         grid=(longest,),
         out_shape=[jax.ShapeDtypeStruct((len(c), tall, width), BF16) for _, _, c in slots],
         in_specs=[
             pl.BlockSpec(memory_space=pltpu.SMEM),
             pl.BlockSpec(memory_space=pl.ANY),
             pl.BlockSpec(local.shape, lambda q: (0, 0)),
-        ],
+        ]
+        + ([] if tags is None else [pl.BlockSpec(tags.shape, lambda q: (0, 0))]),
         out_specs=[spec(len(c)) for _, _, c in slots],
         scratch_shapes=[
             pltpu.VMEM((per_dev + capacity + 16, width), BF16),
@@ -142,7 +152,7 @@
         ),
         compiler_params=pltpu.CompilerParams(vmem_limit_bytes=60 * MIB),
         name="pack_rows",
-    )(send_counts, embeddings, local)
+    )(send_counts, embeddings, local, *([] if tags is None else [tags]))
 
 
 def sums_body(sources, capacity, blocks, had, sent, *refs):
@@ -258,7 +268,7 @@
             bytes_accessed=many * (sources * tall * width * 2 + fine_dev * width * 8),
             transcendentals=0,
         ),
-        compiler_params=pltpu.CompilerParams(vmem_limit_bytes=32 * MIB),
+        compiler_params=pltpu.CompilerParams(vmem_limit_bytes=(10 + 2 * sources) * MIB),
         name="line_sums",
     )(*operands)
 
@@ -355,72 +365,143 @@
     )(coarse_ids)
 
 
-def place_body(group, owner_hot, rank_hot, tags, new, out, placement):
+def place_body(slots, owner_hot, rank_hot, new, *refs):
+    outs, placement = refs[:-1], refs[-1]
     capacity, fine_dev = rank_hot.shape
-    for g in range(group):
-        row = jnp.broadcast_to(owner_hot[g : g + 1, :], (16, fine_dev)).astype(BF16)
-        for at in range(0, capacity, 16):
-            top = g * capacity + at
-            placement[top : top + 16, :] = rank_hot[at : at + 16, :] * row
-    sent = jnp.dot(placement[...], new[...], preferred_element_type=F32).astype(BF16)
-    for g in range(group):
-        out[g, :capacity, :] = sent[g * capacity : (g + 1) * capacity, :]
-        tag = jnp.broadcast_to(tags[g : g + 1, :], (TAIL, capacity))
-        out[g, capacity:, :] = jnp.concatenate([tag, tag], axis=1).astype(BF16)
-
-
-def place(owner_hot, rank_hot, tags, new_fine, group):
-    peers, fine_dev = owner_hot.shape
-    capacity = rank_hot.shape[0]
+    core = lax.rem(lax.axis_index("rows"), 2)
+    for (same_class, step), out in zip(slots, outs):
+        kind = core if same_class else 1 - core
+        for cross in range(SIDE):
+            row = owner_hot[pl.ds(owner_of(kind, step, cross), 1), :]
+            row = jnp.broadcast_to(row, (16, fine_dev)).astype(BF16)
+            for at in range(0, capacity, 16):
+                top = cross * capacity + at
+                placement[top : top + 16, :] = rank_hot[at : at + 16, :] * row
+        sent = jnp.dot(placement[...], new[...], preferred_element_type=F32).astype(BF16)
+        for cross in range(SIDE):
+            out[cross, :, :] = sent[cross * capacity : (cross + 1) * capacity, :]
+
+
+def place(slots, owner_hot, rank_hot, new_fine):
+    capacity, fine_dev = rank_hot.shape
     width = new_fine.shape[1]
-    whole = lambda a: pl.BlockSpec(a.shape, lambda i: (0, 0))
-    return pl.pallas_call(
-        functools.partial(place_body, group),
-        grid=(peers // group,),
-        out_shape=jax.ShapeDtypeStruct((peers, capacity + TAIL, width), BF16),
-        in_specs=[
-            pl.BlockSpec((group, fine_dev), lambda i: (i, 0)),
-            whole(rank_hot),
-            pl.BlockSpec((group, capacity), lambda i: (i, 0)),
-            whole(new_fine),
-        ],
-        out_specs=pl.BlockSpec((group, capacity + TAIL, width), lambda i: (i, 0, 0)),
-        scratch_shapes=[pltpu.VMEM((group * capacity, fine_dev), BF16)],
+    return pl.pallas_call(
+        functools.partial(place_body, slots),
+        out_shape=[jax.ShapeDtypeStruct((SIDE, capacity, width), BF16)] * len(slots),
+        scratch_shapes=[pltpu.VMEM((SIDE * capacity, fine_dev), BF16)],
         compiler_params=pltpu.CompilerParams(vmem_limit_bytes=24 * MIB),
+        cost_estimate=pl.CostEstimate(
+            flops=2 * len(slots) * SIDE * capacity * fine_dev * width,
+            bytes_accessed=fine_dev * width * 2,
+            transcendentals=0,
+        ),
         name="place_clusters",
-    )(owner_hot, rank_hot, tags, new_fine)
-
-
-def coarse_body(received, old, means, onehot, data):
-    peers, tall, _ = received.shape
-    capacity = tall - TAIL
-    coarse_dev = old.shape[0]
-    total = jnp.zeros((coarse_dev, capacity), F32)
+    )(owner_hot, rank_hot, new_fine)
+
+
+def tag_hot_body(sources, *refs):
+    tails, hot, digits = refs[:sources], refs[-2], refs[-1]
+    many, coarse_dev, depth = hot.shape
+    capacity = depth // sources
     row = iota((coarse_dev, capacity), 0).astype(F32) + 1.0
-    for p in range(peers):
-        tag = received[p, capacity:, :].astype(F32)[:1, :capacity]
-        hot = jnp.where(row == tag, 1.0, 0.0)
-        total = total + hot
-        onehot[:, p * capacity : (p + 1) * capacity] = hot.astype(BF16)
-        data[p * capacity : (p + 1) * capacity, :] = received[p, :capacity, :]
-    sums = jnp.dot(onehot[...], data[...], preferred_element_type=F32)
-    count = jnp.sum(total, axis=1, keepdims=True)
-    means[...] = ((sums + old[...].astype(F32)) / (count + 1.0)).astype(BF16)
-
-
-def coarse(received, old_coarse):
-    peers, tall, width = received.shape
-    deep = peers * (tall - TAIL)
+    for cross in range(many):
+        for s in range(sources):
+            at = TAIL - SIDE + cross
+            tag = tails[s][0].astype(F32)[at : at + 1, :capacity]
+            one = jnp.where(row == tag, 1.0, 0.0).astype(BF16)
+            hot[cross, :, s * capacity : (s + 1) * capacity] = one
+        count = lax.dot_general(
+            jnp.ones((8, depth), BF16),
+            hot[cross],
+            (((1,), (1,)), ((), ())),
+            preferred_element_type=F32,
+        )
+        tens = jnp.floor(count / 64.0)
+        digits[cross] = jnp.concatenate([tens, count - 64.0 * tens], axis=0).astype(BF16)
+
+
+def tag_hot(tagged, capacity, capacity_two, coarse_dev):
+    width = tagged[0].shape[2]
+    sources = len(tagged)
+    return pl.pallas_call(
+        functools.partial(tag_hot_body, sources),
+        grid=(1,),
+        out_shape=(
+            jax.ShapeDtypeStruct((SIDE, coarse_dev, sources * capacity_two), BF16),
+            jax.ShapeDtypeStruct((SIDE, 16, coarse_dev), BF16),
+        ),
+        in_specs=[pl.BlockSpec((1, TAIL, width), lambda i: (0, capacity // TAIL, 0))] * sources,
+        out_specs=(
+            pl.BlockSpec((SIDE, coarse_dev, sources * capacity_two), lambda i: (0, 0, 0)),
+            pl.BlockSpec((SIDE, 16, coarse_dev), lambda i: (0, 0, 0)),
+        ),
+        compiler_params=pltpu.CompilerParams(vmem_limit_bytes=12 * MIB),
+        name="tag_hot",
+    )(*tagged)
+
+
+def coarse_sums_body(sources, order, *refs):
+    arrived, (hot, digits), outs, data = (
+        refs[:sources],
+        refs[sources : sources + 2],
+        refs[sources + 2 : -1],
+        refs[-1],
+    )
+    capacity = arrived[0].shape[1]
+    coarse_dev = hot.shape[1]
+    for cross, out in zip(order, outs):
+        for s in range(sources):
+            data[s * capacity : (s + 1) * capacity, :] = arrived[s][cross]
+        total = jnp.dot(hot[cross], data[...], preferred_element_type=F32)
+        if cross == 0:
+            out[...] = total
+        else:
+            out[:coarse_dev, :] = total.astype(BF16)
+            out[coarse_dev:, :] = digits[cross]
+
+
+def coarse_sums(arrived, hot, digits, order):
+    capacity, width = arrived[0].shape[1:]
+    sources = len(arrived)
+    coarse_dev = hot.shape[1]
+    sent = jax.ShapeDtypeStruct((coarse_dev + 16, width), BF16)
+    kept = jax.ShapeDtypeStruct((coarse_dev, width), F32)
+    return pl.pallas_call(
+        functools.partial(coarse_sums_body, sources, order),
+        out_shape=[kept if c == 0 else sent for c in order],
+        scratch_shapes=[pltpu.VMEM((sources * capacity, width), BF16)],
+        compiler_params=pltpu.CompilerParams(vmem_limit_bytes=16 * MIB),
+        name="coarse_sums",
+    )(*arrived, hot, digits)
+
+
+def coarse_body(acc, digits, old, *refs):
+    got, means = refs[:-1], refs[-1]
+    coarse_dev, _ = acc.shape
+    total = acc[...] + old[...].astype(F32)
+    tens = digits[0, :8, :].astype(F32)
+    ones = digits[0, 8:, :].astype(F32)
+    for g in got:
+        total = total + g[:coarse_dev, :].astype(F32)
+        tens = tens + g[coarse_dev : coarse_dev + 8, :].astype(F32)
+        ones = ones + g[coarse_dev + 8 :, :].astype(F32)
+    eye = jnp.where(
+        iota((coarse_dev, coarse_dev), 0) == iota((coarse_dev, coarse_dev), 1), 1.0, 0.0
+    ).astype(BF16)
+    turn = lambda a: lax.dot_general(
+        eye, a.astype(BF16), (((1,), (1,)), ((), ())), preferred_element_type=F32
+    )
+    count = turn(tens) * 64.0 + turn(ones)
+    means[...] = (total / (count[:, :1] + 1.0)).astype(BF16)
+
+
+def coarse(acc, digits, old_coarse, got):
     return pl.pallas_call(
         coarse_body,
         out_shape=jax.ShapeDtypeStruct(old_coarse.shape, BF16),
-        scratch_shapes=[
-            pltpu.VMEM((old_coarse.shape[0], deep), BF16),
-            pltpu.VMEM((deep, width), BF16),
-        ],
-        compiler_params=pltpu.CompilerParams(vmem_limit_bytes=24 * MIB),
+        compiler_params=pltpu.CompilerParams(vmem_limit_bytes=8 * MIB),
         name="coarse_means",
-    )(received, old_coarse)
+    )(acc, digits, old_coarse, *got)
 
 
 def finish_body(groups, at, *refs):
@@ -446,10 +527,6 @@
         compiler_params=pltpu.CompilerParams(vmem_limit_bytes=24 * MIB),
         name="coarse_dirs",
     )(at, *pieces)
-
-
-def exchange(slots):
-    return lax.all_to_all(slots, "rows", split_axis=0, concat_axis=0, tiled=True)
 
 
 def level_step(embeddings, fine_local, send_counts, old_fine, coarse_ids, old_coarse):
@@ -474,17 +551,18 @@
     kept = []
     for s, a in zip(order, keep):
         kept.append(along(a, s, True))
+    owner_hot, rank_hot, tags = plan(
+        coarse_ids.reshape(1, -1), peers, capacity_two, coarse_dev
+    )
     more = pack(
         [(False, s, sent) for s in order]
         + [(False, 0, own + sent), (True, 0, own + sent)]
         + [(k, s, own) for k in (True, False) for s in order],
         *rows,
+        tags,
     )
     swapped = along(more[3], 0, False)
     given = [along(a, s, False) for s, a in zip(order, more[:3])]
-    owner_hot, rank_hot, tags = plan(
-        coarse_ids.reshape(1, -1), peers, capacity_two, coarse_dev
-    )
     near = [(more[4], 0), (swapped, 0)]
     had = line_sums(near + [(kept[0], 1)], capacity, fine_dev, sent)
     had = line_sums([(a, 1) for a in kept[1:]], capacity, fine_dev, sent, (*had, 1))
@@ -497,10 +575,26 @@
         )
         got[cross] = lax.ppermute(part, "rows", cross_pairs(cross))
     acc, counts = line_sums(near + [(a, 0) for a in kept_own + given_own], capacity, fine_dev, own)
+    hot, digits = tag_hot(
+        [more[4], swapped] + kept_own + given_own, capacity, capacity_two, coarse_dev
+    )
     new_fine = update(acc, counts, old_fine, [got[c] for c in steps])
 
-    received = exchange(place(owner_hot, rank_hot, tags, new_fine, 8))
-    means = coarse(received, old_coarse)
+    keep = place([(True, s) for s in order], owner_hot, rank_hot, new_fine)
+    arrived = []
+    for s, a in zip(order, keep):
+        arrived.append(along(a, s, True))
+    give = place(
+        [(False, s) for s in order] + [(False, 0), (True, 0)], owner_hot, rank_hot, new_fine
+    )
+    for s, a in zip(order, give):
+        arrived.append(along(a, s, False))
+    arrived = [give[4], along(give[3], 0, False)] + arrived
+    *sent_sums, acc = coarse_sums(arrived, hot, digits, order + own)
+    got = []
+    for cross, part in zip(order, sent_sums):
+        got.append(lax.ppermute(part, "rows", cross_pairs(cross)))
+    means = coarse(acc, digits, old_coarse, got)
     pieces = [means]
     for step in range(1, groups):
         back = [((g + step) % groups, g) for g in range(groups)]

time: 172 us -> 158 us (0.919)
  blocking collectives: 38.3 us -> 0 us
  waiting for transfers between devices: 42.7 us -> 65.1 us
    all_to_all x1 -> x0, blocking collectives: 38.3 us -> none  [exchange(): lax.all_to_all(slots, 'rows', split_axis=0, concat_axis=0, tiled=True)]
    ppermute x13 -> x20, waiting for transfers between devices: 34.7 us -> 54 us  [along(): return lax.ppermute(slots, 'rows', line_pairs(step, same_class))]
    ppermute x0 -> x3, starting transfers between devices: none -> 4.52 us  [level_step(): got.append(lax.ppermute(part, 'rows', cross_pairs(cross)))]
    ppermute x0 -> x3, waiting for transfers between devices: none -> 3.61 us  [level_step(): got.append(lax.ppermute(part, 'rows', cross_pairs(cross)))]
    ppermute x13 -> x20, starting transfers between devices: 29.4 us -> 26.2 us  [along(): return lax.ppermute(slots, 'rows', line_pairs(step, same_class))]
    pallas_call x3 -> x6, Pallas kernels: 18.4 us -> 19.6 us  [the longest x2 13.4 us: pack(): pl.pallas_call(functools.partial(pack_body, slots, capacity, tags is not...]
  transfers between devices with their start and end apart: 19 -> 29, of which waited for: 8 -> 13; matrix products, arithmetic and copies ran while one was open for 0% -> 0% of each run, Pallas kernels for 18% -> 21%
where the time goes in v2:
time: 158 us; the launch traced here: 157 us
  waiting for transfers between devices  65.1 us (41%)
  Pallas kernels  47.8 us (30%)
  starting transfers between devices  40.9 us (26%)
  local copies, waits for them, and re-layouts  2.57 us (2%)
    ppermute x20, waiting for transfers between devices, along(): return lax.ppermute(slots, 'rows', line_pairs(step, same_class))  54 us
    ppermute x20, starting transfers between devices, along(): return lax.ppermute(slots, 'rows', line_pairs(step, same_class))  26.2 us
    pallas_call x6, Pallas kernels, line_sums(): pl.pallas_call(functools.partial(sums_body, sources, capacity, blocks, ha...  24.1 us
    pallas_call x2, Pallas kernels, pack(): pl.pallas_call(functools.partial(pack_body, slots, capacity, tags is not...  13.4 us
    ppermute x3, waiting for transfers between devices, level_step(): pieces.append(lax.ppermute(means, 'grp', back))  7.45 us
    ppermute x3, starting transfers between devices, level_step(): pieces.append(lax.ppermute(means, 'grp', back))  5.37 us
    ppermute x3, starting transfers between devices, level_step(): got[cross] = lax.ppermute(part, 'rows', cross_pairs(cross))  4.83 us
    pallas_call x2, Pallas kernels, place(): pl.pallas_call(functools.partial(place_body, slots), out_shape=[jax.Shape...  4.69 us
  transfers between devices with their start and end apart: 29, of which 13 were waited for; matrix products, arithmetic and copies ran while one was open for 0% of the time, Pallas kernels for 21%

profile of v2, /device:TPU:0, one launch (start us, length us, event | category | flops | bytes accessed | tf_op | source)
XLA Modules:
  0.0 157.3 jit_solution(17865567789796592574)
XLA Ops:
  2.5 7.8 %pack_rows.2 = (bf16[3,520,256]{2,1,0:T(8,128)(2,1)}, bf16[3,520,256]{2,1,0:T(8,128)(2,1)}, bf16[3,520,256]{2,1,0:T(8,128)(2,1)}, bf16[4,520,256]{2,1,0:T(8,128)...) custom-call(s32[1,32]{1,0:T(1,128)} %counts.3, ...), custom_call_target="tpu_custom_call" | custom-call | bytes 10317824 | tf_op jit(solution)/shard_map/pack_rows/pallas_call | solution.py:131
  10.5 5.6 %pack_rows.3 = (bf16[3,520,256]{2,1,0:T(8,128)(2,1)}, bf16[3,520,256]{2,1,0:T(8,128)(2,1)}, bf16[3,520,256]{2,1,0:T(8,128)(2,1)}) custom-call(s32[1,32]{1,0:T(1,128)} %counts.3, bf16[8192,256]{1,0:T(8,128)(2,1)} %emb.3, s32[64,128]{1,0:T(8,128)} %bitcast.5), custom_call_target="tpu_custom_call" | custom-call | bytes 6590464 | tf_op jit(solution)/shard_map/pack_rows/pallas_call | solution.py:131
  16.1 3.2 %collective-permute-start.12 = (bf16[3,520,256]{2,1,0:T(8,128)(2,1)}, bf16[3,520,256]{2,1,0:T(8,128)(2,1)S(1)}, u32[]{:S(2)}, u32[]{:S(2)}) collective-permute-start(bf16[3,520,256]{2,1,0:T(8,128)(2,1)} %get-tuple-element.55), channel_id=1, source_target_pairs={{0,64},{4,20},{8,72},{12,28},{16,80},{20,4},{24,88},{28,12},{32,96... | collective-permute-start | bytes 2396168 | tf_op jit(solution)/shard_map/ppermute | solution.py:544
  19.9 2.6 %collective-permute-start.11 = (bf16[3,520,256]{2,1,0:T(8,128)(2,1)}, bf16[3,520,256]{2,1,0:T(8,128)(2,1)S(1)}, u32[]{:S(2)}, u32[]{:S(2)}) collective-permute-start(bf16[3,520,256]{2,1,0:T(8,128)(2,1)} %get-tuple-element.54), channel_id=1, source_target_pairs={{0,96},{4,28},{8,104},{12,4},{16,112},{20,12},{24,120},{28,20},{32... | collective-permute-start | bytes 2396168 | tf_op jit(solution)/shard_map/ppermute | solution.py:544
  22.5 13.1 %collective-permute-done.12.refs_2_ = bf16[3,520,256]{2,1,0:T(8,128)(2,1)S(1)} collective-permute-done((bf16[3,520,256]{2,1,0:T(8,128)(2,1)}, bf16[3,520,256]{2,1,0:T(8,128)(2,1)S(1)}, u32[]{:S(2)}, u32[]{:S(2)}) %collective-permute-start.12) | collective-permute-done | bytes 798752 | tf_op jit(solution)/shard_map/ppermute | solution.py:544
  35.7 3.8 %collective-permute-start.9 = (bf16[3,520,256]{2,1,0:T(8,128)(2,1)S(1)}, bf16[3,520,256]{2,1,0:T(8,128)(2,1)S(1)}, u32[]{:S(2)}, u32[]{:S(2)}) collective-permute-start(bf16[3,520,256]{2,1,0:T(8,128)(2,1)S(1)} %copy-done.6), channel_id=1, source_target_pairs={{0,28},{4,96},{8,4},{12,104},{16,12},{20,112},{24,20},{28,120},{32... | collective-permute-start | bytes 2396168 | tf_op jit(solution)/shard_map/ppermute | solution.py:544
  39.4 6.8 %line_sums.7 = (f32[3,2048,256]{2,1,0:T(8,128)S(1)}, f32[3,16,128]{2,1,0:T(8,128)S(1)}) custom-call(bf16[4,520,256]{2,1,0:T(8,128)(2,1)S(1)} %copy-done, bf16[4,520,256]{2,1,0:T(8,128)(2,1)S(1)} %collective-permute-done.refs_1_, bf16[3,520,256]{2,1,0:T(8,128)(2,1)S(1)} %collective-permute-done.12.refs_2_), custom_call_target="tpu_custom_call" | custom-call | flops 4831838208 | bytes 14979072 | tf_op jit(solution)/shard_map/line_sums/pallas_call | solution.py:254
  46.3 6.5 %collective-permute-done.10.refs_0_ = bf16[3,520,256]{2,1,0:T(8,128)(2,1)S(1)} collective-permute-done((bf16[3,520,256]{2,1,0:T(8,128)(2,1)}, bf16[3,520,256]{2,1,0:T(8,128)(2,1)S(1)}, u32[]{:S(2)}, u32[]{:S(2)}) %collective-permute-start.10) | collective-permute-done | bytes 798752 | tf_op jit(solution)/shard_map/ppermute | solution.py:544
  55.4 5.1 %line_sums.8 = (f32[3,2048,256]{2,1,0:T(8,128)S(1)}, f32[3,16,128]{2,1,0:T(8,128)S(1)}) custom-call(bf16[3,520,256]{2,1,0:T(8,128)(2,1)S(1)} %collective-permute-done.10.refs_0_, bf16[3,520,256]{2,1,0:T(8,128)(2,1)S(1)} %collective-permute-done.11.refs_1_, f32[3,2048,256]{2,1,0:T(8,128)S(1)} %get-tuple-element.56.refs_2_, ...), custom_call_target="tpu_custom_call" | custom-call | flops 3221225472 | bytes 14180352 | tf_op jit(solution)/shard_map/line_sums/pallas_call | solution.py:254
  62.8 3.1 %collective-permute-start.15 = (bf16[2064,256]{1,0:T(8,128)(2,1)S(1)}, bf16[2064,256]{1,0:T(8,128)(2,1)S(1)}, u32[]{:S(2)}, u32[]{:S(2)}) collective-permute-start(bf16[2064,256]{1,0:T(8,128)(2,1)S(1)} %line_sums.11), channel_id=1, source_target_pairs={{0,24},{4,100},{8,0},{12,108},{16,8},{20,116},{24,16},{28,124},{32... | collective-permute-start | bytes 3170312 | tf_op jit(solution)/shard_map/ppermute | solution.py:576
  72.3 3.2 %collective-permute-start.3 = (bf16[1,520,256]{2,1,0:T(8,128)(2,1)S(1)}, bf16[1,520,256]{2,1,0:T(8,128)(2,1)S(1)}, u32[]{:S(2)}, u32[]{:S(2)}) collective-permute-start(bf16[1,520,256]{2,1,0:T(8,128)(2,1)S(1)} %copy-done.10), channel_id=1, source_target_pairs={{0,96},{4,28},{8,104},{12,4},{16,112},{20,12},{24,120},{28,20},{32... | collective-permute-start | bytes 798728 | tf_op jit(solution)/shard_map/ppermute | solution.py:544
  75.5 18.0 %collective-permute-done.3.refs_4_ = bf16[1,520,256]{2,1,0:T(8,128)(2,1)S(1)} collective-permute-done((bf16[1,520,256]{2,1,0:T(8,128)(2,1)S(1)}, bf16[1,520,256]{2,1,0:T(8,128)(2,1)S(1)}, u32[]{:S(2)}, u32[]{:S(2)}) %collective-permute-start.3) | collective-permute-done | bytes 266272 | tf_op jit(solution)/shard_map/ppermute | solution.py:544
  93.6 3.3 %collective-permute-done.4.refs_5_ = bf16[1,520,256]{2,1,0:T(8,128)(2,1)S(1)} collective-permute-done((bf16[1,520,256]{2,1,0:T(8,128)(2,1)S(1)}, bf16[1,520,256]{2,1,0:T(8,128)(2,1)S(1)}, u32[]{:S(2)}, u32[]{:S(2)}) %collective-permute-start.4) | collective-permute-done | bytes 266272 | tf_op jit(solution)/shard_map/ppermute | solution.py:544
  97.3 3.4 %collective-permute-done.5.refs_6_ = bf16[1,520,256]{2,1,0:T(8,128)(2,1)S(1)} collective-permute-done((bf16[1,520,256]{2,1,0:T(8,128)(2,1)S(1)}, bf16[1,520,256]{2,1,0:T(8,128)(2,1)S(1)}, u32[]{:S(2)}, u32[]{:S(2)}) %collective-permute-start.5) | collective-permute-done | bytes 266272 | tf_op jit(solution)/shard_map/ppermute | solution.py:544
  100.6 2.9 %collective-permute-done.6.refs_7_ = bf16[1,520,256]{2,1,0:T(8,128)(2,1)S(1)} collective-permute-done((bf16[1,520,256]{2,1,0:T(8,128)(2,1)S(1)}, bf16[1,520,256]{2,1,0:T(8,128)(2,1)S(1)}, u32[]{:S(2)}, u32[]{:S(2)}) %collective-permute-start.6) | collective-permute-done | bytes 266272 | tf_op jit(solution)/shard_map/ppermute | solution.py:544
  103.5 5.3 %line_sums.6 = (f32[1,2048,256]{2,1,0:T(8,128)S(1)}, f32[1,16,128]{2,1,0:T(8,128)S(1)}) custom-call(bf16[4,520,256]{2,1,0:T(8,128)(2,1)S(1)} %copy-done, bf16[4,520,256]{2,1,0:T(8,128)(2,1)S(1)} %collective-permute-done.refs_1_, bf16[1,520,256]{2,1,0:T(8,128)(2,1)S(1)} %collective-permute-done.1.refs_2_, ...), custom_call_target="tpu_custom_call" | custom-call | flops 4294967296 | bytes 6324224 | tf_op jit(solution)/shard_map/line_sums/pallas_call | solution.py:254
  114.0 3.8 %collective-permute-start.17 = (bf16[4,128,256]{2,1,0:T(8,128)(2,1)S(1)}, bf16[4,128,256]{2,1,0:T(8,128)(2,1)S(1)}, u32[]{:S(2)}, u32[]{:S(2)}) collective-permute-start(bf16[4,128,256]{2,1,0:T(8,128)(2,1)S(1)} %get-tuple-element.64), channel_id=1, source_target_pairs={{0,64},{4,20},{8,72},{12,28},{16,80},{20,4},{24,88},{28,12},{32,96... | collective-permute-start | bytes 786440 | tf_op jit(solution)/shard_map/ppermute | solution.py:544
  117.8 3.2 %collective-permute-start.19 = (bf16[4,128,256]{2,1,0:T(8,128)(2,1)S(1)}, bf16[4,128,256]{2,1,0:T(8,128)(2,1)S(1)}, u32[]{:S(2)}, u32[]{:S(2)}) collective-permute-start(bf16[4,128,256]{2,1,0:T(8,128)(2,1)S(1)} %get-tuple-element.66), channel_id=1, source_target_pairs={{0,96},{4,28},{8,104},{12,4},{16,112},{20,12},{24,120},{28,20},{32... | collective-permute-start | bytes 786440 | tf_op jit(solution)/shard_map/ppermute | solution.py:544
  121.0 2.9 %place_clusters.2 = (bf16[4,128,256]{2,1,0:T(8,128)(2,1)S(1)}, bf16[4,128,256]{2,1,0:T(8,128)(2,1)S(1)}, bf16[4,128,256]{2,1,0:T(8,128)(2,1)S(1)}, bf16[4,128,25...) custom-call(f32[32,2048]{1,0:T(8,128)S(1)} %get-tuple-element.60.owner_hot, bf16[128,2048]{1,0:T(8,128)(2,1)S(1)} %get-tuple-element.61.rank_hot, ...), custom_call_target="tpu_custom_call" | custom-call | flops 2684354560 | bytes 1048576 | tf_op jit(solution)/shard_map/place_clusters/pallas_call | solution.py:388
  127.5 4.1 %collective-permute-done.20.refs_5_ = bf16[4,128,256]{2,1,0:T(8,128)(2,1)S(1)} collective-permute-done((bf16[4,128,256]{2,1,0:T(8,128)(2,1)S(1)}, bf16[4,128,256]{2,1,0:T(8,128)(2,1)S(1)}, u32[]{:S(2)}, u32[]{:S(2)}) %collective-permute-start.20) | collective-permute-done | bytes 262176 | tf_op jit(solution)/shard_map/ppermute | solution.py:544
  131.5 2.7 %collective-permute-done.21.refs_6_ = bf16[4,128,256]{2,1,0:T(8,128)(2,1)S(1)} collective-permute-done((bf16[4,128,256]{2,1,0:T(8,128)(2,1)S(1)}, bf16[4,128,256]{2,1,0:T(8,128)(2,1)S(1)}, u32[]{:S(2)}, u32[]{:S(2)}) %collective-permute-start.21) | collective-permute-done | bytes 262176 | tf_op jit(solution)/shard_map/ppermute | solution.py:544
  136.7 2.7 %collective-permute-start.25 = (bf16[272,256]{1,0:T(8,128)(2,1)S(1)}, bf16[272,256]{1,0:T(8,128)(2,1)S(1)}, u32[]{:S(2)}, u32[]{:S(2)}) collective-permute-start(bf16[272,256]{1,0:T(8,128)(2,1)S(1)} %get-tuple-element.75), channel_id=1, source_target_pairs={{0,24},{4,100},{8,0},{12,108},{16,8},{20,116},{24,16},{28,124},{32... | collective-permute-start | bytes 417800 | tf_op jit(solution)/shard_map/ppermute | solution.py:596
  143.4 4.1 %collective-permute-start.26 = (bf16[256,256]{1,0:T(8,128)(2,1)S(1)}, bf16[256,256]{1,0:T(8,128)(2,1)S(1)}, u32[]{:S(2)}, u32[]{:S(2)}) collective-permute-start(bf16[256,256]{1,0:T(8,128)(2,1)S(1)} %coarse_means.1.refs_0_), channel_id=1, source_target_pairs={{1,0},{2,1},{3,2},{0,3},{5,4},{6,5},{7,6},{4,7},{9,8},{10,9},{11,1... | collective-permute-start | bytes 393224 | tf_op jit(solution)/shard_map/ppermute | solution.py:601
  148.7 4.0 %collective-permute-done.26.refs_1_ = bf16[256,256]{1,0:T(8,128)(2,1)S(1)} collective-permute-done((bf16[256,256]{1,0:T(8,128)(2,1)S(1)}, bf16[256,256]{1,0:T(8,128)(2,1)S(1)}, u32[]{:S(2)}, u32[]{:S(2)}) %collective-permute-start.26) | collective-permute-done | bytes 131104 | tf_op jit(solution)/shard_map/ppermute | solution.py:601
  (76 shorter events, 35.1 us)
Async XLA Ops:
  10.4 25.3 %collective-permute-start = (bf16[4,520,256]{2,1,0:T(8,128)(2,1)}, bf16[4,520,256]{2,1,0:T(8,128)(2,1)S(1)}, u32[]{:S(2)}, u32[]{:S(2)}) collective-permute-start(bf16[4,520,256]{2,1,0:T(8,128)(2,1)} %get-tuple-element.41), channel_id=1, source_target_pairs={{0,4},{4,0},{8,12},{12,8},{16,20},{20,16},{24,28},{28,24},{32,36},... | collective-permute-start | bytes 3194888 | tf_op jit(solution)/shard_map/ppermute | solution.py:544
  16.1 19.6 %collective-permute-start.12 = (bf16[3,520,256]{2,1,0:T(8,128)(2,1)}, bf16[3,520,256]{2,1,0:T(8,128)(2,1)S(1)}, u32[]{:S(2)}, u32[]{:S(2)}) collective-permute-start(bf16[3,520,256]{2,1,0:T(8,128)(2,1)} %get-tuple-element.55), channel_id=1, source_target_pairs={{0,64},{4,20},{8,72},{12,28},{16,80},{20,4},{24,88},{28,12},{32,96... | collective-permute-start | bytes 2396168 | tf_op jit(solution)/shard_map/ppermute | solution.py:544
  19.3 33.5 %collective-permute-start.10 = (bf16[3,520,256]{2,1,0:T(8,128)(2,1)}, bf16[3,520,256]{2,1,0:T(8,128)(2,1)S(1)}, u32[]{:S(2)}, u32[]{:S(2)}) collective-permute-start(bf16[3,520,256]{2,1,0:T(8,128)(2,1)} %get-tuple-element.53), channel_id=1, source_target_pairs={{0,32},{4,12},{8,40},{12,20},{16,48},{20,28},{24,56},{28,4},{32,64... | collective-permute-start | bytes 2396168 | tf_op jit(solution)/shard_map/ppermute | solution.py:544
  19.9 35.5 %collective-permute-start.11 = (bf16[3,520,256]{2,1,0:T(8,128)(2,1)}, bf16[3,520,256]{2,1,0:T(8,128)(2,1)S(1)}, u32[]{:S(2)}, u32[]{:S(2)}) collective-permute-start(bf16[3,520,256]{2,1,0:T(8,128)(2,1)} %get-tuple-element.54), channel_id=1, source_target_pairs={{0,96},{4,28},{8,104},{12,4},{16,112},{20,12},{24,120},{28,20},{32... | collective-permute-start | bytes 2396168 | tf_op jit(solution)/shard_map/ppermute | solution.py:544
  22.5 38.0 %collective-permute-start.7 = (bf16[3,520,256]{2,1,0:T(8,128)(2,1)}, bf16[3,520,256]{2,1,0:T(8,128)(2,1)S(1)}, u32[]{:S(2)}, u32[]{:S(2)}) collective-permute-start(bf16[3,520,256]{2,1,0:T(8,128)(2,1)} %get-tuple-element.50), channel_id=1, source_target_pairs={{0,20},{4,64},{8,28},{12,72},{16,4},{20,80},{24,12},{28,88},{32,52... | collective-permute-start | bytes 2396168 | tf_op jit(solution)/shard_map/ppermute | solution.py:544
  35.7 24.8 %collective-permute-start.8 = (bf16[3,520,256]{2,1,0:T(8,128)(2,1)}, bf16[3,520,256]{2,1,0:T(8,128)(2,1)S(1)}, u32[]{:S(2)}, u32[]{:S(2)}) collective-permute-start(bf16[3,520,256]{2,1,0:T(8,128)(2,1)} %get-tuple-element.51), channel_id=1, source_target_pairs={{0,12},{4,32},{8,20},{12,40},{16,28},{20,48},{24,4},{28,56},{32,44... | collective-permute-start | bytes 2396168 | tf_op jit(solution)/shard_map/ppermute | solution.py:544
  35.7 24.8 %collective-permute-start.9 = (bf16[3,520,256]{2,1,0:T(8,128)(2,1)S(1)}, bf16[3,520,256]{2,1,0:T(8,128)(2,1)S(1)}, u32[]{:S(2)}, u32[]{:S(2)}) collective-permute-start(bf16[3,520,256]{2,1,0:T(8,128)(2,1)S(1)} %copy-done.6), channel_id=1, source_target_pairs={{0,28},{4,96},{8,4},{12,104},{16,12},{20,112},{24,20},{28,120},{32... | collective-permute-start | bytes 2396168 | tf_op jit(solution)/shard_map/ppermute | solution.py:544
  52.8 19.5 %collective-permute-start.1 = (bf16[1,520,256]{2,1,0:T(8,128)(2,1)S(1)}, bf16[1,520,256]{2,1,0:T(8,128)(2,1)S(1)}, u32[]{:S(2)}, u32[]{:S(2)}) collective-permute-start(bf16[1,520,256]{2,1,0:T(8,128)(2,1)S(1)} %copy-done.12), channel_id=1, source_target_pairs={{0,64},{4,20},{8,72},{12,28},{16,80},{20,4},{24,88},{28,12},{32,96... | collective-permute-start | bytes 798728 | tf_op jit(solution)/shard_map/ppermute | solution.py:544
  55.4 20.1 %collective-permute-start.2 = (bf16[1,520,256]{2,1,0:T(8,128)(2,1)S(1)}, bf16[1,520,256]{2,1,0:T(8,128)(2,1)S(1)}, u32[]{:S(2)}, u32[]{:S(2)}) collective-permute-start(bf16[1,520,256]{2,1,0:T(8,128)(2,1)S(1)} %copy-done.11), channel_id=1, source_target_pairs={{0,32},{4,12},{8,40},{12,20},{16,48},{20,28},{24,56},{28,4},{32,64... | collective-permute-start | bytes 798728 | tf_op jit(solution)/shard_map/ppermute | solution.py:544
  62.8 45.9 %collective-permute-start.15 = (bf16[2064,256]{1,0:T(8,128)(2,1)S(1)}, bf16[2064,256]{1,0:T(8,128)(2,1)S(1)}, u32[]{:S(2)}, u32[]{:S(2)}) collective-permute-start(bf16[2064,256]{1,0:T(8,128)(2,1)S(1)} %line_sums.11), channel_id=1, source_target_pairs={{0,24},{4,100},{8,0},{12,108},{16,8},{20,116},{24,16},{28,124},{32... | collective-permute-start | bytes 3170312 | tf_op jit(solution)/shard_map/ppermute | solution.py:576
  68.2 40.5 %collective-permute-start.14 = (bf16[2064,256]{1,0:T(8,128)(2,1)S(1)}, bf16[2064,256]{1,0:T(8,128)(2,1)S(1)}, u32[]{:S(2)}, u32[]{:S(2)}) collective-permute-start(bf16[2064,256]{1,0:T(8,128)(2,1)S(1)} %line_sums.10), channel_id=1, source_target_pairs={{0,16},{4,68},{8,24},{12,76},{16,0},{20,84},{24,8},{28,92},{32,48}... | collective-permute-start | bytes 3170312 | tf_op jit(solution)/shard_map/ppermute | solution.py:576
  71.2 37.5 %collective-permute-start.13 = (bf16[2064,256]{1,0:T(8,128)(2,1)S(1)}, bf16[2064,256]{1,0:T(8,128)(2,1)S(1)}, u32[]{:S(2)}, u32[]{:S(2)}) collective-permute-start(bf16[2064,256]{1,0:T(8,128)(2,1)S(1)} %line_sums.9), channel_id=1, source_target_pairs={{0,8},{4,36},{8,16},{12,44},{16,24},{20,52},{24,0},{28,60},{32,40}... | collective-permute-start | bytes 3170312 | tf_op jit(solution)/shard_map/ppermute | solution.py:576
  72.3 21.3 %collective-permute-start.3 = (bf16[1,520,256]{2,1,0:T(8,128)(2,1)S(1)}, bf16[1,520,256]{2,1,0:T(8,128)(2,1)S(1)}, u32[]{:S(2)}, u32[]{:S(2)}) collective-permute-start(bf16[1,520,256]{2,1,0:T(8,128)(2,1)S(1)} %copy-done.10), channel_id=1, source_target_pairs={{0,96},{4,28},{8,104},{12,4},{16,112},{20,12},{24,120},{28,20},{32... | collective-permute-start | bytes 798728 | tf_op jit(solution)/shard_map/ppermute | solution.py:544
  75.5 21.4 %collective-permute-start.4 = (bf16[1,520,256]{2,1,0:T(8,128)(2,1)S(1)}, bf16[1,520,256]{2,1,0:T(8,128)(2,1)S(1)}, u32[]{:S(2)}, u32[]{:S(2)}) collective-permute-start(bf16[1,520,256]{2,1,0:T(8,128)(2,1)S(1)} %copy-done.9), channel_id=1, source_target_pairs={{0,20},{4,64},{8,28},{12,72},{16,4},{20,80},{24,12},{28,88},{32,52... | collective-permute-start | bytes 798728 | tf_op jit(solution)/shard_map/ppermute | solution.py:544
  93.6 7.1 %collective-permute-start.5 = (bf16[1,520,256]{2,1,0:T(8,128)(2,1)S(1)}, bf16[1,520,256]{2,1,0:T(8,128)(2,1)S(1)}, u32[]{:S(2)}, u32[]{:S(2)}) collective-permute-start(bf16[1,520,256]{2,1,0:T(8,128)(2,1)S(1)} %copy-done.8), channel_id=1, source_target_pairs={{0,12},{4,32},{8,20},{12,40},{16,28},{20,48},{24,4},{28,56},{32,44... | collective-permute-start | bytes 798728 | tf_op jit(solution)/shard_map/ppermute | solution.py:544
  114.0 11.3 %collective-permute-start.17 = (bf16[4,128,256]{2,1,0:T(8,128)(2,1)S(1)}, bf16[4,128,256]{2,1,0:T(8,128)(2,1)S(1)}, u32[]{:S(2)}, u32[]{:S(2)}) collective-permute-start(bf16[4,128,256]{2,1,0:T(8,128)(2,1)S(1)} %get-tuple-element.64), channel_id=1, source_target_pairs={{0,64},{4,20},{8,72},{12,28},{16,80},{20,4},{24,88},{28,12},{32,96... | collective-permute-start | bytes 786440 | tf_op jit(solution)/shard_map/ppermute | solution.py:544
  117.8 7.6 %collective-permute-start.18 = (bf16[4,128,256]{2,1,0:T(8,128)(2,1)S(1)}, bf16[4,128,256]{2,1,0:T(8,128)(2,1)S(1)}, u32[]{:S(2)}, u32[]{:S(2)}) collective-permute-start(bf16[4,128,256]{2,1,0:T(8,128)(2,1)S(1)} %get-tuple-element.65), channel_id=1, source_target_pairs={{0,32},{4,12},{8,40},{12,20},{16,48},{20,28},{24,56},{28,4},{32,64... | collective-permute-start | bytes 786440 | tf_op jit(solution)/shard_map/ppermute | solution.py:544
  117.8 9.6 %collective-permute-start.19 = (bf16[4,128,256]{2,1,0:T(8,128)(2,1)S(1)}, bf16[4,128,256]{2,1,0:T(8,128)(2,1)S(1)}, u32[]{:S(2)}, u32[]{:S(2)}) collective-permute-start(bf16[4,128,256]{2,1,0:T(8,128)(2,1)S(1)} %get-tuple-element.66), channel_id=1, source_target_pairs={{0,96},{4,28},{8,104},{12,4},{16,112},{20,12},{24,120},{28,20},{32... | collective-permute-start | bytes 786440 | tf_op jit(solution)/shard_map/ppermute | solution.py:544
  124.0 7.5 %collective-permute-start.20 = (bf16[4,128,256]{2,1,0:T(8,128)(2,1)S(1)}, bf16[4,128,256]{2,1,0:T(8,128)(2,1)S(1)}, u32[]{:S(2)}, u32[]{:S(2)}) collective-permute-start(bf16[4,128,256]{2,1,0:T(8,128)(2,1)S(1)} %get-tuple-element.67), channel_id=1, source_target_pairs={{0,20},{4,64},{8,28},{12,72},{16,4},{20,80},{24,12},{28,88},{32,52... | collective-permute-start | bytes 786440 | tf_op jit(solution)/shard_map/ppermute | solution.py:544
  125.3 8.9 %collective-permute-start.21 = (bf16[4,128,256]{2,1,0:T(8,128)(2,1)S(1)}, bf16[4,128,256]{2,1,0:T(8,128)(2,1)S(1)}, u32[]{:S(2)}, u32[]{:S(2)}) collective-permute-start(bf16[4,128,256]{2,1,0:T(8,128)(2,1)S(1)} %get-tuple-element.68), channel_id=1, source_target_pairs={{0,12},{4,32},{8,20},{12,40},{16,28},{20,48},{24,4},{28,56},{32,44... | collective-permute-start | bytes 786440 | tf_op jit(solution)/shard_map/ppermute | solution.py:544
  125.4 8.8 %collective-permute-start.22 = (bf16[4,128,256]{2,1,0:T(8,128)(2,1)S(1)}, bf16[4,128,256]{2,1,0:T(8,128)(2,1)S(1)}, u32[]{:S(2)}, u32[]{:S(2)}) collective-permute-start(bf16[4,128,256]{2,1,0:T(8,128)(2,1)S(1)} %get-tuple-element.69), channel_id=1, source_target_pairs={{0,28},{4,96},{8,4},{12,104},{16,12},{20,112},{24,20},{28,120},{32... | collective-permute-start | bytes 786440 | tf_op jit(solution)/shard_map/ppermute | solution.py:544
  143.4 9.4 %collective-permute-start.26 = (bf16[256,256]{1,0:T(8,128)(2,1)S(1)}, bf16[256,256]{1,0:T(8,128)(2,1)S(1)}, u32[]{:S(2)}, u32[]{:S(2)}) collective-permute-start(bf16[256,256]{1,0:T(8,128)(2,1)S(1)} %coarse_means.1.refs_0_), channel_id=1, source_target_pairs={{1,0},{2,1},{3,2},{0,3},{5,4},{6,5},{7,6},{4,7},{9,8},{10,9},{11,1... | collective-permute-start | bytes 393224 | tf_op jit(solution)/shard_map/ppermute | solution.py:601
  147.5 7.7 %collective-permute-start.27 = (bf16[256,256]{1,0:T(8,128)(2,1)S(1)}, bf16[256,256]{1,0:T(8,128)(2,1)S(1)}, u32[]{:S(2)}, u32[]{:S(2)}) collective-permute-start(bf16[256,256]{1,0:T(8,128)(2,1)S(1)} %coarse_means.1.refs_0_), channel_id=1, source_target_pairs={{2,0},{3,1},{0,2},{1,3},{6,4},{7,5},{4,6},{5,7},{10,8},{11,9},{8,1... | collective-permute-start | bytes 393224 | tf_op jit(solution)/shard_map/ppermute | solution.py:601
  147.5 8.7 %collective-permute-start.28 = (bf16[256,256]{1,0:T(8,128)(2,1)S(1)}, bf16[256,256]{1,0:T(8,128)(2,1)S(1)}, u32[]{:S(2)}, u32[]{:S(2)}) collective-permute-start(bf16[256,256]{1,0:T(8,128)(2,1)S(1)} %coarse_means.1.refs_0_), channel_id=1, source_target_pairs={{3,0},{0,1},{1,2},{2,3},{7,4},{4,5},{5,6},{6,7},{11,8},{8,9},{9,10... | collective-permute-start | bytes 393224 | tf_op jit(solution)/shard_map/ppermute | solution.py:601
  (18 other events, 202.3 us)

commit v3 on v2

--- a/solution.py
+++ b/solution.py
@@ -55,31 +55,44 @@
 def pack_body(slots, capacity, tagged, counts, emb, local, *rest):
     tags = rest[0] if tagged else None
     rest = rest[1:] if tagged else rest
-    outs, (rows, labels, starts, done) = rest[: len(slots)], rest[len(slots) :]
+    outs, (windows, labels, starts, done) = rest[: len(slots)], rest[len(slots) :]
     per_dev, width = emb.shape
+    span = capacity + 16
     label_rows = local.shape[0]
     owners = counts.shape[1]
     at_step = pl.program_id(0)
+    core = lax.rem(lax.axis_index("rows"), 2)
+
+    def fetch(at, cross, base):
+        low = jnp.minimum(base, per_dev - span)
+        return pltpu.make_async_copy(
+            emb.at[pl.ds(pl.multiple_of(low, 16), span), :],
+            windows.at[at, cross, :span, :],
+            done.at[at, cross],
+        )
 
     @pl.when(at_step == 0)
     def _():
-        fetch = pltpu.make_async_copy(emb, rows.at[:per_dev, :], done)
-        fetch.start()
-
         def add(o, total):
             starts[o] = total
             return total + counts[0, o]
 
         lax.fori_loop(0, owners, add, 0)
+        for cross in range(max(len(c) for _, _, c in slots)):
+            for at, (same_class, step, crosses) in enumerate(slots):
+                if cross < len(crosses):
+                    kind = core if same_class else 1 - core
+                    first = starts[owner_of(kind, step, crosses[cross])]
+                    fetch(at, cross, first // 16 * 16).start()
         labels[:label_rows, :] = local[...]
         labels[label_rows:, :] = jnp.zeros((16, LANES), jnp.int32)
-        rows[per_dev:, :] = jnp.zeros((capacity + 16, width), BF16)
-        fetch.wait()
-
-    core = lax.rem(lax.axis_index("rows"), 2)
+        for at, (_, _, crosses) in enumerate(slots):
+            for cross in range(len(crosses)):
+                windows[at, cross, span:, :] = jnp.zeros((80, width), BF16)
+
     line = iota((TAIL, LANES), 0) * LANES + iota((TAIL, LANES), 1)
     lane = iota((TAIL, LANES), 1)
-    for (same_class, step, crosses), out in zip(slots, outs):
+    for at_slot, ((same_class, step, crosses), out) in enumerate(zip(slots, outs)):
 
         @pl.when(at_step < len(crosses))
         def _():
@@ -88,14 +101,17 @@
             owner = owner_of(kind, step, cross)
             first = starts[owner]
             count = counts[0, owner]
-            aligned = first // 16
-            turn = first - aligned * 16
+            base16 = first // 16 * 16
+            turn = first - base16
             far = turn >= 8
             small = jnp.where(far, turn - 8, turn)
             turn_back = lax.rem(8 - small, 8)
             kept = iota((9, 8, width), 1) < 8 - small
+            behind = base16 - jnp.minimum(base16, per_dev - span)
+            fetch(at_slot, at_step, base16).wait()
             for at in range(0, capacity, 64):
-                window = rows[pl.ds(pl.multiple_of(aligned * 16 + at, 16), 80), :]
+                top = pl.multiple_of(jnp.minimum(behind + at, span), 16)
+                window = windows[at_slot, at_step, pl.ds(top, 80), :]
                 window = window.astype(F32).reshape(10, 8, width)
                 window = pltpu.roll(window, turn_back, 1)
                 moved = jnp.where(kept, window[:9], window[1:])
@@ -119,8 +135,8 @@
             out[0, capacity:, :] = jnp.concatenate([high, low], axis=1).astype(BF16)
 
 
-def pack(slots, send_counts, embeddings, local, capacity, tags=None):
-    per_dev, width = embeddings.shape
+def pack(slots, send_counts, embeddings, local, capacity, tags=None, limit=None):
+    _, width = embeddings.shape
     tall = capacity + TAIL
     longest = max(len(c) for _, _, c in slots)
 
@@ -128,29 +144,30 @@
         return pl.BlockSpec((1, tall, width), lambda q: (jnp.minimum(q, length - 1), 0, 0))
 
     many = sum(len(c) for _, _, c in slots)
+    held = len(slots) * longest * (capacity + 96) * width * 2 + len(slots) * 2 * tall * width * 2
     return pl.pallas_call(
         functools.partial(pack_body, slots, capacity, tags is not None),
         grid=(longest,),
         out_shape=[jax.ShapeDtypeStruct((len(c), tall, width), BF16) for _, _, c in slots],
         in_specs=[
             pl.BlockSpec(memory_space=pltpu.SMEM),
-            pl.BlockSpec(memory_space=pl.ANY),
+            pl.BlockSpec(memory_space=pltpu.HBM),
             pl.BlockSpec(local.shape, lambda q: (0, 0)),
         ]
         + ([] if tags is None else [pl.BlockSpec(tags.shape, lambda q: (0, 0))]),
         out_specs=[spec(len(c)) for _, _, c in slots],
         scratch_shapes=[
-            pltpu.VMEM((per_dev + capacity + 16, width), BF16),
+            pltpu.VMEM((len(slots), longest, capacity + 96, width), BF16),
             pltpu.VMEM((local.shape[0] + 16, LANES), jnp.int32),
             pltpu.SMEM((send_counts.shape[1],), jnp.int32),
-            pltpu.SemaphoreType.DMA,
+            pltpu.SemaphoreType.DMA((len(slots), longest)),
         ],
+        compiler_params=pltpu.CompilerParams(vmem_limit_bytes=limit or held + 6 * MIB),
         cost_estimate=pl.CostEstimate(
             flops=0,
-            bytes_accessed=per_dev * width * 2 + many * tall * width * 2,
+            bytes_accessed=2 * many * tall * width * 2,
             transcendentals=0,
         ),
-        compiler_params=pltpu.CompilerParams(vmem_limit_bytes=60 * MIB),
         name="pack_rows",
     )(send_counts, embeddings, local, *([] if tags is None else [tags]))
 
@@ -273,12 +290,14 @@
     )(*operands)
 
 
-def update_body(acc, counts, old, *refs):
+def update_body(slots, acc, counts, old, owner_hot, rank_hot, *refs):
     steps = SIDE - 1
-    got, tails, new, column = refs[:steps], refs[steps : 2 * steps], refs[-2], refs[-1]
+    got, tails, refs = refs[:steps], refs[steps : 2 * steps], refs[2 * steps :]
+    new, whole, outs, (column, placement) = refs[0], refs[1], refs[2:-2], refs[-2:]
     digits = counts.shape[1]
     part = pl.program_id(0)
-    group = old.shape[0] // LANES
+    size = old.shape[0]
+    group = size // LANES
 
     @pl.when(part == 0)
     def _():
@@ -303,29 +322,44 @@
                 for g in got:
                     total = total + g[at, :].astype(F32)
                 count = column[:, p * group + h : p * group + h + 1]
-                new[at, :] = (total / (count + 1.0)).astype(BF16)
-
-
-def update(acc, counts, old_fine, got):
+                fresh = (total / (count + 1.0)).astype(BF16)
+                new[at, :] = fresh
+                whole[p * size + h * LANES : p * size + (h + 1) * LANES, :] = fresh
+
+    @pl.when(part == pl.num_programs(0) - 1)
+    def _():
+        place_body(slots, owner_hot, rank_hot, whole, *outs, placement)
+
+
+def update(acc, counts, old_fine, got, slots, owner_hot, rank_hot):
     fine_dev, width = old_fine.shape
+    capacity = rank_hot.shape[0]
     digits = fine_dev // LANES
     size = fine_dev // 4
-    return pl.pallas_call(
-        update_body,
+    fixed = lambda a: pl.BlockSpec(a.shape, lambda m: (0, 0))
+    return pl.pallas_call(
+        functools.partial(update_body, slots),
         grid=(fine_dev // size,),
-        out_shape=jax.ShapeDtypeStruct((fine_dev, width), BF16),
+        out_shape=[jax.ShapeDtypeStruct((fine_dev, width), BF16)] * 2
+        + [jax.ShapeDtypeStruct((SIDE, capacity, width), BF16)] * len(slots),
         in_specs=[
             pl.BlockSpec((1, size, width), lambda m: (0, m, 0)),
             pl.BlockSpec((1, digits, LANES), lambda m: (0, 0, 0)),
             pl.BlockSpec((size, width), lambda m: (m, 0)),
+            fixed(owner_hot),
+            fixed(rank_hot),
         ]
         + [pl.BlockSpec((size, width), lambda m: (m, 0))] * len(got)
         + [pl.BlockSpec((16, width), lambda m: (fine_dev // 16, 0))] * len(got),
-        out_specs=pl.BlockSpec((size, width), lambda m: (m, 0)),
-        scratch_shapes=[pltpu.VMEM((LANES, digits), F32)],
+        out_specs=[pl.BlockSpec((size, width), lambda m: (m, 0)), fixed(old_fine)]
+        + [pl.BlockSpec((SIDE, capacity, width), lambda m: (0, 0, 0))] * len(slots),
+        scratch_shapes=[
+            pltpu.VMEM((LANES, digits), F32),
+            pltpu.VMEM((SIDE * capacity, fine_dev), BF16),
+        ],
         compiler_params=pltpu.CompilerParams(vmem_limit_bytes=24 * MIB),
         name="new_fine",
-    )(acc, counts, old_fine, *got, *got)
+    )(acc, counts, old_fine, owner_hot, rank_hot, *got, *got)
 
 
 def plan_body(coarse_dev, ids, owner_hot, rank_hot, labels):
@@ -547,10 +581,12 @@
     sent, own = tuple(steps), (0,)
     order = (2, 1, 3)
 
-    keep = pack([(True, s, sent) for s in order], *rows)
     kept = []
-    for s, a in zip(order, keep):
-        kept.append(along(a, s, True))
+    for part, group in (("far", order[:1]), ("near", order[1:])):
+        limit = 60 * MIB if part == "far" else None
+        keep = pack([(True, s, sent) for s in group], *rows, limit=limit)
+        for s, a in zip(group, keep):
+            kept.append(along(a, s, True))
     owner_hot, rank_hot, tags = plan(
         coarse_ids.reshape(1, -1), peers, capacity_two, coarse_dev
     )
@@ -578,14 +614,20 @@
     hot, digits = tag_hot(
         [more[4], swapped] + kept_own + given_own, capacity, capacity_two, coarse_dev
     )
-    new_fine = update(acc, counts, old_fine, [got[c] for c in steps])
-
-    keep = place([(True, s) for s in order], owner_hot, rank_hot, new_fine)
+    new_fine, near_fine, *keep = update(
+        acc,
+        counts,
+        old_fine,
+        [got[c] for c in steps],
+        [(True, s) for s in order],
+        owner_hot,
+        rank_hot,
+    )
     arrived = []
     for s, a in zip(order, keep):
         arrived.append(along(a, s, True))
     give = place(
-        [(False, s) for s in order] + [(False, 0), (True, 0)], owner_hot, rank_hot, new_fine
+        [(False, s) for s in order] + [(False, 0), (True, 0)], owner_hot, rank_hot, near_fine
     )
     for s, a in zip(order, give):
         arrived.append(along(a, s, False))

time: 158 us -> 165 us (1.044)
  local copies, waits for them, and re-layouts: 2.57 us -> 13.4 us
  waiting for transfers between devices: 65.1 us -> 58.3 us
  starting transfers between devices: 40.9 us -> 45.8 us
  Pallas kernels: 47.8 us -> 45.1 us
    unnamed x26 -> x54, local copies, waits for them, and re-layouts: 2.57 us -> 13.4 us
    ppermute x20, waiting for transfers between devices: 54 us -> 46.9 us  [along(): return lax.ppermute(slots, 'rows', line_pairs(step, same_class))]
    ppermute x20, starting transfers between devices: 26.2 us -> 31.2 us  [along(): return lax.ppermute(slots, 'rows', line_pairs(step, same_class))]
    pallas_call x2 -> x3, Pallas kernels: 13.4 us -> 10.8 us  [pack(): pl.pallas_call(functools.partial(pack_body, slots, capacity, tags is not...]
    pallas_call x2 -> x1, Pallas kernels: 4.69 us -> 2.87 us  [place(): pl.pallas_call(functools.partial(place_body, slots), out_shape=[jax.Shape...]
    pallas_call x1, Pallas kernels: 2.2 us -> 3.9 us  [update(): pl.pallas_call(functools.partial(update_body, slots), grid=(fine_dev // s...]
  transfers between devices with their start and end apart: 29 -> 29, of which waited for: 13 -> 16; matrix products, arithmetic and copies ran while one was open for 0% -> 0% of each run, Pallas kernels for 21% -> 19%
where the time goes in v3:
time: 165 us; the launch traced here: 164 us
  waiting for transfers between devices  58.3 us (35%)
  starting transfers between devices  45.8 us (28%)
  Pallas kernels  45.1 us (27%)
  local copies, waits for them, and re-layouts  13.4 us (8%)
    ppermute x20, waiting for transfers between devices, along(): return lax.ppermute(slots, 'rows', line_pairs(step, same_class))  46.9 us
    ppermute x20, starting transfers between devices, along(): return lax.ppermute(slots, 'rows', line_pairs(step, same_class))  31.2 us
    pallas_call x6, Pallas kernels, line_sums(): pl.pallas_call(functools.partial(sums_body, sources, capacity, blocks, ha...  24.1 us
    unnamed x54, local copies, waits for them, and re-layouts  13.4 us
    pallas_call x3, Pallas kernels, pack(): pl.pallas_call(functools.partial(pack_body, slots, capacity, tags is not...  10.8 us
    ppermute x3, waiting for transfers between devices, level_step(): pieces.append(lax.ppermute(means, 'grp', back))  7.43 us
    ppermute x3, starting transfers between devices, level_step(): pieces.append(lax.ppermute(means, 'grp', back))  5.37 us
    ppermute x3, starting transfers between devices, level_step(): got[cross] = lax.ppermute(part, 'rows', cross_pairs(cross))  5.01 us
  transfers between devices with their start and end apart: 29, of which 16 were waited for; matrix products, arithmetic and copies ran while one was open for 0% of the time, Pallas kernels for 19%

profile of v3, /device:TPU:0, one launch (start us, length us, event | category | flops | bytes accessed | tf_op | source)
XLA Modules:
  0.0 163.6 jit_solution(12721400690863282396)
XLA Ops:
  5.5 5.2 %pack_rows.3 = (bf16[3,520,256]{2,1,0:T(8,128)(2,1)S(1)}, bf16[3,520,256]{2,1,0:T(8,128)(2,1)S(1)}, bf16[3,520,256]{2,1,0:T(8,128)(2,1)S(1)}, bf16[4,520,256]{2,...) custom-call(s32[1,32]{1,0:T(1,128)S(1)} %copy-done.7, ...), custom_call_target="tpu_custom_call" | custom-call | bytes 12247040 | tf_op jit(solution)/shard_map/pack_rows/pallas_call | solution.py:148
  17.7 3.7 %pack_rows.5 = bf16[3,520,256]{2,1,0:T(8,128)(2,1)} custom-call(s32[1,32]{1,0:T(1,128)} %counts.5, bf16[8192,256]{1,0:T(8,128)(2,1)} %emb.5, s32[64,128]{1,0:T(8,128)} %bitcast.3), custom_call_target="tpu_custom_call" | custom-call | bytes 1597440 | tf_op jit(solution)/shard_map/pack_rows/pallas_call | solution.py:148
  21.4 3.2 %collective-permute-start.12 = (bf16[3,520,256]{2,1,0:T(8,128)(2,1)}, bf16[3,520,256]{2,1,0:T(8,128)(2,1)S(1)}, u32[]{:S(2)}, u32[]{:S(2)}) collective-permute-start(bf16[3,520,256]{2,1,0:T(8,128)(2,1)} %pack_rows.5), channel_id=1, source_target_pairs={{0,64},{4,20},{8,72},{12,28},{16,80},{20,4},{24,88},{28,12},{32,96... | collective-permute-start | bytes 2396168 | tf_op jit(solution)/shard_map/ppermute | solution.py:578
  29.4 2.6 %collective-permute-start.11 = (bf16[3,520,256]{2,1,0:T(8,128)(2,1)S(1)}, bf16[3,520,256]{2,1,0:T(8,128)(2,1)S(1)}, u32[]{:S(2)}, u32[]{:S(2)}) collective-permute-start(bf16[3,520,256]{2,1,0:T(8,128)(2,1)S(1)} %get-tuple-element.57), channel_id=1, source_target_pairs={{0,96},{4,28},{8,104},{12,4},{16,112},{20,12},{24,120},{28,20},{32... | collective-permute-start | bytes 2396168 | tf_op jit(solution)/shard_map/ppermute | solution.py:578
  32.0 4.9 %collective-permute-done.12.refs_2_ = bf16[3,520,256]{2,1,0:T(8,128)(2,1)S(1)} collective-permute-done((bf16[3,520,256]{2,1,0:T(8,128)(2,1)}, bf16[3,520,256]{2,1,0:T(8,128)(2,1)S(1)}, u32[]{:S(2)}, u32[]{:S(2)}) %collective-permute-start.12) | collective-permute-done | bytes 798752 | tf_op jit(solution)/shard_map/ppermute | solution.py:578
  36.9 3.9 %collective-permute-start.9 = (bf16[3,520,256]{2,1,0:T(8,128)(2,1)S(1)}, bf16[3,520,256]{2,1,0:T(8,128)(2,1)S(1)}, u32[]{:S(2)}, u32[]{:S(2)}) collective-permute-start(bf16[3,520,256]{2,1,0:T(8,128)(2,1)S(1)} %copy-done.10), channel_id=1, source_target_pairs={{0,28},{4,96},{8,4},{12,104},{16,12},{20,112},{24,20},{28,120},{32... | collective-permute-start | bytes 2396168 | tf_op jit(solution)/shard_map/ppermute | solution.py:578
  40.8 6.8 %line_sums.7 = (f32[3,2048,256]{2,1,0:T(8,128)S(1)}, f32[3,16,128]{2,1,0:T(8,128)S(1)}) custom-call(bf16[4,520,256]{2,1,0:T(8,128)(2,1)S(1)} %get-tuple-element.41.refs_0_, bf16[4,520,256]{2,1,0:T(8,128)(2,1)S(1)} %collective-permute-done.refs_1_, bf16[3,520,256]{2,1,0:T(8,128)(2,1)S(1)} %collective-permute-done.12.refs_2_), custom_call_target="tpu_custom_call" | custom-call | flops 4831838208 | bytes 14979072 | tf_op jit(solution)/shard_map/line_sums/pallas_call | solution.py:271
  47.6 9.8 %collective-permute-done.10.refs_0_ = bf16[3,520,256]{2,1,0:T(8,128)(2,1)S(1)} collective-permute-done((bf16[3,520,256]{2,1,0:T(8,128)(2,1)S(1)}, bf16[3,520,256]{2,1,0:T(8,128)(2,1)S(1)}, u32[]{:S(2)}, u32[]{:S(2)}) %collective-permute-start.10) | collective-permute-done | bytes 798752 | tf_op jit(solution)/shard_map/ppermute | solution.py:578
  57.5 5.1 %collective-permute-start.1 = (bf16[1,520,256]{2,1,0:T(8,128)(2,1)S(1)}, bf16[1,520,256]{2,1,0:T(8,128)(2,1)S(1)}, u32[]{:S(2)}, u32[]{:S(2)}) collective-permute-start(bf16[1,520,256]{2,1,0:T(8,128)(2,1)S(1)} %copy-done.26), channel_id=1, source_target_pairs={{0,64},{4,20},{8,72},{12,28},{16,80},{20,4},{24,88},{28,12},{32,96... | collective-permute-start | bytes 798728 | tf_op jit(solution)/shard_map/ppermute | solution.py:578
  62.6 5.1 %line_sums.8 = (f32[3,2048,256]{2,1,0:T(8,128)S(1)}, f32[3,16,128]{2,1,0:T(8,128)S(1)}) custom-call(bf16[3,520,256]{2,1,0:T(8,128)(2,1)S(1)} %collective-permute-done.10.refs_0_, bf16[3,520,256]{2,1,0:T(8,128)(2,1)S(1)} %collective-permute-done.11.refs_1_, f32[3,2048,256]{2,1,0:T(8,128)S(1)} %get-tuple-element.58.refs_2_, ...), custom_call_target="tpu_custom_call" | custom-call | flops 3221225472 | bytes 14180352 | tf_op jit(solution)/shard_map/line_sums/pallas_call | solution.py:271
  70.0 3.1 %collective-permute-start.15 = (bf16[2064,256]{1,0:T(8,128)(2,1)S(1)}, bf16[2064,256]{1,0:T(8,128)(2,1)S(1)}, u32[]{:S(2)}, u32[]{:S(2)}) collective-permute-start(bf16[2064,256]{1,0:T(8,128)(2,1)S(1)} %line_sums.11), channel_id=1, source_target_pairs={{0,24},{4,100},{8,0},{12,108},{16,8},{20,116},{24,16},{28,124},{32... | collective-permute-start | bytes 3170312 | tf_op jit(solution)/shard_map/ppermute | solution.py:612
  79.7 3.2 %collective-permute-start.3 = (bf16[1,520,256]{2,1,0:T(8,128)(2,1)S(1)}, bf16[1,520,256]{2,1,0:T(8,128)(2,1)S(1)}, u32[]{:S(2)}, u32[]{:S(2)}) collective-permute-start(bf16[1,520,256]{2,1,0:T(8,128)(2,1)S(1)} %copy-done.22), channel_id=1, source_target_pairs={{0,96},{4,28},{8,104},{12,4},{16,112},{20,12},{24,120},{28,20},{32... | collective-permute-start | bytes 798728 | tf_op jit(solution)/shard_map/ppermute | solution.py:578
  82.9 17.8 %collective-permute-done.3.refs_4_ = bf16[1,520,256]{2,1,0:T(8,128)(2,1)S(1)} collective-permute-done((bf16[1,520,256]{2,1,0:T(8,128)(2,1)S(1)}, bf16[1,520,256]{2,1,0:T(8,128)(2,1)S(1)}, u32[]{:S(2)}, u32[]{:S(2)}) %collective-permute-start.3) | collective-permute-done | bytes 266272 | tf_op jit(solution)/shard_map/ppermute | solution.py:578
  100.7 3.5 %collective-permute-done.4.refs_5_ = bf16[1,520,256]{2,1,0:T(8,128)(2,1)S(1)} collective-permute-done((bf16[1,520,256]{2,1,0:T(8,128)(2,1)S(1)}, bf16[1,520,256]{2,1,0:T(8,128)(2,1)S(1)}, u32[]{:S(2)}, u32[]{:S(2)}) %collective-permute-start.4) | collective-permute-done | bytes 266272 | tf_op jit(solution)/shard_map/ppermute | solution.py:578
  104.5 3.3 %collective-permute-done.5.refs_6_ = bf16[1,520,256]{2,1,0:T(8,128)(2,1)S(1)} collective-permute-done((bf16[1,520,256]{2,1,0:T(8,128)(2,1)S(1)}, bf16[1,520,256]{2,1,0:T(8,128)(2,1)S(1)}, u32[]{:S(2)}, u32[]{:S(2)}) %collective-permute-start.5) | collective-permute-done | bytes 266272 | tf_op jit(solution)/shard_map/ppermute | solution.py:578
  110.0 5.3 %line_sums.6 = (f32[1,2048,256]{2,1,0:T(8,128)S(1)}, f32[1,16,128]{2,1,0:T(8,128)S(1)}) custom-call(bf16[4,520,256]{2,1,0:T(8,128)(2,1)S(1)} %get-tuple-element.41.refs_0_, bf16[4,520,256]{2,1,0:T(8,128)(2,1)S(1)} %collective-permute-done.refs_1_, bf16[1,520,256]{2,1,0:T(8,128)(2,1)S(1)} %collective-permute-done.1.refs_2_, ...), custom_call_target="tpu_custom_call" | custom-call | flops 4294967296 | bytes 6324224 | tf_op jit(solution)/shard_map/line_sums/pallas_call | solution.py:271
  115.3 3.9 %new_fine.1 = (bf16[2048,256]{1,0:T(8,128)(2,1)}, bf16[2048,256]{1,0:T(8,128)(2,1)S(1)}, bf16[4,128,256]{2,1,0:T(8,128)(2,1)S(1)}, bf16[4,128,256]{2,1,0:T(8,128)(2,1)S(1)}, bf16[4,128,256]{2,1,0:T(8,128)(2,1)S(1)}) custom-call(f32[1,2048,256]{2,1,0:T(8,128)S(1)} %get-tuple-element.49.acc, f32[1,16,128]{2,1,0:T(8,128)S(1)} %get-tuple-element.50.counts, ...), custom_call_target="tpu_custom_call" | custom-call | tf_op jit(solution)/shard_map/new_fine/pallas_call | solution.py:340
  119.2 2.9 %place_clusters.1 = (bf16[4,128,256]{2,1,0:T(8,128)(2,1)S(1)}, bf16[4,128,256]{2,1,0:T(8,128)(2,1)S(1)}, bf16[4,128,256]{2,1,0:T(8,128)(2,1)S(1)}, bf16[4,128,25...) custom-call(f32[32,2048]{1,0:T(8,128)S(1)} %get-tuple-element.51.owner_hot, bf16[128,2048]{1,0:T(8,128)(2,1)S(1)} %get-tuple-element.52.rank_hot, ...), custom_call_target="tpu_custom_call" | custom-call | flops 2684354560 | bytes 1048576 | tf_op jit(solution)/shard_map/place_clusters/pallas_call | solution.py:422
  125.3 2.6 %collective-permute-start.22 = (bf16[4,128,256]{2,1,0:T(8,128)(2,1)S(1)}, bf16[4,128,256]{2,1,0:T(8,128)(2,1)S(1)}, u32[]{:S(2)}, u32[]{:S(2)}) collective-permute-start(bf16[4,128,256]{2,1,0:T(8,128)(2,1)S(1)} %get-tuple-element.71), channel_id=1, source_target_pairs={{0,28},{4,96},{8,4},{12,104},{16,12},{20,112},{24,20},{28,120},{32... | collective-permute-start | bytes 786440 | tf_op jit(solution)/shard_map/ppermute | solution.py:578
  127.9 3.2 %collective-permute-start.17 = (bf16[4,128,256]{2,1,0:T(8,128)(2,1)S(1)}, bf16[4,128,256]{2,1,0:T(8,128)(2,1)S(1)}, u32[]{:S(2)}, u32[]{:S(2)}) collective-permute-start(bf16[4,128,256]{2,1,0:T(8,128)(2,1)S(1)} %get-tuple-element.66), channel_id=1, source_target_pairs={{0,64},{4,20},{8,72},{12,28},{16,80},{20,4},{24,88},{28,12},{32,96... | collective-permute-start | bytes 786440 | tf_op jit(solution)/shard_map/ppermute | solution.py:578
  131.6 3.2 %collective-permute-start.19 = (bf16[4,128,256]{2,1,0:T(8,128)(2,1)S(1)}, bf16[4,128,256]{2,1,0:T(8,128)(2,1)S(1)}, u32[]{:S(2)}, u32[]{:S(2)}) collective-permute-start(bf16[4,128,256]{2,1,0:T(8,128)(2,1)S(1)} %get-tuple-element.68), channel_id=1, source_target_pairs={{0,96},{4,28},{8,104},{12,4},{16,112},{20,12},{24,120},{28,20},{32... | collective-permute-start | bytes 786440 | tf_op jit(solution)/shard_map/ppermute | solution.py:578
  142.9 2.6 %collective-permute-start.25 = (bf16[272,256]{1,0:T(8,128)(2,1)S(1)}, bf16[272,256]{1,0:T(8,128)(2,1)S(1)}, u32[]{:S(2)}, u32[]{:S(2)}) collective-permute-start(bf16[272,256]{1,0:T(8,128)(2,1)S(1)} %get-tuple-element.77), channel_id=1, source_target_pairs={{0,24},{4,100},{8,0},{12,108},{16,8},{20,116},{24,16},{28,124},{32... | collective-permute-start | bytes 417800 | tf_op jit(solution)/shard_map/ppermute | solution.py:638
  149.7 4.1 %collective-permute-start.26 = (bf16[256,256]{1,0:T(8,128)(2,1)S(1)}, bf16[256,256]{1,0:T(8,128)(2,1)S(1)}, u32[]{:S(2)}, u32[]{:S(2)}) collective-permute-start(bf16[256,256]{1,0:T(8,128)(2,1)S(1)} %coarse_means.1.refs_0_), channel_id=1, source_target_pairs={{1,0},{2,1},{3,2},{0,3},{5,4},{6,5},{7,6},{4,7},{9,8},{10,9},{11,1... | collective-permute-start | bytes 393224 | tf_op jit(solution)/shard_map/ppermute | solution.py:643
  155.0 4.0 %collective-permute-done.26.refs_1_ = bf16[256,256]{1,0:T(8,128)(2,1)S(1)} collective-permute-done((bf16[256,256]{1,0:T(8,128)(2,1)S(1)}, bf16[256,256]{1,0:T(8,128)(2,1)S(1)}, u32[]{:S(2)}, u32[]{:S(2)}) %collective-permute-start.26) | collective-permute-done | bytes 131104 | tf_op jit(solution)/shard_map/ppermute | solution.py:643
  (104 shorter events, 49.6 us)
Async XLA Ops:
  17.7 19.2 %collective-permute-start = (bf16[4,520,256]{2,1,0:T(8,128)(2,1)S(1)}, bf16[4,520,256]{2,1,0:T(8,128)(2,1)S(1)}, u32[]{:S(2)}, u32[]{:S(2)}) collective-permute-start(bf16[4,520,256]{2,1,0:T(8,128)(2,1)S(1)} %get-tuple-element.42), channel_id=1, source_target_pairs={{0,4},{4,0},{8,12},{12,8},{16,20},{20,16},{24,28},{28,24},{32,36},... | collective-permute-start | bytes 3194888 | tf_op jit(solution)/shard_map/ppermute | solution.py:578
  21.4 15.5 %collective-permute-start.12 = (bf16[3,520,256]{2,1,0:T(8,128)(2,1)}, bf16[3,520,256]{2,1,0:T(8,128)(2,1)S(1)}, u32[]{:S(2)}, u32[]{:S(2)}) collective-permute-start(bf16[3,520,256]{2,1,0:T(8,128)(2,1)} %pack_rows.5), channel_id=1, source_target_pairs={{0,64},{4,20},{8,72},{12,28},{16,80},{20,4},{24,88},{28,12},{32,96... | collective-permute-start | bytes 2396168 | tf_op jit(solution)/shard_map/ppermute | solution.py:578
  28.7 28.8 %collective-permute-start.10 = (bf16[3,520,256]{2,1,0:T(8,128)(2,1)S(1)}, bf16[3,520,256]{2,1,0:T(8,128)(2,1)S(1)}, u32[]{:S(2)}, u32[]{:S(2)}) collective-permute-start(bf16[3,520,256]{2,1,0:T(8,128)(2,1)S(1)} %get-tuple-element.56), channel_id=1, source_target_pairs={{0,32},{4,12},{8,40},{12,20},{16,48},{20,28},{24,56},{28,4},{32,64... | collective-permute-start | bytes 2396168 | tf_op jit(solution)/shard_map/ppermute | solution.py:578
  29.4 33.2 %collective-permute-start.11 = (bf16[3,520,256]{2,1,0:T(8,128)(2,1)S(1)}, bf16[3,520,256]{2,1,0:T(8,128)(2,1)S(1)}, u32[]{:S(2)}, u32[]{:S(2)}) collective-permute-start(bf16[3,520,256]{2,1,0:T(8,128)(2,1)S(1)} %get-tuple-element.57), channel_id=1, source_target_pairs={{0,96},{4,28},{8,104},{12,4},{16,112},{20,12},{24,120},{28,20},{32... | collective-permute-start | bytes 2396168 | tf_op jit(solution)/shard_map/ppermute | solution.py:578
  32.0 35.6 %collective-permute-start.7 = (bf16[3,520,256]{2,1,0:T(8,128)(2,1)S(1)}, bf16[3,520,256]{2,1,0:T(8,128)(2,1)S(1)}, u32[]{:S(2)}, u32[]{:S(2)}) collective-permute-start(bf16[3,520,256]{2,1,0:T(8,128)(2,1)S(1)} %copy-done.14), channel_id=1, source_target_pairs={{0,20},{4,64},{8,28},{12,72},{16,4},{20,80},{24,12},{28,88},{32,52... | collective-permute-start | bytes 2396168 | tf_op jit(solution)/shard_map/ppermute | solution.py:578
  36.9 30.8 %collective-permute-start.8 = (bf16[3,520,256]{2,1,0:T(8,128)(2,1)S(1)}, bf16[3,520,256]{2,1,0:T(8,128)(2,1)S(1)}, u32[]{:S(2)}, u32[]{:S(2)}) collective-permute-start(bf16[3,520,256]{2,1,0:T(8,128)(2,1)S(1)} %copy-done.12), channel_id=1, source_target_pairs={{0,12},{4,32},{8,20},{12,40},{16,28},{20,48},{24,4},{28,56},{32,44... | collective-permute-start | bytes 2396168 | tf_op jit(solution)/shard_map/ppermute | solution.py:578
  36.9 30.8 %collective-permute-start.9 = (bf16[3,520,256]{2,1,0:T(8,128)(2,1)S(1)}, bf16[3,520,256]{2,1,0:T(8,128)(2,1)S(1)}, u32[]{:S(2)}, u32[]{:S(2)}) collective-permute-start(bf16[3,520,256]{2,1,0:T(8,128)(2,1)S(1)} %copy-done.10), channel_id=1, source_target_pairs={{0,28},{4,96},{8,4},{12,104},{16,12},{20,112},{24,20},{28,120},{32... | collective-permute-start | bytes 2396168 | tf_op jit(solution)/shard_map/ppermute | solution.py:578
  57.5 22.2 %collective-permute-start.1 = (bf16[1,520,256]{2,1,0:T(8,128)(2,1)S(1)}, bf16[1,520,256]{2,1,0:T(8,128)(2,1)S(1)}, u32[]{:S(2)}, u32[]{:S(2)}) collective-permute-start(bf16[1,520,256]{2,1,0:T(8,128)(2,1)S(1)} %copy-done.26), channel_id=1, source_target_pairs={{0,64},{4,20},{8,72},{12,28},{16,80},{20,4},{24,88},{28,12},{32,96... | collective-permute-start | bytes 798728 | tf_op jit(solution)/shard_map/ppermute | solution.py:578
  62.6 20.3 %collective-permute-start.2 = (bf16[1,520,256]{2,1,0:T(8,128)(2,1)S(1)}, bf16[1,520,256]{2,1,0:T(8,128)(2,1)S(1)}, u32[]{:S(2)}, u32[]{:S(2)}) collective-permute-start(bf16[1,520,256]{2,1,0:T(8,128)(2,1)S(1)} %copy-done.24), channel_id=1, source_target_pairs={{0,32},{4,12},{8,40},{12,20},{16,48},{20,28},{24,56},{28,4},{32,64... | collective-permute-start | bytes 798728 | tf_op jit(solution)/shard_map/ppermute | solution.py:578
  70.0 45.3 %collective-permute-start.15 = (bf16[2064,256]{1,0:T(8,128)(2,1)S(1)}, bf16[2064,256]{1,0:T(8,128)(2,1)S(1)}, u32[]{:S(2)}, u32[]{:S(2)}) collective-permute-start(bf16[2064,256]{1,0:T(8,128)(2,1)S(1)} %line_sums.11), channel_id=1, source_target_pairs={{0,24},{4,100},{8,0},{12,108},{16,8},{20,116},{24,16},{28,124},{32... | collective-permute-start | bytes 3170312 | tf_op jit(solution)/shard_map/ppermute | solution.py:612
  75.4 39.8 %collective-permute-start.14 = (bf16[2064,256]{1,0:T(8,128)(2,1)S(1)}, bf16[2064,256]{1,0:T(8,128)(2,1)S(1)}, u32[]{:S(2)}, u32[]{:S(2)}) collective-permute-start(bf16[2064,256]{1,0:T(8,128)(2,1)S(1)} %line_sums.10), channel_id=1, source_target_pairs={{0,16},{4,68},{8,24},{12,76},{16,0},{20,84},{24,8},{28,92},{32,48}... | collective-permute-start | bytes 3170312 | tf_op jit(solution)/shard_map/ppermute | solution.py:612
  78.6 36.7 %collective-permute-start.13 = (bf16[2064,256]{1,0:T(8,128)(2,1)S(1)}, bf16[2064,256]{1,0:T(8,128)(2,1)S(1)}, u32[]{:S(2)}, u32[]{:S(2)}) collective-permute-start(bf16[2064,256]{1,0:T(8,128)(2,1)S(1)} %line_sums.9), channel_id=1, source_target_pairs={{0,8},{4,36},{8,16},{12,44},{16,24},{20,52},{24,0},{28,60},{32,40}... | collective-permute-start | bytes 3170312 | tf_op jit(solution)/shard_map/ppermute | solution.py:612
  79.7 21.0 %collective-permute-start.3 = (bf16[1,520,256]{2,1,0:T(8,128)(2,1)S(1)}, bf16[1,520,256]{2,1,0:T(8,128)(2,1)S(1)}, u32[]{:S(2)}, u32[]{:S(2)}) collective-permute-start(bf16[1,520,256]{2,1,0:T(8,128)(2,1)S(1)} %copy-done.22), channel_id=1, source_target_pairs={{0,96},{4,28},{8,104},{12,4},{16,112},{20,12},{24,120},{28,20},{32... | collective-permute-start | bytes 798728 | tf_op jit(solution)/shard_map/ppermute | solution.py:578
  82.9 21.3 %collective-permute-start.4 = (bf16[1,520,256]{2,1,0:T(8,128)(2,1)S(1)}, bf16[1,520,256]{2,1,0:T(8,128)(2,1)S(1)}, u32[]{:S(2)}, u32[]{:S(2)}) collective-permute-start(bf16[1,520,256]{2,1,0:T(8,128)(2,1)S(1)} %copy-done.20), channel_id=1, source_target_pairs={{0,20},{4,64},{8,28},{12,72},{16,4},{20,80},{24,12},{28,88},{32,52... | collective-permute-start | bytes 798728 | tf_op jit(solution)/shard_map/ppermute | solution.py:578
  122.1 9.0 %collective-permute-start.16 = (bf16[4,128,256]{2,1,0:T(8,128)(2,1)S(1)}, bf16[4,128,256]{2,1,0:T(8,128)(2,1)S(1)}, u32[]{:S(2)}, u32[]{:S(2)}) collective-permute-start(bf16[4,128,256]{2,1,0:T(8,128)(2,1)S(1)} %get-tuple-element.65), channel_id=1, source_target_pairs={{0,4},{4,0},{8,12},{12,8},{16,20},{20,16},{24,28},{28,24},{32,36},... | collective-permute-start | bytes 786440 | tf_op jit(solution)/shard_map/ppermute | solution.py:578
  124.2 7.4 %collective-permute-start.20 = (bf16[4,128,256]{2,1,0:T(8,128)(2,1)S(1)}, bf16[4,128,256]{2,1,0:T(8,128)(2,1)S(1)}, u32[]{:S(2)}, u32[]{:S(2)}) collective-permute-start(bf16[4,128,256]{2,1,0:T(8,128)(2,1)S(1)} %get-tuple-element.69), channel_id=1, source_target_pairs={{0,20},{4,64},{8,28},{12,72},{16,4},{20,80},{24,12},{28,88},{32,52... | collective-permute-start | bytes 786440 | tf_op jit(solution)/shard_map/ppermute | solution.py:578
  124.8 11.0 %collective-permute-start.21 = (bf16[4,128,256]{2,1,0:T(8,128)(2,1)S(1)}, bf16[4,128,256]{2,1,0:T(8,128)(2,1)S(1)}, u32[]{:S(2)}, u32[]{:S(2)}) collective-permute-start(bf16[4,128,256]{2,1,0:T(8,128)(2,1)S(1)} %get-tuple-element.70), channel_id=1, source_target_pairs={{0,12},{4,32},{8,20},{12,40},{16,28},{20,48},{24,4},{28,56},{32,44... | collective-permute-start | bytes 786440 | tf_op jit(solution)/shard_map/ppermute | solution.py:578
  125.3 12.4 %collective-permute-start.22 = (bf16[4,128,256]{2,1,0:T(8,128)(2,1)S(1)}, bf16[4,128,256]{2,1,0:T(8,128)(2,1)S(1)}, u32[]{:S(2)}, u32[]{:S(2)}) collective-permute-start(bf16[4,128,256]{2,1,0:T(8,128)(2,1)S(1)} %get-tuple-element.71), channel_id=1, source_target_pairs={{0,28},{4,96},{8,4},{12,104},{16,12},{20,112},{24,20},{28,120},{32... | collective-permute-start | bytes 786440 | tf_op jit(solution)/shard_map/ppermute | solution.py:578
  127.9 9.8 %collective-permute-start.17 = (bf16[4,128,256]{2,1,0:T(8,128)(2,1)S(1)}, bf16[4,128,256]{2,1,0:T(8,128)(2,1)S(1)}, u32[]{:S(2)}, u32[]{:S(2)}) collective-permute-start(bf16[4,128,256]{2,1,0:T(8,128)(2,1)S(1)} %get-tuple-element.66), channel_id=1, source_target_pairs={{0,64},{4,20},{8,72},{12,28},{16,80},{20,4},{24,88},{28,12},{32,96... | collective-permute-start | bytes 786440 | tf_op jit(solution)/shard_map/ppermute | solution.py:578
  131.1 8.9 %collective-permute-start.18 = (bf16[4,128,256]{2,1,0:T(8,128)(2,1)S(1)}, bf16[4,128,256]{2,1,0:T(8,128)(2,1)S(1)}, u32[]{:S(2)}, u32[]{:S(2)}) collective-permute-start(bf16[4,128,256]{2,1,0:T(8,128)(2,1)S(1)} %get-tuple-element.67), channel_id=1, source_target_pairs={{0,32},{4,12},{8,40},{12,20},{16,48},{20,28},{24,56},{28,4},{32,64... | collective-permute-start | bytes 786440 | tf_op jit(solution)/shard_map/ppermute | solution.py:578
  131.6 8.9 %collective-permute-start.19 = (bf16[4,128,256]{2,1,0:T(8,128)(2,1)S(1)}, bf16[4,128,256]{2,1,0:T(8,128)(2,1)S(1)}, u32[]{:S(2)}, u32[]{:S(2)}) collective-permute-start(bf16[4,128,256]{2,1,0:T(8,128)(2,1)S(1)} %get-tuple-element.68), channel_id=1, source_target_pairs={{0,96},{4,28},{8,104},{12,4},{16,112},{20,12},{24,120},{28,20},{32... | collective-permute-start | bytes 786440 | tf_op jit(solution)/shard_map/ppermute | solution.py:578
  149.7 9.4 %collective-permute-start.26 = (bf16[256,256]{1,0:T(8,128)(2,1)S(1)}, bf16[256,256]{1,0:T(8,128)(2,1)S(1)}, u32[]{:S(2)}, u32[]{:S(2)}) collective-permute-start(bf16[256,256]{1,0:T(8,128)(2,1)S(1)} %coarse_means.1.refs_0_), channel_id=1, source_target_pairs={{1,0},{2,1},{3,2},{0,3},{5,4},{6,5},{7,6},{4,7},{9,8},{10,9},{11,1... | collective-permute-start | bytes 393224 | tf_op jit(solution)/shard_map/ppermute | solution.py:643
  153.8 7.6 %collective-permute-start.27 = (bf16[256,256]{1,0:T(8,128)(2,1)S(1)}, bf16[256,256]{1,0:T(8,128)(2,1)S(1)}, u32[]{:S(2)}, u32[]{:S(2)}) collective-permute-start(bf16[256,256]{1,0:T(8,128)(2,1)S(1)} %coarse_means.1.refs_0_), channel_id=1, source_target_pairs={{2,0},{3,1},{0,2},{1,3},{6,4},{7,5},{4,6},{5,7},{10,8},{11,9},{8,1... | collective-permute-start | bytes 393224 | tf_op jit(solution)/shard_map/ppermute | solution.py:643
  153.8 8.7 %collective-permute-start.28 = (bf16[256,256]{1,0:T(8,128)(2,1)S(1)}, bf16[256,256]{1,0:T(8,128)(2,1)S(1)}, u32[]{:S(2)}, u32[]{:S(2)}) collective-permute-start(bf16[256,256]{1,0:T(8,128)(2,1)S(1)} %coarse_means.1.refs_0_), channel_id=1, source_target_pairs={{3,0},{0,1},{1,2},{2,3},{7,4},{4,5},{5,6},{6,7},{11,8},{8,9},{9,10... | collective-permute-start | bytes 393224 | tf_op jit(solution)/shard_map/ppermute | solution.py:643
  (32 other events, 210.2 us)

commit v4 on v3

--- a/solution.py
+++ b/solution.py
@@ -55,7 +55,7 @@
 def pack_body(slots, capacity, tagged, counts, emb, local, *rest):
     tags = rest[0] if tagged else None
     rest = rest[1:] if tagged else rest
-    outs, (windows, labels, starts, done) = rest[: len(slots)], rest[len(slots) :]
+    outs, (windows, labels, starts, done, arrived) = rest[: len(slots)], rest[len(slots) :]
     per_dev, width = emb.shape
     span = capacity + 16
     label_rows = local.shape[0]
@@ -73,6 +73,9 @@
 
     @pl.when(at_step == 0)
     def _():
+        fetch_labels = pltpu.make_async_copy(local, labels.at[:label_rows, :], arrived)
+        fetch_labels.start()
+
         def add(o, total):
             starts[o] = total
             return total + counts[0, o]
@@ -84,11 +87,11 @@
                     kind = core if same_class else 1 - core
                     first = starts[owner_of(kind, step, crosses[cross])]
                     fetch(at, cross, first // 16 * 16).start()
-        labels[:label_rows, :] = local[...]
         labels[label_rows:, :] = jnp.zeros((16, LANES), jnp.int32)
         for at, (_, _, crosses) in enumerate(slots):
             for cross in range(len(crosses)):
                 windows[at, cross, span:, :] = jnp.zeros((80, width), BF16)
+        fetch_labels.wait()
 
     line = iota((TAIL, LANES), 0) * LANES + iota((TAIL, LANES), 1)
     lane = iota((TAIL, LANES), 1)
@@ -152,7 +155,7 @@
         in_specs=[
             pl.BlockSpec(memory_space=pltpu.SMEM),
             pl.BlockSpec(memory_space=pltpu.HBM),
-            pl.BlockSpec(local.shape, lambda q: (0, 0)),
+            pl.BlockSpec(memory_space=pltpu.HBM),
         ]
         + ([] if tags is None else [pl.BlockSpec(tags.shape, lambda q: (0, 0))]),
         out_specs=[spec(len(c)) for _, _, c in slots],
@@ -161,6 +164,7 @@
             pltpu.VMEM((local.shape[0] + 16, LANES), jnp.int32),
             pltpu.SMEM((send_counts.shape[1],), jnp.int32),
             pltpu.SemaphoreType.DMA((len(slots), longest)),
+            pltpu.SemaphoreType.DMA,
         ],
         compiler_params=pltpu.CompilerParams(vmem_limit_bytes=limit or held + 6 * MIB),
         cost_estimate=pl.CostEstimate(
@@ -172,10 +176,11 @@
     )(send_counts, embeddings, local, *([] if tags is None else [tags]))
 
 
-def sums_body(sources, capacity, blocks, had, sent, *refs):
+def sums_body(lowest, capacity, crosses, had_lowest, sent, *refs):
+    sources = len(lowest)
     arrived, refs = refs[:sources], refs[sources:]
     had_acc, had_counts = None, None
-    if had:
+    if had_lowest is not None:
         had_acc, had_counts, refs = refs[0], refs[1], refs[2:]
     if sent:
         out, low_hot, high_hot, onehot, data = refs
@@ -184,18 +189,19 @@
         out, out_counts, low_hot, high_hot, onehot, data = refs
     digits = high_hot.shape[0]
     depth = sources * capacity
-    part = pl.program_id(1)
     size = onehot.shape[0]
-
-    @pl.when(part == 0)
-    def _():
+    group = size // LANES
+    fine_dev = digits * LANES
+
+    def one(i):
         for s in range(sources):
-            tail = arrived[s][0, capacity:, :].astype(F32)
-            data[s * capacity : (s + 1) * capacity, :] = arrived[s][0, :capacity, :]
-            for i in range(capacity // LANES):
-                at = s * capacity + i * LANES
-                high = tail[i : i + 1, :LANES]
-                low = tail[i : i + 1, LANES : 2 * LANES]
+            slot = arrived[s].at[crosses[0] - lowest[s] + i]
+            tail = slot[capacity:, :].astype(F32)
+            data[s * capacity : (s + 1) * capacity, :] = slot[:capacity, :]
+            for part in range(capacity // LANES):
+                at = s * capacity + part * LANES
+                high = tail[part : part + 1, :LANES]
+                low = tail[part : part + 1, LANES : 2 * LANES]
                 low_hot[:, at : at + LANES] = jnp.where(
                     iota((LANES, LANES), 0).astype(F32) == low, 1.0, 0.0
                 ).astype(BF16)
@@ -209,28 +215,32 @@
             preferred_element_type=F32,
         )
         if had_counts is not None:
-            counts = counts + had_counts[0]
+            counts = counts + had_counts[crosses[0] - had_lowest + i]
         if sent:
             tens = jnp.floor(counts / 64.0)
-            out[blocks * size :, :] = jnp.concatenate(
-                [tens, counts - 64.0 * tens], axis=1
-            ).astype(BF16)
+            out[fine_dev:, :] = jnp.concatenate([tens, counts - 64.0 * tens], axis=1).astype(BF16)
         else:
-            out_counts[0] = counts
-
-    group = size // LANES
-    for h in range(group):
-        row = high_hot[pl.ds(pl.multiple_of(part * group, group), group), :][h : h + 1, :]
-        row = jnp.broadcast_to(row, (16, depth)).astype(BF16)
-        for at in range(0, LANES, 16):
-            onehot[h * LANES + at : h * LANES + at + 16, :] = low_hot[at : at + 16, :] * row
-    total = jnp.dot(onehot[...], data[...], preferred_element_type=F32)
-    if had_acc is not None:
-        total = total + had_acc[0]
-    if sent:
-        out[pl.ds(pl.multiple_of(part * size, size), size), :] = total.astype(BF16)
+            out_counts[i] = counts
+        for part in range(digits // group):
+            for h in range(group):
+                at_high = part * group + h
+                row = jnp.broadcast_to(high_hot[at_high : at_high + 1, :], (16, depth)).astype(BF16)
+                for at in range(0, LANES, 16):
+                    top = h * LANES + at
+                    onehot[top : top + 16, :] = low_hot[at : at + 16, :] * row
+            total = jnp.dot(onehot[...], data[...], preferred_element_type=F32)
+            rows = slice(part * size, (part + 1) * size)
+            if had_acc is not None:
+                total = total + had_acc[crosses[0] - had_lowest + i, rows, :]
+            if sent:
+                out[rows, :] = total.astype(BF16)
+            else:
+                out[i, rows, :] = total
+
+    if len(crosses) == 1:
+        one(0)
     else:
-        out[0] = total
+        pl.loop(0, len(crosses))(one)
 
 
 def line_sums(arrived, capacity, fine_dev, crosses, had=None, send=False):
@@ -239,127 +249,78 @@
     sources = len(arrived)
     digits = fine_dev // LANES
     size = fine_dev // 2
-    blocks = fine_dev // size
     many = len(crosses)
-
-    def source(lowest):
-        at = crosses[0] - lowest
-        return pl.BlockSpec((1, tall, width), lambda q, m: (at + q, 0, 0))
-
     operands = [a for a, _ in arrived]
-    in_specs = [source(lowest) for _, lowest in arrived]
+    had_lowest = None
     if had is not None:
-        acc, counts, lowest = had
-        at = crosses[0] - lowest
+        acc, counts, had_lowest = had
         operands += [acc, counts]
-        in_specs += [
-            pl.BlockSpec((1, size, width), lambda q, m: (at + q, m, 0)),
-            pl.BlockSpec((1, digits, LANES), lambda q, m: (at + q, 0, 0)),
-        ]
     if send:
         out_shape = jax.ShapeDtypeStruct((fine_dev + 16, width), BF16)
-        out_specs = pl.BlockSpec((fine_dev + 16, width), lambda q, m: (0, 0))
     else:
         out_shape = (
             jax.ShapeDtypeStruct((many, fine_dev, width), F32),
             jax.ShapeDtypeStruct((many, digits, LANES), F32),
         )
-        out_specs = (
-            pl.BlockSpec((1, size, width), lambda q, m: (q, m, 0)),
-            pl.BlockSpec((1, digits, LANES), lambda q, m: (q, 0, 0)),
-        )
-    return pl.pallas_call(
-        functools.partial(sums_body, sources, capacity, blocks, had is not None, send),
-        grid=(many, blocks),
+    body = functools.partial(
+        sums_body, tuple(low for _, low in arrived), capacity, crosses, had_lowest, send
+    )
+    return pl.pallas_call(
+        body,
         out_shape=out_shape,
-        in_specs=in_specs,
-        out_specs=out_specs,
         scratch_shapes=[
             pltpu.VMEM((LANES, sources * capacity), BF16),
             pltpu.VMEM((digits, sources * capacity), F32),
             pltpu.VMEM((size, sources * capacity), BF16),
             pltpu.VMEM((sources * capacity, width), BF16),
         ],
+        compiler_params=pltpu.CompilerParams(vmem_limit_bytes=(8 + 2 * sources) * MIB),
         cost_estimate=pl.CostEstimate(
             flops=2 * many * sources * capacity * fine_dev * width,
             bytes_accessed=many * (sources * tall * width * 2 + fine_dev * width * 8),
             transcendentals=0,
         ),
-        compiler_params=pltpu.CompilerParams(vmem_limit_bytes=(10 + 2 * sources) * MIB),
         name="line_sums",
     )(*operands)
 
 
 def update_body(slots, acc, counts, old, owner_hot, rank_hot, *refs):
     steps = SIDE - 1
-    got, tails, refs = refs[:steps], refs[steps : 2 * steps], refs[2 * steps :]
-    new, whole, outs, (column, placement) = refs[0], refs[1], refs[2:-2], refs[-2:]
-    digits = counts.shape[1]
-    part = pl.program_id(0)
-    size = old.shape[0]
-    group = size // LANES
-
-    @pl.when(part == 0)
-    def _():
-        count = counts[0]
-        for tail in tails:
-            value = tail[...].astype(F32)
-            count = count + value[:, :LANES] * 64.0 + value[:, LANES : 2 * LANES]
-        tens = jnp.floor(count / 64.0)
-        eye = jnp.where(iota((LANES, LANES), 0) == iota((LANES, LANES), 1), 1.0, 0.0)
-        turn = lambda a: lax.dot_general(
-            eye.astype(BF16), a.astype(BF16), (((1,), (1,)), ((), ())), preferred_element_type=F32
-        )
-        column[...] = turn(tens) * 64.0 + turn(count - 64.0 * tens)
-
-    for p in range(digits // group):
-
-        @pl.when(part == p)
-        def _():
-            for h in range(group):
-                at = slice(h * LANES, (h + 1) * LANES)
-                total = acc[0, at, :] + old[at, :].astype(F32)
-                for g in got:
-                    total = total + g[at, :].astype(F32)
-                count = column[:, p * group + h : p * group + h + 1]
-                fresh = (total / (count + 1.0)).astype(BF16)
-                new[at, :] = fresh
-                whole[p * size + h * LANES : p * size + (h + 1) * LANES, :] = fresh
-
-    @pl.when(part == pl.num_programs(0) - 1)
-    def _():
-        place_body(slots, owner_hot, rank_hot, whole, *outs, placement)
+    got, refs = refs[:steps], refs[steps:]
+    new, whole, outs, placement = refs[0], refs[1], refs[2:-1], refs[-1]
+    fine_dev = old.shape[0]
+    count = counts[0]
+    for g in got:
+        value = g[fine_dev:, :].astype(F32)
+        count = count + value[:, :LANES] * 64.0 + value[:, LANES : 2 * LANES]
+    tens = jnp.floor(count / 64.0)
+    eye = jnp.where(iota((LANES, LANES), 0) == iota((LANES, LANES), 1), 1.0, 0.0)
+    turn = lambda a: lax.dot_general(
+        eye.astype(BF16), a.astype(BF16), (((1,), (1,)), ((), ())), preferred_element_type=F32
+    )
+    column = turn(tens) * 64.0 + turn(count - 64.0 * tens)
+    for h in range(fine_dev // LANES):
+        at = slice(h * LANES, (h + 1) * LANES)
+        total = acc[0, at, :] + old[at, :].astype(F32)
+        for g in got:
+            total = total + g[at, :].astype(F32)
+        fresh = (total / (column[:, h : h + 1] + 1.0)).astype(BF16)
+        new[at, :] = fresh
+        whole[at, :] = fresh
+    place_body(slots, owner_hot, rank_hot, whole, *outs, placement)
 
 
 def update(acc, counts, old_fine, got, slots, owner_hot, rank_hot):
     fine_dev, width = old_fine.shape
     capacity = rank_hot.shape[0]
-    digits = fine_dev // LANES
-    size = fine_dev // 4
-    fixed = lambda a: pl.BlockSpec(a.shape, lambda m: (0, 0))
     return pl.pallas_call(
         functools.partial(update_body, slots),
-        grid=(fine_dev // size,),
         out_shape=[jax.ShapeDtypeStruct((fine_dev, width), BF16)] * 2
         + [jax.ShapeDtypeStruct((SIDE, capacity, width), BF16)] * len(slots),
-        in_specs=[
-            pl.BlockSpec((1, size, width), lambda m: (0, m, 0)),
-            pl.BlockSpec((1, digits, LANES), lambda m: (0, 0, 0)),
-            pl.BlockSpec((size, width), lambda m: (m, 0)),
-            fixed(owner_hot),
-            fixed(rank_hot),
-        ]
-        + [pl.BlockSpec((size, width), lambda m: (m, 0))] * len(got)
-        + [pl.BlockSpec((16, width), lambda m: (fine_dev // 16, 0))] * len(got),
-        out_specs=[pl.BlockSpec((size, width), lambda m: (m, 0)), fixed(old_fine)]
-        + [pl.BlockSpec((SIDE, capacity, width), lambda m: (0, 0, 0))] * len(slots),
-        scratch_shapes=[
-            pltpu.VMEM((LANES, digits), F32),
-            pltpu.VMEM((SIDE * capacity, fine_dev), BF16),
-        ],
+        scratch_shapes=[pltpu.VMEM((SIDE * capacity, fine_dev), BF16)],
         compiler_params=pltpu.CompilerParams(vmem_limit_bytes=24 * MIB),
         name="new_fine",
-    )(acc, counts, old_fine, owner_hot, rank_hot, *got, *got)
+    )(acc, counts, old_fine, owner_hot, rank_hot, *got)
 
 
 def plan_body(coarse_dev, ids, owner_hot, rank_hot, labels):
@@ -583,7 +544,7 @@
 
     kept = []
     for part, group in (("far", order[:1]), ("near", order[1:])):
-        limit = 60 * MIB if part == "far" else None
+        limit = 61 * MIB
         keep = pack([(True, s, sent) for s in group], *rows, limit=limit)
         for s, a in zip(group, keep):
             kept.append(along(a, s, True))
@@ -626,12 +587,11 @@
     arrived = []
     for s, a in zip(order, keep):
         arrived.append(along(a, s, True))
-    give = place(
-        [(False, s) for s in order] + [(False, 0), (True, 0)], owner_hot, rank_hot, near_fine
-    )
+    give = place([(False, s) for s in order], owner_hot, rank_hot, near_fine)
     for s, a in zip(order, give):
         arrived.append(along(a, s, False))
-    arrived = [give[4], along(give[3], 0, False)] + arrived
+    here = place([(False, 0), (True, 0)], owner_hot, rank_hot, near_fine)
+    arrived = [here[1], along(here[0], 0, False)] + arrived
     *sent_sums, acc = coarse_sums(arrived, hot, digits, order + own)
     got = []
     for cross, part in zip(order, sent_sums):

time: 165 us -> 163 us (0.988)
  starting transfers between devices: 45.8 us -> 49.9 us
  waiting for transfers between devices: 58.3 us -> 55.4 us
  local copies, waits for them, and re-layouts: 13.4 us -> 11.2 us
    pallas_call x7, Pallas kernels: 28 us -> 24.3 us  [the longest x6 21.5 us: line_sums(): pl.pallas_call(body, out_shape=out_shape, scratch_shapes=[pltpu.VMEM((LAN...]
    ppermute x3, starting transfers between devices: 4.23 us -> 7.13 us  [level_step(): got.append(lax.ppermute(part, 'rows', cross_pairs(cross)))]
    pallas_call x3, Pallas kernels: 10.8 us -> 13.6 us  [pack(): pl.pallas_call(functools.partial(pack_body, slots, capacity, tags is not...]
    unnamed x54 -> x42, local copies, waits for them, and re-layouts: 13.4 us -> 11.2 us
    ppermute x20, waiting for transfers between devices: 46.9 us -> 45 us  [along(): return lax.ppermute(slots, 'rows', line_pairs(step, same_class))]
  transfers between devices with their start and end apart: 29 -> 29, of which waited for: 16 -> 13; matrix products, arithmetic and copies ran while one was open for 0% -> 0% of each run, Pallas kernels for 19% -> 19%
where the time goes in v4:
time: 163 us; the launch traced here: 162 us
  waiting for transfers between devices  55.4 us (34%)
  starting transfers between devices  49.9 us (31%)
  Pallas kernels  44.4 us (27%)
  local copies, waits for them, and re-layouts  11.2 us (7%)
    ppermute x20, waiting for transfers between devices, along(): return lax.ppermute(slots, 'rows', line_pairs(step, same_class))  45 us
    ppermute x20, starting transfers between devices, along(): return lax.ppermute(slots, 'rows', line_pairs(step, same_class))  32.4 us
    pallas_call x6, Pallas kernels, line_sums(): pl.pallas_call(body, out_shape=out_shape, scratch_shapes=[pltpu.VMEM((LAN...  21.5 us
    pallas_call x3, Pallas kernels, pack(): pl.pallas_call(functools.partial(pack_body, slots, capacity, tags is not...  13.6 us
    unnamed x42, local copies, waits for them, and re-layouts  11.2 us
    ppermute x3, waiting for transfers between devices, level_step(): pieces.append(lax.ppermute(means, 'grp', back))  7.33 us
    ppermute x3, starting transfers between devices, level_step(): got.append(lax.ppermute(part, 'rows', cross_pairs(cross)))  7.13 us
    ppermute x3, starting transfers between devices, level_step(): pieces.append(lax.ppermute(means, 'grp', back))  5.37 us
  transfers between devices with their start and end apart: 29, of which 13 were waited for; matrix products, arithmetic and copies ran while one was open for 0% of the time, Pallas kernels for 19%

profile of v4, /device:TPU:0, one launch (start us, length us, event | category | flops | bytes accessed | tf_op | source)
XLA Modules:
  0.0 161.9 jit_solution(13164591784100547309)
XLA Ops:
  5.5 6.1 %pack_rows.3 = (bf16[3,520,256]{2,1,0:T(8,128)(2,1)S(1)}, bf16[3,520,256]{2,1,0:T(8,128)(2,1)S(1)}, bf16[3,520,256]{2,1,0:T(8,128)(2,1)S(1)}, bf16[4,520,256]{2,...) custom-call(s32[1,32]{1,0:T(1,128)S(1)} %copy-done.5, ...), custom_call_target="tpu_custom_call" | custom-call | bytes 12247040 | tf_op jit(solution)/shard_map/pack_rows/pallas_call | solution.py:151
  18.5 3.6 %pack_rows.5 = bf16[3,520,256]{2,1,0:T(8,128)(2,1)} custom-call(s32[1,32]{1,0:T(1,128)} %counts.5, bf16[8192,256]{1,0:T(8,128)(2,1)} %emb.5, s32[64,128]{1,0:T(8,128)} %bitcast.3), custom_call_target="tpu_custom_call" | custom-call | bytes 1597440 | tf_op jit(solution)/shard_map/pack_rows/pallas_call | solution.py:151
  22.1 3.2 %collective-permute-start.12 = (bf16[3,520,256]{2,1,0:T(8,128)(2,1)}, bf16[3,520,256]{2,1,0:T(8,128)(2,1)}, u32[]{:S(2)}, u32[]{:S(2)}) collective-permute-start(bf16[3,520,256]{2,1,0:T(8,128)(2,1)} %pack_rows.5), channel_id=1, source_target_pairs={{0,64},{4,20},{8,72},{12,28},{16,80},{20,4},{24,88},{28,12},{32,96... | collective-permute-start | bytes 2396168 | tf_op jit(solution)/shard_map/ppermute | solution.py:539
  25.3 4.0 %pack_rows.4 = (bf16[3,520,256]{2,1,0:T(8,128)(2,1)}, bf16[3,520,256]{2,1,0:T(8,128)(2,1)}) custom-call(s32[1,32]{1,0:T(1,128)} %counts.5, bf16[8192,256]{1,0:T(8,128)(2,1)} %emb.5, s32[64,128]{1,0:T(8,128)} %bitcast.4), custom_call_target="tpu_custom_call" | custom-call | bytes 3194880 | tf_op jit(solution)/shard_map/pack_rows/pallas_call | solution.py:151
  30.0 2.6 %collective-permute-start.11 = (bf16[3,520,256]{2,1,0:T(8,128)(2,1)}, bf16[3,520,256]{2,1,0:T(8,128)(2,1)S(1)}, u32[]{:S(2)}, u32[]{:S(2)}) collective-permute-start(bf16[3,520,256]{2,1,0:T(8,128)(2,1)} %get-tuple-element.57), channel_id=1, source_target_pairs={{0,96},{4,28},{8,104},{12,4},{16,112},{20,12},{24,120},{28,20},{32... | collective-permute-start | bytes 2396168 | tf_op jit(solution)/shard_map/ppermute | solution.py:539
  32.6 4.8 %collective-permute-done.12.refs_2_ = bf16[3,520,256]{2,1,0:T(8,128)(2,1)} collective-permute-done((bf16[3,520,256]{2,1,0:T(8,128)(2,1)}, bf16[3,520,256]{2,1,0:T(8,128)(2,1)}, u32[]{:S(2)}, u32[]{:S(2)}) %collective-permute-start.12) | collective-permute-done | bytes 798752 | tf_op jit(solution)/shard_map/ppermute | solution.py:539
  37.4 4.0 %collective-permute-start.9 = (bf16[3,520,256]{2,1,0:T(8,128)(2,1)}, bf16[3,520,256]{2,1,0:T(8,128)(2,1)S(1)}, u32[]{:S(2)}, u32[]{:S(2)}) collective-permute-start(bf16[3,520,256]{2,1,0:T(8,128)(2,1)} %copy-done.6), channel_id=1, source_target_pairs={{0,28},{4,96},{8,4},{12,104},{16,12},{20,112},{24,20},{28,120},{32... | collective-permute-start | bytes 2396168 | tf_op jit(solution)/shard_map/ppermute | solution.py:539
  41.5 6.9 %line_sums.7 = (f32[3,2048,256]{2,1,0:T(8,128)S(1)}, f32[3,16,128]{2,1,0:T(8,128)S(1)}) custom-call(bf16[4,520,256]{2,1,0:T(8,128)(2,1)S(1)} %get-tuple-element.41.refs_0_, bf16[4,520,256]{2,1,0:T(8,128)(2,1)S(1)} %collective-permute-done.refs_1_, bf16[3,520,256]{2,1,0:T(8,128)(2,1)} %collective-permute-done.12.refs_2_), custom_call_target="tpu_custom_call" | custom-call | flops 4831838208 | bytes 14979072 | tf_op jit(solution)/shard_map/line_sums/pallas_call | solution.py:268
  48.4 9.7 %collective-permute-done.10.refs_0_ = bf16[3,520,256]{2,1,0:T(8,128)(2,1)S(1)} collective-permute-done((bf16[3,520,256]{2,1,0:T(8,128)(2,1)}, bf16[3,520,256]{2,1,0:T(8,128)(2,1)S(1)}, u32[]{:S(2)}, u32[]{:S(2)}) %collective-permute-start.10) | collective-permute-done | bytes 798752 | tf_op jit(solution)/shard_map/ppermute | solution.py:539
  58.1 5.0 %collective-permute-start.1 = (bf16[1,520,256]{2,1,0:T(8,128)(2,1)S(1)}, bf16[1,520,256]{2,1,0:T(8,128)(2,1)S(1)}, u32[]{:S(2)}, u32[]{:S(2)}) collective-permute-start(bf16[1,520,256]{2,1,0:T(8,128)(2,1)S(1)} %copy-done.20), channel_id=1, source_target_pairs={{0,64},{4,20},{8,72},{12,28},{16,80},{20,4},{24,88},{28,12},{32,96... | collective-permute-start | bytes 798728 | tf_op jit(solution)/shard_map/ppermute | solution.py:539
  63.1 4.0 %line_sums.8 = (f32[3,2048,256]{2,1,0:T(8,128)S(1)}, f32[3,16,128]{2,1,0:T(8,128)S(1)}) custom-call(bf16[3,520,256]{2,1,0:T(8,128)(2,1)S(1)} %collective-permute-done.10.refs_0_, bf16[3,520,256]{2,1,0:T(8,128)(2,1)S(1)} %collective-permute-done.11.refs_1_, f32[3,2048,256]{2,1,0:T(8,128)S(1)} %get-tuple-element.58.refs_2_, ...), custom_call_target="tpu_custom_call" | custom-call | flops 3221225472 | bytes 14180352 | tf_op jit(solution)/shard_map/line_sums/pallas_call | solution.py:268
  69.1 3.3 %collective-permute-start.15 = (bf16[2064,256]{1,0:T(8,128)(2,1)S(1)}, bf16[2064,256]{1,0:T(8,128)(2,1)S(1)}, u32[]{:S(2)}, u32[]{:S(2)}) collective-permute-start(bf16[2064,256]{1,0:T(8,128)(2,1)S(1)} %line_sums.11), channel_id=1, source_target_pairs={{0,24},{4,100},{8,0},{12,108},{16,8},{20,116},{24,16},{28,124},{32... | collective-permute-start | bytes 3170312 | tf_op jit(solution)/shard_map/ppermute | solution.py:573
  78.0 3.2 %collective-permute-start.3 = (bf16[1,520,256]{2,1,0:T(8,128)(2,1)S(1)}, bf16[1,520,256]{2,1,0:T(8,128)(2,1)S(1)}, u32[]{:S(2)}, u32[]{:S(2)}) collective-permute-start(bf16[1,520,256]{2,1,0:T(8,128)(2,1)S(1)} %copy-done.16), channel_id=1, source_target_pairs={{0,96},{4,28},{8,104},{12,4},{16,112},{20,12},{24,120},{28,20},{32... | collective-permute-start | bytes 798728 | tf_op jit(solution)/shard_map/ppermute | solution.py:539
  81.2 18.8 %collective-permute-done.3.refs_4_ = bf16[1,520,256]{2,1,0:T(8,128)(2,1)S(1)} collective-permute-done((bf16[1,520,256]{2,1,0:T(8,128)(2,1)S(1)}, bf16[1,520,256]{2,1,0:T(8,128)(2,1)S(1)}, u32[]{:S(2)}, u32[]{:S(2)}) %collective-permute-start.3) | collective-permute-done | bytes 266272 | tf_op jit(solution)/shard_map/ppermute | solution.py:539
  100.0 2.9 %collective-permute-done.4.refs_5_ = bf16[1,520,256]{2,1,0:T(8,128)(2,1)S(1)} collective-permute-done((bf16[1,520,256]{2,1,0:T(8,128)(2,1)S(1)}, bf16[1,520,256]{2,1,0:T(8,128)(2,1)S(1)}, u32[]{:S(2)}, u32[]{:S(2)}) %collective-permute-start.4) | collective-permute-done | bytes 266272 | tf_op jit(solution)/shard_map/ppermute | solution.py:539
  103.7 3.4 %collective-permute-done.5.refs_6_ = bf16[1,520,256]{2,1,0:T(8,128)(2,1)S(1)} collective-permute-done((bf16[1,520,256]{2,1,0:T(8,128)(2,1)S(1)}, bf16[1,520,256]{2,1,0:T(8,128)(2,1)S(1)}, u32[]{:S(2)}, u32[]{:S(2)}) %collective-permute-start.5) | collective-permute-done | bytes 266272 | tf_op jit(solution)/shard_map/ppermute | solution.py:539
  108.8 4.8 %line_sums.6 = (f32[1,2048,256]{2,1,0:T(8,128)S(1)}, f32[1,16,128]{2,1,0:T(8,128)S(1)}) custom-call(bf16[4,520,256]{2,1,0:T(8,128)(2,1)S(1)} %get-tuple-element.41.refs_0_, bf16[4,520,256]{2,1,0:T(8,128)(2,1)S(1)} %collective-permute-done.refs_1_, bf16[1,520,256]{2,1,0:T(8,128)(2,1)S(1)} %collective-permute-done.1.refs_2_, ...), custom_call_target="tpu_custom_call" | custom-call | flops 4294967296 | bytes 6324224 | tf_op jit(solution)/shard_map/line_sums/pallas_call | solution.py:268
  113.6 2.8 %new_fine.1 = (bf16[2048,256]{1,0:T(8,128)(2,1)}, bf16[2048,256]{1,0:T(8,128)(2,1)S(1)}, bf16[4,128,256]{2,1,0:T(8,128)(2,1)S(1)}, bf16[4,128,256]{2,1,0:T(8,128)(2,1)S(1)}, bf16[4,128,256]{2,1,0:T(8,128)(2,1)S(1)}) custom-call(f32[1,2048,256]{2,1,0:T(8,128)S(1)} %get-tuple-element.49.acc, f32[1,16,128]{2,1,0:T(8,128)S(1)} %get-tuple-element.50.counts, ...), custom_call_target="tpu_custom_call" | custom-call | tf_op jit(solution)/shard_map/new_fine/pallas_call | solution.py:316
  128.8 4.3 %collective-permute-start.19 = (bf16[4,128,256]{2,1,0:T(8,128)(2,1)S(1)}, bf16[4,128,256]{2,1,0:T(8,128)(2,1)S(1)}, u32[]{:S(2)}, u32[]{:S(2)}) collective-permute-start(bf16[4,128,256]{2,1,0:T(8,128)(2,1)S(1)} %get-tuple-element.68), channel_id=1, source_target_pairs={{0,96},{4,28},{8,104},{12,4},{16,112},{20,12},{24,120},{28,20},{32... | collective-permute-start | bytes 786440 | tf_op jit(solution)/shard_map/ppermute | solution.py:539
  137.7 3.9 %collective-permute-start.23 = (bf16[272,256]{1,0:T(8,128)(2,1)S(1)}, bf16[272,256]{1,0:T(8,128)(2,1)S(1)}, u32[]{:S(2)}, u32[]{:S(2)}) collective-permute-start(bf16[272,256]{1,0:T(8,128)(2,1)S(1)} %get-tuple-element.75), channel_id=1, source_target_pairs={{0,16},{4,68},{8,24},{12,76},{16,0},{20,84},{24,8},{28,92},{32,48}... | collective-permute-start | bytes 417800 | tf_op jit(solution)/shard_map/ppermute | solution.py:598
  141.9 2.9 %collective-permute-start.25 = (bf16[272,256]{1,0:T(8,128)(2,1)S(1)}, bf16[272,256]{1,0:T(8,128)(2,1)S(1)}, u32[]{:S(2)}, u32[]{:S(2)}) collective-permute-start(bf16[272,256]{1,0:T(8,128)(2,1)S(1)} %get-tuple-element.77), channel_id=1, source_target_pairs={{0,24},{4,100},{8,0},{12,108},{16,8},{20,116},{24,16},{28,124},{32... | collective-permute-start | bytes 417800 | tf_op jit(solution)/shard_map/ppermute | solution.py:598
  144.8 3.0 %collective-permute-done.24.refs_1_ = bf16[272,256]{1,0:T(8,128)(2,1)S(1)} collective-permute-done((bf16[272,256]{1,0:T(8,128)(2,1)S(1)}, bf16[272,256]{1,0:T(8,128)(2,1)S(1)}, u32[]{:S(2)}, u32[]{:S(2)}) %collective-permute-start.24) | collective-permute-done | bytes 139296 | tf_op jit(solution)/shard_map/ppermute | solution.py:598
  148.1 4.1 %collective-permute-start.26 = (bf16[256,256]{1,0:T(8,128)(2,1)S(1)}, bf16[256,256]{1,0:T(8,128)(2,1)S(1)}, u32[]{:S(2)}, u32[]{:S(2)}) collective-permute-start(bf16[256,256]{1,0:T(8,128)(2,1)S(1)} %coarse_means.1.refs_0_), channel_id=1, source_target_pairs={{1,0},{2,1},{3,2},{0,3},{5,4},{6,5},{7,6},{4,7},{9,8},{10,9},{11,1... | collective-permute-start | bytes 393224 | tf_op jit(solution)/shard_map/ppermute | solution.py:603
  153.5 3.9 %collective-permute-done.26.refs_1_ = bf16[256,256]{1,0:T(8,128)(2,1)S(1)} collective-permute-done((bf16[256,256]{1,0:T(8,128)(2,1)S(1)}, bf16[256,256]{1,0:T(8,128)(2,1)S(1)}, u32[]{:S(2)}, u32[]{:S(2)}) %collective-permute-start.26) | collective-permute-done | bytes 131104 | tf_op jit(solution)/shard_map/ppermute | solution.py:603
  (93 shorter events, 45.7 us)
Async XLA Ops:
  18.5 18.9 %collective-permute-start = (bf16[4,520,256]{2,1,0:T(8,128)(2,1)}, bf16[4,520,256]{2,1,0:T(8,128)(2,1)S(1)}, u32[]{:S(2)}, u32[]{:S(2)}) collective-permute-start(bf16[4,520,256]{2,1,0:T(8,128)(2,1)} %get-tuple-element.42), channel_id=1, source_target_pairs={{0,4},{4,0},{8,12},{12,8},{16,20},{20,16},{24,28},{28,24},{32,36},... | collective-permute-start | bytes 3194888 | tf_op jit(solution)/shard_map/ppermute | solution.py:539
  22.1 15.4 %collective-permute-start.12 = (bf16[3,520,256]{2,1,0:T(8,128)(2,1)}, bf16[3,520,256]{2,1,0:T(8,128)(2,1)}, u32[]{:S(2)}, u32[]{:S(2)}) collective-permute-start(bf16[3,520,256]{2,1,0:T(8,128)(2,1)} %pack_rows.5), channel_id=1, source_target_pairs={{0,64},{4,20},{8,72},{12,28},{16,80},{20,4},{24,88},{28,12},{32,96... | collective-permute-start | bytes 2396168 | tf_op jit(solution)/shard_map/ppermute | solution.py:539
  29.3 28.8 %collective-permute-start.10 = (bf16[3,520,256]{2,1,0:T(8,128)(2,1)}, bf16[3,520,256]{2,1,0:T(8,128)(2,1)S(1)}, u32[]{:S(2)}, u32[]{:S(2)}) collective-permute-start(bf16[3,520,256]{2,1,0:T(8,128)(2,1)} %get-tuple-element.56), channel_id=1, source_target_pairs={{0,32},{4,12},{8,40},{12,20},{16,48},{20,28},{24,56},{28,4},{32,64... | collective-permute-start | bytes 2396168 | tf_op jit(solution)/shard_map/ppermute | solution.py:539
  30.0 33.1 %collective-permute-start.11 = (bf16[3,520,256]{2,1,0:T(8,128)(2,1)}, bf16[3,520,256]{2,1,0:T(8,128)(2,1)S(1)}, u32[]{:S(2)}, u32[]{:S(2)}) collective-permute-start(bf16[3,520,256]{2,1,0:T(8,128)(2,1)} %get-tuple-element.57), channel_id=1, source_target_pairs={{0,96},{4,28},{8,104},{12,4},{16,112},{20,12},{24,120},{28,20},{32... | collective-permute-start | bytes 2396168 | tf_op jit(solution)/shard_map/ppermute | solution.py:539
  32.6 34.5 %collective-permute-start.7 = (bf16[3,520,256]{2,1,0:T(8,128)(2,1)}, bf16[3,520,256]{2,1,0:T(8,128)(2,1)S(1)}, u32[]{:S(2)}, u32[]{:S(2)}) collective-permute-start(bf16[3,520,256]{2,1,0:T(8,128)(2,1)} %copy-done.8), channel_id=1, source_target_pairs={{0,20},{4,64},{8,28},{12,72},{16,4},{20,80},{24,12},{28,88},{32,52... | collective-permute-start | bytes 2396168 | tf_op jit(solution)/shard_map/ppermute | solution.py:539
  37.4 29.7 %collective-permute-start.8 = (bf16[3,520,256]{2,1,0:T(8,128)(2,1)}, bf16[3,520,256]{2,1,0:T(8,128)(2,1)S(1)}, u32[]{:S(2)}, u32[]{:S(2)}) collective-permute-start(bf16[3,520,256]{2,1,0:T(8,128)(2,1)} %copy-done.7), channel_id=1, source_target_pairs={{0,12},{4,32},{8,20},{12,40},{16,28},{20,48},{24,4},{28,56},{32,44... | collective-permute-start | bytes 2396168 | tf_op jit(solution)/shard_map/ppermute | solution.py:539
  37.4 29.7 %collective-permute-start.9 = (bf16[3,520,256]{2,1,0:T(8,128)(2,1)}, bf16[3,520,256]{2,1,0:T(8,128)(2,1)S(1)}, u32[]{:S(2)}, u32[]{:S(2)}) collective-permute-start(bf16[3,520,256]{2,1,0:T(8,128)(2,1)} %copy-done.6), channel_id=1, source_target_pairs={{0,28},{4,96},{8,4},{12,104},{16,12},{20,112},{24,20},{28,120},{32... | collective-permute-start | bytes 2396168 | tf_op jit(solution)/shard_map/ppermute | solution.py:539
  58.1 19.9 %collective-permute-start.1 = (bf16[1,520,256]{2,1,0:T(8,128)(2,1)S(1)}, bf16[1,520,256]{2,1,0:T(8,128)(2,1)S(1)}, u32[]{:S(2)}, u32[]{:S(2)}) collective-permute-start(bf16[1,520,256]{2,1,0:T(8,128)(2,1)S(1)} %copy-done.20), channel_id=1, source_target_pairs={{0,64},{4,20},{8,72},{12,28},{16,80},{20,4},{24,88},{28,12},{32,96... | collective-permute-start | bytes 798728 | tf_op jit(solution)/shard_map/ppermute | solution.py:539
  63.1 18.1 %collective-permute-start.2 = (bf16[1,520,256]{2,1,0:T(8,128)(2,1)S(1)}, bf16[1,520,256]{2,1,0:T(8,128)(2,1)S(1)}, u32[]{:S(2)}, u32[]{:S(2)}) collective-permute-start(bf16[1,520,256]{2,1,0:T(8,128)(2,1)S(1)} %copy-done.18), channel_id=1, source_target_pairs={{0,32},{4,12},{8,40},{12,20},{16,48},{20,28},{24,56},{28,4},{32,64... | collective-permute-start | bytes 798728 | tf_op jit(solution)/shard_map/ppermute | solution.py:539
  69.1 44.5 %collective-permute-start.15 = (bf16[2064,256]{1,0:T(8,128)(2,1)S(1)}, bf16[2064,256]{1,0:T(8,128)(2,1)S(1)}, u32[]{:S(2)}, u32[]{:S(2)}) collective-permute-start(bf16[2064,256]{1,0:T(8,128)(2,1)S(1)} %line_sums.11), channel_id=1, source_target_pairs={{0,24},{4,100},{8,0},{12,108},{16,8},{20,116},{24,16},{28,124},{32... | collective-permute-start | bytes 3170312 | tf_op jit(solution)/shard_map/ppermute | solution.py:573
  74.3 39.3 %collective-permute-start.14 = (bf16[2064,256]{1,0:T(8,128)(2,1)S(1)}, bf16[2064,256]{1,0:T(8,128)(2,1)S(1)}, u32[]{:S(2)}, u32[]{:S(2)}) collective-permute-start(bf16[2064,256]{1,0:T(8,128)(2,1)S(1)} %line_sums.10), channel_id=1, source_target_pairs={{0,16},{4,68},{8,24},{12,76},{16,0},{20,84},{24,8},{28,92},{32,48}... | collective-permute-start | bytes 3170312 | tf_op jit(solution)/shard_map/ppermute | solution.py:573
  76.9 36.6 %collective-permute-start.13 = (bf16[2064,256]{1,0:T(8,128)(2,1)S(1)}, bf16[2064,256]{1,0:T(8,128)(2,1)S(1)}, u32[]{:S(2)}, u32[]{:S(2)}) collective-permute-start(bf16[2064,256]{1,0:T(8,128)(2,1)S(1)} %line_sums.9), channel_id=1, source_target_pairs={{0,8},{4,36},{8,16},{12,44},{16,24},{20,52},{24,0},{28,60},{32,40}... | collective-permute-start | bytes 3170312 | tf_op jit(solution)/shard_map/ppermute | solution.py:573
  78.0 22.0 %collective-permute-start.3 = (bf16[1,520,256]{2,1,0:T(8,128)(2,1)S(1)}, bf16[1,520,256]{2,1,0:T(8,128)(2,1)S(1)}, u32[]{:S(2)}, u32[]{:S(2)}) collective-permute-start(bf16[1,520,256]{2,1,0:T(8,128)(2,1)S(1)} %copy-done.16), channel_id=1, source_target_pairs={{0,96},{4,28},{8,104},{12,4},{16,112},{20,12},{24,120},{28,20},{32... | collective-permute-start | bytes 798728 | tf_op jit(solution)/shard_map/ppermute | solution.py:539
  81.2 21.7 %collective-permute-start.4 = (bf16[1,520,256]{2,1,0:T(8,128)(2,1)S(1)}, bf16[1,520,256]{2,1,0:T(8,128)(2,1)S(1)}, u32[]{:S(2)}, u32[]{:S(2)}) collective-permute-start(bf16[1,520,256]{2,1,0:T(8,128)(2,1)S(1)} %copy-done.14), channel_id=1, source_target_pairs={{0,20},{4,64},{8,28},{12,72},{16,4},{20,80},{24,12},{28,88},{32,52... | collective-permute-start | bytes 798728 | tf_op jit(solution)/shard_map/ppermute | solution.py:539
  118.2 9.0 %collective-permute-start.20 = (bf16[4,128,256]{2,1,0:T(8,128)(2,1)S(1)}, bf16[4,128,256]{2,1,0:T(8,128)(2,1)S(1)}, u32[]{:S(2)}, u32[]{:S(2)}) collective-permute-start(bf16[4,128,256]{2,1,0:T(8,128)(2,1)S(1)} %get-tuple-element.69), channel_id=1, source_target_pairs={{0,20},{4,64},{8,28},{12,72},{16,4},{20,80},{24,12},{28,88},{32,52... | collective-permute-start | bytes 786440 | tf_op jit(solution)/shard_map/ppermute | solution.py:539
  120.7 8.0 %collective-permute-start.21 = (bf16[4,128,256]{2,1,0:T(8,128)(2,1)S(1)}, bf16[4,128,256]{2,1,0:T(8,128)(2,1)S(1)}, u32[]{:S(2)}, u32[]{:S(2)}) collective-permute-start(bf16[4,128,256]{2,1,0:T(8,128)(2,1)S(1)} %get-tuple-element.70), channel_id=1, source_target_pairs={{0,12},{4,32},{8,20},{12,40},{16,28},{20,48},{24,4},{28,56},{32,44... | collective-permute-start | bytes 786440 | tf_op jit(solution)/shard_map/ppermute | solution.py:539
  121.4 12.5 %collective-permute-start.22 = (bf16[4,128,256]{2,1,0:T(8,128)(2,1)S(1)}, bf16[4,128,256]{2,1,0:T(8,128)(2,1)S(1)}, u32[]{:S(2)}, u32[]{:S(2)}) collective-permute-start(bf16[4,128,256]{2,1,0:T(8,128)(2,1)S(1)} %get-tuple-element.71), channel_id=1, source_target_pairs={{0,28},{4,96},{8,4},{12,104},{16,12},{20,112},{24,20},{28,120},{32... | collective-permute-start | bytes 786440 | tf_op jit(solution)/shard_map/ppermute | solution.py:539
  123.0 10.8 %collective-permute-start.16 = (bf16[4,128,256]{2,1,0:T(8,128)(2,1)S(1)}, bf16[4,128,256]{2,1,0:T(8,128)(2,1)S(1)}, u32[]{:S(2)}, u32[]{:S(2)}) collective-permute-start(bf16[4,128,256]{2,1,0:T(8,128)(2,1)S(1)} %get-tuple-element.65), channel_id=1, source_target_pairs={{0,4},{4,0},{8,12},{12,8},{16,20},{20,16},{24,28},{28,24},{32,36},... | collective-permute-start | bytes 786440 | tf_op jit(solution)/shard_map/ppermute | solution.py:539
  125.5 8.4 %collective-permute-start.17 = (bf16[4,128,256]{2,1,0:T(8,128)(2,1)S(1)}, bf16[4,128,256]{2,1,0:T(8,128)(2,1)S(1)}, u32[]{:S(2)}, u32[]{:S(2)}) collective-permute-start(bf16[4,128,256]{2,1,0:T(8,128)(2,1)S(1)} %get-tuple-element.66), channel_id=1, source_target_pairs={{0,64},{4,20},{8,72},{12,28},{16,80},{20,4},{24,88},{28,12},{32,96... | collective-permute-start | bytes 786440 | tf_op jit(solution)/shard_map/ppermute | solution.py:539
  127.2 8.9 %collective-permute-start.18 = (bf16[4,128,256]{2,1,0:T(8,128)(2,1)S(1)}, bf16[4,128,256]{2,1,0:T(8,128)(2,1)S(1)}, u32[]{:S(2)}, u32[]{:S(2)}) collective-permute-start(bf16[4,128,256]{2,1,0:T(8,128)(2,1)S(1)} %get-tuple-element.67), channel_id=1, source_target_pairs={{0,32},{4,12},{8,40},{12,20},{16,48},{20,28},{24,56},{28,4},{32,64... | collective-permute-start | bytes 786440 | tf_op jit(solution)/shard_map/ppermute | solution.py:539
  128.8 8.2 %collective-permute-start.19 = (bf16[4,128,256]{2,1,0:T(8,128)(2,1)S(1)}, bf16[4,128,256]{2,1,0:T(8,128)(2,1)S(1)}, u32[]{:S(2)}, u32[]{:S(2)}) collective-permute-start(bf16[4,128,256]{2,1,0:T(8,128)(2,1)S(1)} %get-tuple-element.68), channel_id=1, source_target_pairs={{0,96},{4,28},{8,104},{12,4},{16,112},{20,12},{24,120},{28,20},{32... | collective-permute-start | bytes 786440 | tf_op jit(solution)/shard_map/ppermute | solution.py:539
  148.1 9.3 %collective-permute-start.26 = (bf16[256,256]{1,0:T(8,128)(2,1)S(1)}, bf16[256,256]{1,0:T(8,128)(2,1)S(1)}, u32[]{:S(2)}, u32[]{:S(2)}) collective-permute-start(bf16[256,256]{1,0:T(8,128)(2,1)S(1)} %coarse_means.1.refs_0_), channel_id=1, source_target_pairs={{1,0},{2,1},{3,2},{0,3},{5,4},{6,5},{7,6},{4,7},{9,8},{10,9},{11,1... | collective-permute-start | bytes 393224 | tf_op jit(solution)/shard_map/ppermute | solution.py:603
  152.2 7.5 %collective-permute-start.27 = (bf16[256,256]{1,0:T(8,128)(2,1)S(1)}, bf16[256,256]{1,0:T(8,128)(2,1)S(1)}, u32[]{:S(2)}, u32[]{:S(2)}) collective-permute-start(bf16[256,256]{1,0:T(8,128)(2,1)S(1)} %coarse_means.1.refs_0_), channel_id=1, source_target_pairs={{2,0},{3,1},{0,2},{1,3},{6,4},{7,5},{4,6},{5,7},{10,8},{11,9},{8,1... | collective-permute-start | bytes 393224 | tf_op jit(solution)/shard_map/ppermute | solution.py:603
  152.2 8.6 %collective-permute-start.28 = (bf16[256,256]{1,0:T(8,128)(2,1)S(1)}, bf16[256,256]{1,0:T(8,128)(2,1)S(1)}, u32[]{:S(2)}, u32[]{:S(2)}) collective-permute-start(bf16[256,256]{1,0:T(8,128)(2,1)S(1)} %coarse_means.1.refs_0_), channel_id=1, source_target_pairs={{3,0},{0,1},{1,2},{2,3},{7,4},{4,5},{5,6},{6,7},{11,8},{8,9},{9,10... | collective-permute-start | bytes 393224 | tf_op jit(solution)/shard_map/ppermute | solution.py:603
  (26 other events, 168.2 us)

commit v5 on v4

--- a/solution.py
+++ b/solution.py
@@ -99,7 +99,8 @@
 
         @pl.when(at_step < len(crosses))
         def _():
-            cross = at_step + crosses[0]
+            stride = crosses[1] - crosses[0] if len(crosses) > 1 else 1
+            cross = at_step * stride + crosses[0]
             kind = core if same_class else 1 - core
             owner = owner_of(kind, step, cross)
             first = starts[owner]
@@ -552,24 +553,25 @@
         coarse_ids.reshape(1, -1), peers, capacity_two, coarse_dev
     )
     more = pack(
-        [(False, s, sent) for s in order]
+        [(False, s, (2,)) for s in order]
         + [(False, 0, own + sent), (True, 0, own + sent)]
-        + [(k, s, own) for k in (True, False) for s in order],
+        + [(k, s, own) for k in (True, False) for s in order]
+        + [(False, s, (1, 3)) for s in order],
         *rows,
         tags,
     )
     swapped = along(more[3], 0, False)
-    given = [along(a, s, False) for s, a in zip(order, more[:3])]
+    far_given = [along(a, s, False) for s, a in zip(order, more[:3])]
+    given = [along(a, s, False) for s, a in zip(order, more[11:])]
     near = [(more[4], 0), (swapped, 0)]
     had = line_sums(near + [(kept[0], 1)], capacity, fine_dev, sent)
     had = line_sums([(a, 1) for a in kept[1:]], capacity, fine_dev, sent, (*had, 1))
     kept_own = [along(a, s, True) for s, a in zip(order, more[5:8])]
-    given_own = [along(a, s, False) for s, a in zip(order, more[8:])]
+    given_own = [along(a, s, False) for s, a in zip(order, more[8:11])]
     got = {}
     for cross in order:
-        part = line_sums(
-            [(a, 1) for a in given], capacity, fine_dev, (cross,), (*had, 1), send=True
-        )
+        source = [(a, 2) for a in far_given] if cross == 2 else [(a, (cross + 1) // 2) for a in given]
+        part = line_sums(source, capacity, fine_dev, (cross,), (*had, 1), send=True)
         got[cross] = lax.ppermute(part, "rows", cross_pairs(cross))
     acc, counts = line_sums(near + [(a, 0) for a in kept_own + given_own], capacity, fine_dev, own)
     hot, digits = tag_hot(

time: 163 us -> 162 us (level)
  waiting for transfers between devices: 55.4 us -> 49.9 us
  starting transfers between devices: 49.9 us -> 53.1 us
  local copies, waits for them, and re-layouts: 11.2 us -> 13.1 us
    ppermute x20 -> x23, starting transfers between devices: 32.4 us -> 37.4 us  [along(): return lax.ppermute(slots, 'rows', line_pairs(step, same_class))]
    ppermute x20 -> x23, waiting for transfers between devices: 45 us -> 42.2 us  [along(): return lax.ppermute(slots, 'rows', line_pairs(step, same_class))]
    ppermute x3, waiting for transfers between devices: 7.33 us -> 4.65 us  [level_step(): pieces.append(lax.ppermute(means, 'grp', back))]
    unnamed x42 -> x54, local copies, waits for them, and re-layouts: 11.2 us -> 13.1 us
    ppermute x3, starting transfers between devices: 7.13 us -> 5.22 us  [level_step(): got.append(lax.ppermute(part, 'rows', cross_pairs(cross)))]
  transfers between devices with their start and end apart: 29 -> 32, of which waited for: 13 -> 12; matrix products, arithmetic and copies ran while one was open for 0% -> 0% of each run, Pallas kernels for 19% -> 20%
where the time goes in v5:
time: 162 us
  starting transfers between devices  53.1 us (33%)
  waiting for transfers between devices  49.9 us (31%)
  Pallas kernels  44.8 us (28%)
  local copies, waits for them, and re-layouts  13.1 us (8%)
    ppermute x23, waiting for transfers between devices, along(): return lax.ppermute(slots, 'rows', line_pairs(step, same_class))  42.2 us
    ppermute x23, starting transfers between devices, along(): return lax.ppermute(slots, 'rows', line_pairs(step, same_class))  37.4 us
    pallas_call x6, Pallas kernels, line_sums(): pl.pallas_call(body, out_shape=out_shape, scratch_shapes=[pltpu.VMEM((LAN...  21.4 us
    pallas_call x3, Pallas kernels, pack(): pl.pallas_call(functools.partial(pack_body, slots, capacity, tags is not...  14 us
    unnamed x54, local copies, waits for them, and re-layouts  13.1 us
    ppermute x3, starting transfers between devices, level_step(): pieces.append(lax.ppermute(means, 'grp', back))  6.58 us
    ppermute x3, starting transfers between devices, level_step(): got.append(lax.ppermute(part, 'rows', cross_pairs(cross)))  5.22 us
    ppermute x3, waiting for transfers between devices, level_step(): pieces.append(lax.ppermute(means, 'grp', back))  4.65 us
  transfers between devices with their start and end apart: 32, of which 12 were waited for; matrix products, arithmetic and copies ran while one was open for 0% of the time, Pallas kernels for 20%

profile of v5, /device:TPU:0, one launch (start us, length us, event | category | flops | bytes accessed | tf_op | source)
XLA Modules:
  0.0 161.8 jit_solution(9572324154640061337)
XLA Ops:
  5.5 6.5 %pack_rows.3 = (bf16[1,520,256]{2,1,0:T(8,128)(2,1)S(1)}, bf16[1,520,256]{2,1,0:T(8,128)(2,1)S(1)}, bf16[1,520,256]{2,1,0:T(8,128)(2,1)S(1)}, bf16[4,520,256]{2,...) custom-call(s32[1,32]{1,0:T(1,128)S(1)} %copy-done.5, ...), custom_call_target="tpu_custom_call" | custom-call | bytes 12247040 | tf_op jit(solution)/shard_map/pack_rows/pallas_call | solution.py:152
  20.9 3.5 %pack_rows.5 = bf16[3,520,256]{2,1,0:T(8,128)(2,1)} custom-call(s32[1,32]{1,0:T(1,128)} %counts.5, bf16[8192,256]{1,0:T(8,128)(2,1)} %emb.5, s32[64,128]{1,0:T(8,128)} %bitcast.3), custom_call_target="tpu_custom_call" | custom-call | bytes 1597440 | tf_op jit(solution)/shard_map/pack_rows/pallas_call | solution.py:152
  24.4 3.2 %collective-permute-start.12 = (bf16[3,520,256]{2,1,0:T(8,128)(2,1)}, bf16[3,520,256]{2,1,0:T(8,128)(2,1)}, u32[]{:S(2)}, u32[]{:S(2)}) collective-permute-start(bf16[3,520,256]{2,1,0:T(8,128)(2,1)} %pack_rows.5), channel_id=1, source_target_pairs={{0,64},{4,20},{8,72},{12,28},{16,80},{20,4},{24,88},{28,12},{32,96... | collective-permute-start | bytes 2396168 | tf_op jit(solution)/shard_map/ppermute | solution.py:540
  27.6 4.0 %pack_rows.4 = (bf16[3,520,256]{2,1,0:T(8,128)(2,1)}, bf16[3,520,256]{2,1,0:T(8,128)(2,1)}) custom-call(s32[1,32]{1,0:T(1,128)} %counts.5, bf16[8192,256]{1,0:T(8,128)(2,1)} %emb.5, s32[64,128]{1,0:T(8,128)} %bitcast.4), custom_call_target="tpu_custom_call" | custom-call | bytes 3194880 | tf_op jit(solution)/shard_map/pack_rows/pallas_call | solution.py:152
  32.3 2.6 %collective-permute-start.11 = (bf16[3,520,256]{2,1,0:T(8,128)(2,1)}, bf16[3,520,256]{2,1,0:T(8,128)(2,1)S(1)}, u32[]{:S(2)}, u32[]{:S(2)}) collective-permute-start(bf16[3,520,256]{2,1,0:T(8,128)(2,1)} %get-tuple-element.60), channel_id=1, source_target_pairs={{0,96},{4,28},{8,104},{12,4},{16,112},{20,12},{24,120},{28,20},{32... | collective-permute-start | bytes 2396168 | tf_op jit(solution)/shard_map/ppermute | solution.py:540
  34.9 4.9 %collective-permute-done.12.refs_2_ = bf16[3,520,256]{2,1,0:T(8,128)(2,1)} collective-permute-done((bf16[3,520,256]{2,1,0:T(8,128)(2,1)}, bf16[3,520,256]{2,1,0:T(8,128)(2,1)}, u32[]{:S(2)}, u32[]{:S(2)}) %collective-permute-start.12) | collective-permute-done | bytes 798752 | tf_op jit(solution)/shard_map/ppermute | solution.py:540
  39.8 4.0 %collective-permute-start.9 = (bf16[2,520,256]{2,1,0:T(8,128)(2,1)}, bf16[2,520,256]{2,1,0:T(8,128)(2,1)S(1)}, u32[]{:S(2)}, u32[]{:S(2)}) collective-permute-start(bf16[2,520,256]{2,1,0:T(8,128)(2,1)} %copy-done.6), channel_id=1, source_target_pairs={{0,28},{4,96},{8,4},{12,104},{16,12},{20,112},{24,20},{28,120},{32... | collective-permute-start | bytes 1597448 | tf_op jit(solution)/shard_map/ppermute | solution.py:540
  43.9 6.9 %line_sums.7 = (f32[3,2048,256]{2,1,0:T(8,128)S(1)}, f32[3,16,128]{2,1,0:T(8,128)S(1)}) custom-call(bf16[4,520,256]{2,1,0:T(8,128)(2,1)S(1)} %get-tuple-element.44.refs_0_, bf16[4,520,256]{2,1,0:T(8,128)(2,1)S(1)} %collective-permute-done.refs_1_, bf16[3,520,256]{2,1,0:T(8,128)(2,1)} %collective-permute-done.12.refs_2_), custom_call_target="tpu_custom_call" | custom-call | flops 4831838208 | bytes 14979072 | tf_op jit(solution)/shard_map/line_sums/pallas_call | solution.py:269
  50.8 6.8 %collective-permute-done.10.refs_0_ = bf16[3,520,256]{2,1,0:T(8,128)(2,1)S(1)} collective-permute-done((bf16[3,520,256]{2,1,0:T(8,128)(2,1)}, bf16[3,520,256]{2,1,0:T(8,128)(2,1)S(1)}, u32[]{:S(2)}, u32[]{:S(2)}) %collective-permute-start.10) | collective-permute-done | bytes 798752 | tf_op jit(solution)/shard_map/ppermute | solution.py:540
  57.6 3.9 %collective-permute-start.1 = (bf16[1,520,256]{2,1,0:T(8,128)(2,1)S(1)}, bf16[1,520,256]{2,1,0:T(8,128)(2,1)S(1)}, u32[]{:S(2)}, u32[]{:S(2)}) collective-permute-start(bf16[1,520,256]{2,1,0:T(8,128)(2,1)S(1)} %copy-done.20), channel_id=1, source_target_pairs={{0,64},{4,20},{8,72},{12,28},{16,80},{20,4},{24,88},{28,12},{32,96... | collective-permute-start | bytes 798728 | tf_op jit(solution)/shard_map/ppermute | solution.py:540
  61.5 4.0 %line_sums.8 = (f32[3,2048,256]{2,1,0:T(8,128)S(1)}, f32[3,16,128]{2,1,0:T(8,128)S(1)}) custom-call(bf16[3,520,256]{2,1,0:T(8,128)(2,1)S(1)} %collective-permute-done.10.refs_0_, bf16[3,520,256]{2,1,0:T(8,128)(2,1)S(1)} %collective-permute-done.11.refs_1_, f32[3,2048,256]{2,1,0:T(8,128)S(1)} %get-tuple-element.61.refs_2_, ...), custom_call_target="tpu_custom_call" | custom-call | flops 3221225472 | bytes 14180352 | tf_op jit(solution)/shard_map/line_sums/pallas_call | solution.py:269
  66.2 2.9 %collective-permute-start.15 = (bf16[1,520,256]{2,1,0:T(8,128)(2,1)S(1)}, bf16[1,520,256]{2,1,0:T(8,128)(2,1)S(1)}, u32[]{:S(2)}, u32[]{:S(2)}) collective-permute-start(bf16[1,520,256]{2,1,0:T(8,128)(2,1)S(1)} %copy-done.24), channel_id=1, source_target_pairs={{0,12},{4,32},{8,20},{12,40},{16,28},{20,48},{24,4},{28,56},{32,44... | collective-permute-start | bytes 798728 | tf_op jit(solution)/shard_map/ppermute | solution.py:540
  75.8 2.8 %collective-permute-start.18 = (bf16[2064,256]{1,0:T(8,128)(2,1)S(1)}, bf16[2064,256]{1,0:T(8,128)(2,1)S(1)}, u32[]{:S(2)}, u32[]{:S(2)}) collective-permute-start(bf16[2064,256]{1,0:T(8,128)(2,1)S(1)} %line_sums.11), channel_id=1, source_target_pairs={{0,24},{4,100},{8,0},{12,108},{16,8},{20,116},{24,16},{28,124},{32... | collective-permute-start | bytes 3170312 | tf_op jit(solution)/shard_map/ppermute | solution.py:575
  84.2 6.8 %collective-permute-done.3.refs_4_ = bf16[1,520,256]{2,1,0:T(8,128)(2,1)S(1)} collective-permute-done((bf16[1,520,256]{2,1,0:T(8,128)(2,1)S(1)}, bf16[1,520,256]{2,1,0:T(8,128)(2,1)S(1)}, u32[]{:S(2)}, u32[]{:S(2)}) %collective-permute-start.3) | collective-permute-done | bytes 266272 | tf_op jit(solution)/shard_map/ppermute | solution.py:540
  91.0 13.0 %collective-permute-done.4.refs_5_ = bf16[1,520,256]{2,1,0:T(8,128)(2,1)S(1)} collective-permute-done((bf16[1,520,256]{2,1,0:T(8,128)(2,1)S(1)}, bf16[1,520,256]{2,1,0:T(8,128)(2,1)S(1)}, u32[]{:S(2)}, u32[]{:S(2)}) %collective-permute-start.4) | collective-permute-done | bytes 266272 | tf_op jit(solution)/shard_map/ppermute | solution.py:540
  103.9 6.0 %collective-permute-start.6 = (bf16[1,520,256]{2,1,0:T(8,128)(2,1)S(1)}, bf16[1,520,256]{2,1,0:T(8,128)(2,1)S(1)}, u32[]{:S(2)}, u32[]{:S(2)}) collective-permute-start(bf16[1,520,256]{2,1,0:T(8,128)(2,1)S(1)} %copy-done.10), channel_id=1, source_target_pairs={{0,28},{4,96},{8,4},{12,104},{16,12},{20,112},{24,20},{28,120},{32... | collective-permute-start | bytes 798728 | tf_op jit(solution)/shard_map/ppermute | solution.py:540
  109.9 3.9 %collective-permute-done.6.refs_7_ = bf16[1,520,256]{2,1,0:T(8,128)(2,1)S(1)} collective-permute-done((bf16[1,520,256]{2,1,0:T(8,128)(2,1)S(1)}, bf16[1,520,256]{2,1,0:T(8,128)(2,1)S(1)}, u32[]{:S(2)}, u32[]{:S(2)}) %collective-permute-start.6) | collective-permute-done | bytes 266272 | tf_op jit(solution)/shard_map/ppermute | solution.py:540
  113.8 4.8 %line_sums.6 = (f32[1,2048,256]{2,1,0:T(8,128)S(1)}, f32[1,16,128]{2,1,0:T(8,128)S(1)}) custom-call(bf16[4,520,256]{2,1,0:T(8,128)(2,1)S(1)} %get-tuple-element.44.refs_0_, bf16[4,520,256]{2,1,0:T(8,128)(2,1)S(1)} %collective-permute-done.refs_1_, bf16[1,520,256]{2,1,0:T(8,128)(2,1)S(1)} %collective-permute-done.1.refs_2_, ...), custom_call_target="tpu_custom_call" | custom-call | flops 4294967296 | bytes 6324224 | tf_op jit(solution)/shard_map/line_sums/pallas_call | solution.py:269
  118.7 2.8 %new_fine.1 = (bf16[2048,256]{1,0:T(8,128)(2,1)}, bf16[2048,256]{1,0:T(8,128)(2,1)S(1)}, bf16[4,128,256]{2,1,0:T(8,128)(2,1)S(1)}, bf16[4,128,256]{2,1,0:T(8,128)(2,1)S(1)}, bf16[4,128,256]{2,1,0:T(8,128)(2,1)S(1)}) custom-call(f32[1,2048,256]{2,1,0:T(8,128)S(1)} %get-tuple-element.52.acc, f32[1,16,128]{2,1,0:T(8,128)S(1)} %get-tuple-element.53.counts, ...), custom_call_target="tpu_custom_call" | custom-call | tf_op jit(solution)/shard_map/new_fine/pallas_call | solution.py:317
  134.5 3.0 %collective-permute-done.23.refs_5_ = bf16[4,128,256]{2,1,0:T(8,128)(2,1)S(1)} collective-permute-done((bf16[4,128,256]{2,1,0:T(8,128)(2,1)S(1)}, bf16[4,128,256]{2,1,0:T(8,128)(2,1)S(1)}, u32[]{:S(2)}, u32[]{:S(2)}) %collective-permute-start.23) | collective-permute-done | bytes 262176 | tf_op jit(solution)/shard_map/ppermute | solution.py:540
  137.5 2.7 %collective-permute-done.24.refs_6_ = bf16[4,128,256]{2,1,0:T(8,128)(2,1)S(1)} collective-permute-done((bf16[4,128,256]{2,1,0:T(8,128)(2,1)S(1)}, bf16[4,128,256]{2,1,0:T(8,128)(2,1)S(1)}, u32[]{:S(2)}, u32[]{:S(2)}) %collective-permute-start.24) | collective-permute-done | bytes 262176 | tf_op jit(solution)/shard_map/ppermute | solution.py:540
  143.4 2.8 %collective-permute-start.28 = (bf16[272,256]{1,0:T(8,128)(2,1)S(1)}, bf16[272,256]{1,0:T(8,128)(2,1)S(1)}, u32[]{:S(2)}, u32[]{:S(2)}) collective-permute-start(bf16[272,256]{1,0:T(8,128)(2,1)S(1)} %get-tuple-element.83), channel_id=1, source_target_pairs={{0,24},{4,100},{8,0},{12,108},{16,8},{20,116},{24,16},{28,124},{32... | collective-permute-start | bytes 417800 | tf_op jit(solution)/shard_map/ppermute | solution.py:600
  151.5 3.6 %collective-permute-start.30 = (bf16[256,256]{1,0:T(8,128)(2,1)S(1)}, bf16[256,256]{1,0:T(8,128)(2,1)S(1)}, u32[]{:S(2)}, u32[]{:S(2)}) collective-permute-start(bf16[256,256]{1,0:T(8,128)(2,1)S(1)} %coarse_means.1.refs_0_), channel_id=1, source_target_pairs={{2,0},{3,1},{0,2},{1,3},{6,4},{7,5},{4,6},{5,7},{10,8},{11,9},{8,1... | collective-permute-start | bytes 393224 | tf_op jit(solution)/shard_map/ppermute | solution.py:605
  157.0 3.7 %collective-permute-done.30.refs_2_ = bf16[256,256]{1,0:T(8,128)(2,1)S(1)} collective-permute-done((bf16[256,256]{1,0:T(8,128)(2,1)S(1)}, bf16[256,256]{1,0:T(8,128)(2,1)S(1)}, u32[]{:S(2)}, u32[]{:S(2)}) %collective-permute-start.30) | collective-permute-done | bytes 131104 | tf_op jit(solution)/shard_map/ppermute | solution.py:605
  (111 shorter events, 51.7 us)
Async XLA Ops:
  20.9 18.9 %collective-permute-start = (bf16[4,520,256]{2,1,0:T(8,128)(2,1)}, bf16[4,520,256]{2,1,0:T(8,128)(2,1)S(1)}, u32[]{:S(2)}, u32[]{:S(2)}) collective-permute-start(bf16[4,520,256]{2,1,0:T(8,128)(2,1)} %get-tuple-element.45), channel_id=1, source_target_pairs={{0,4},{4,0},{8,12},{12,8},{16,20},{20,16},{24,28},{28,24},{32,36},... | collective-permute-start | bytes 3194888 | tf_op jit(solution)/shard_map/ppermute | solution.py:540
  24.4 15.4 %collective-permute-start.12 = (bf16[3,520,256]{2,1,0:T(8,128)(2,1)}, bf16[3,520,256]{2,1,0:T(8,128)(2,1)}, u32[]{:S(2)}, u32[]{:S(2)}) collective-permute-start(bf16[3,520,256]{2,1,0:T(8,128)(2,1)} %pack_rows.5), channel_id=1, source_target_pairs={{0,64},{4,20},{8,72},{12,28},{16,80},{20,4},{24,88},{28,12},{32,96... | collective-permute-start | bytes 2396168 | tf_op jit(solution)/shard_map/ppermute | solution.py:540
  31.6 26.0 %collective-permute-start.10 = (bf16[3,520,256]{2,1,0:T(8,128)(2,1)}, bf16[3,520,256]{2,1,0:T(8,128)(2,1)S(1)}, u32[]{:S(2)}, u32[]{:S(2)}) collective-permute-start(bf16[3,520,256]{2,1,0:T(8,128)(2,1)} %get-tuple-element.59), channel_id=1, source_target_pairs={{0,32},{4,12},{8,40},{12,20},{16,48},{20,28},{24,56},{28,4},{32,64... | collective-permute-start | bytes 2396168 | tf_op jit(solution)/shard_map/ppermute | solution.py:540
  32.3 29.2 %collective-permute-start.11 = (bf16[3,520,256]{2,1,0:T(8,128)(2,1)}, bf16[3,520,256]{2,1,0:T(8,128)(2,1)S(1)}, u32[]{:S(2)}, u32[]{:S(2)}) collective-permute-start(bf16[3,520,256]{2,1,0:T(8,128)(2,1)} %get-tuple-element.60), channel_id=1, source_target_pairs={{0,96},{4,28},{8,104},{12,4},{16,112},{20,12},{24,120},{28,20},{32... | collective-permute-start | bytes 2396168 | tf_op jit(solution)/shard_map/ppermute | solution.py:540
  34.9 30.6 %collective-permute-start.7 = (bf16[2,520,256]{2,1,0:T(8,128)(2,1)}, bf16[2,520,256]{2,1,0:T(8,128)(2,1)S(1)}, u32[]{:S(2)}, u32[]{:S(2)}) collective-permute-start(bf16[2,520,256]{2,1,0:T(8,128)(2,1)} %copy-done.8), channel_id=1, source_target_pairs={{0,20},{4,64},{8,28},{12,72},{16,4},{20,80},{24,12},{28,88},{32,52... | collective-permute-start | bytes 1597448 | tf_op jit(solution)/shard_map/ppermute | solution.py:540
  39.8 26.4 %collective-permute-start.8 = (bf16[2,520,256]{2,1,0:T(8,128)(2,1)}, bf16[2,520,256]{2,1,0:T(8,128)(2,1)S(1)}, u32[]{:S(2)}, u32[]{:S(2)}) collective-permute-start(bf16[2,520,256]{2,1,0:T(8,128)(2,1)} %copy-done.7), channel_id=1, source_target_pairs={{0,12},{4,32},{8,20},{12,40},{16,28},{20,48},{24,4},{28,56},{32,44... | collective-permute-start | bytes 1597448 | tf_op jit(solution)/shard_map/ppermute | solution.py:540
  39.8 29.3 %collective-permute-start.9 = (bf16[2,520,256]{2,1,0:T(8,128)(2,1)}, bf16[2,520,256]{2,1,0:T(8,128)(2,1)S(1)}, u32[]{:S(2)}, u32[]{:S(2)}) collective-permute-start(bf16[2,520,256]{2,1,0:T(8,128)(2,1)} %copy-done.6), channel_id=1, source_target_pairs={{0,28},{4,96},{8,4},{12,104},{16,12},{20,112},{24,20},{28,120},{32... | collective-permute-start | bytes 1597448 | tf_op jit(solution)/shard_map/ppermute | solution.py:540
  57.6 24.0 %collective-permute-start.1 = (bf16[1,520,256]{2,1,0:T(8,128)(2,1)S(1)}, bf16[1,520,256]{2,1,0:T(8,128)(2,1)S(1)}, u32[]{:S(2)}, u32[]{:S(2)}) collective-permute-start(bf16[1,520,256]{2,1,0:T(8,128)(2,1)S(1)} %copy-done.20), channel_id=1, source_target_pairs={{0,64},{4,20},{8,72},{12,28},{16,80},{20,4},{24,88},{28,12},{32,96... | collective-permute-start | bytes 798728 | tf_op jit(solution)/shard_map/ppermute | solution.py:540
  61.4 22.8 %collective-permute-start.2 = (bf16[1,520,256]{2,1,0:T(8,128)(2,1)S(1)}, bf16[1,520,256]{2,1,0:T(8,128)(2,1)S(1)}, u32[]{:S(2)}, u32[]{:S(2)}) collective-permute-start(bf16[1,520,256]{2,1,0:T(8,128)(2,1)S(1)} %copy-done.18), channel_id=1, source_target_pairs={{0,32},{4,12},{8,40},{12,20},{16,48},{20,28},{24,56},{28,4},{32,64... | collective-permute-start | bytes 798728 | tf_op jit(solution)/shard_map/ppermute | solution.py:540
  65.5 9.1 %collective-permute-start.14 = (bf16[1,520,256]{2,1,0:T(8,128)(2,1)S(1)}, bf16[1,520,256]{2,1,0:T(8,128)(2,1)S(1)}, u32[]{:S(2)}, u32[]{:S(2)}) collective-permute-start(bf16[1,520,256]{2,1,0:T(8,128)(2,1)S(1)} %copy-done.26), channel_id=1, source_target_pairs={{0,20},{4,64},{8,28},{12,72},{16,4},{20,80},{24,12},{28,88},{32,52... | collective-permute-start | bytes 798728 | tf_op jit(solution)/shard_map/ppermute | solution.py:540
  66.2 9.6 %collective-permute-start.15 = (bf16[1,520,256]{2,1,0:T(8,128)(2,1)S(1)}, bf16[1,520,256]{2,1,0:T(8,128)(2,1)S(1)}, u32[]{:S(2)}, u32[]{:S(2)}) collective-permute-start(bf16[1,520,256]{2,1,0:T(8,128)(2,1)S(1)} %copy-done.24), channel_id=1, source_target_pairs={{0,12},{4,32},{8,20},{12,40},{16,28},{20,48},{24,4},{28,56},{32,44... | collective-permute-start | bytes 798728 | tf_op jit(solution)/shard_map/ppermute | solution.py:540
  69.1 9.5 %collective-permute-start.16 = (bf16[1,520,256]{2,1,0:T(8,128)(2,1)S(1)}, bf16[1,520,256]{2,1,0:T(8,128)(2,1)S(1)}, u32[]{:S(2)}, u32[]{:S(2)}) collective-permute-start(bf16[1,520,256]{2,1,0:T(8,128)(2,1)S(1)} %copy-done.22), channel_id=1, source_target_pairs={{0,28},{4,96},{8,4},{12,104},{16,12},{20,112},{24,20},{28,120},{32... | collective-permute-start | bytes 798728 | tf_op jit(solution)/shard_map/ppermute | solution.py:540
  74.7 44.0 %collective-permute-start.13 = (bf16[2064,256]{1,0:T(8,128)(2,1)S(1)}, bf16[2064,256]{1,0:T(8,128)(2,1)S(1)}, u32[]{:S(2)}, u32[]{:S(2)}) collective-permute-start(bf16[2064,256]{1,0:T(8,128)(2,1)S(1)} %line_sums.9), channel_id=1, source_target_pairs={{0,8},{4,36},{8,16},{12,44},{16,24},{20,52},{24,0},{28,60},{32,40}... | collective-permute-start | bytes 3170312 | tf_op jit(solution)/shard_map/ppermute | solution.py:575
  75.8 42.9 %collective-permute-start.18 = (bf16[2064,256]{1,0:T(8,128)(2,1)S(1)}, bf16[2064,256]{1,0:T(8,128)(2,1)S(1)}, u32[]{:S(2)}, u32[]{:S(2)}) collective-permute-start(bf16[2064,256]{1,0:T(8,128)(2,1)S(1)} %line_sums.11), channel_id=1, source_target_pairs={{0,24},{4,100},{8,0},{12,108},{16,8},{20,116},{24,16},{28,124},{32... | collective-permute-start | bytes 3170312 | tf_op jit(solution)/shard_map/ppermute | solution.py:575
  80.5 38.1 %collective-permute-start.17 = (bf16[2064,256]{1,0:T(8,128)(2,1)S(1)}, bf16[2064,256]{1,0:T(8,128)(2,1)S(1)}, u32[]{:S(2)}, u32[]{:S(2)}) collective-permute-start(bf16[2064,256]{1,0:T(8,128)(2,1)S(1)} %line_sums.10), channel_id=1, source_target_pairs={{0,16},{4,68},{8,24},{12,76},{16,0},{20,84},{24,8},{28,92},{32,48}... | collective-permute-start | bytes 3170312 | tf_op jit(solution)/shard_map/ppermute | solution.py:575
  81.6 9.4 %collective-permute-start.3 = (bf16[1,520,256]{2,1,0:T(8,128)(2,1)S(1)}, bf16[1,520,256]{2,1,0:T(8,128)(2,1)S(1)}, u32[]{:S(2)}, u32[]{:S(2)}) collective-permute-start(bf16[1,520,256]{2,1,0:T(8,128)(2,1)S(1)} %copy-done.16), channel_id=1, source_target_pairs={{0,96},{4,28},{8,104},{12,4},{16,112},{20,12},{24,120},{28,20},{32... | collective-permute-start | bytes 798728 | tf_op jit(solution)/shard_map/ppermute | solution.py:540
  84.2 19.7 %collective-permute-start.4 = (bf16[1,520,256]{2,1,0:T(8,128)(2,1)S(1)}, bf16[1,520,256]{2,1,0:T(8,128)(2,1)S(1)}, u32[]{:S(2)}, u32[]{:S(2)}) collective-permute-start(bf16[1,520,256]{2,1,0:T(8,128)(2,1)S(1)} %copy-done.14), channel_id=1, source_target_pairs={{0,20},{4,64},{8,28},{12,72},{16,4},{20,80},{24,12},{28,88},{32,52... | collective-permute-start | bytes 798728 | tf_op jit(solution)/shard_map/ppermute | solution.py:540
  91.0 18.9 %collective-permute-start.5 = (bf16[1,520,256]{2,1,0:T(8,128)(2,1)S(1)}, bf16[1,520,256]{2,1,0:T(8,128)(2,1)S(1)}, u32[]{:S(2)}, u32[]{:S(2)}) collective-permute-start(bf16[1,520,256]{2,1,0:T(8,128)(2,1)S(1)} %copy-done.12), channel_id=1, source_target_pairs={{0,12},{4,32},{8,20},{12,40},{16,28},{20,48},{24,4},{28,56},{32,44... | collective-permute-start | bytes 798728 | tf_op jit(solution)/shard_map/ppermute | solution.py:540
  103.9 9.9 %collective-permute-start.6 = (bf16[1,520,256]{2,1,0:T(8,128)(2,1)S(1)}, bf16[1,520,256]{2,1,0:T(8,128)(2,1)S(1)}, u32[]{:S(2)}, u32[]{:S(2)}) collective-permute-start(bf16[1,520,256]{2,1,0:T(8,128)(2,1)S(1)} %copy-done.10), channel_id=1, source_target_pairs={{0,28},{4,96},{8,4},{12,104},{16,12},{20,112},{24,20},{28,120},{32... | collective-permute-start | bytes 798728 | tf_op jit(solution)/shard_map/ppermute | solution.py:540
  121.5 10.6 %collective-permute-start.20 = (bf16[4,128,256]{2,1,0:T(8,128)(2,1)S(1)}, bf16[4,128,256]{2,1,0:T(8,128)(2,1)S(1)}, u32[]{:S(2)}, u32[]{:S(2)}) collective-permute-start(bf16[4,128,256]{2,1,0:T(8,128)(2,1)S(1)} %get-tuple-element.72), channel_id=1, source_target_pairs={{0,64},{4,20},{8,72},{12,28},{16,80},{20,4},{24,88},{28,12},{32,96... | collective-permute-start | bytes 786440 | tf_op jit(solution)/shard_map/ppermute | solution.py:540
  123.6 8.5 %collective-permute-start.21 = (bf16[4,128,256]{2,1,0:T(8,128)(2,1)S(1)}, bf16[4,128,256]{2,1,0:T(8,128)(2,1)S(1)}, u32[]{:S(2)}, u32[]{:S(2)}) collective-permute-start(bf16[4,128,256]{2,1,0:T(8,128)(2,1)S(1)} %get-tuple-element.73), channel_id=1, source_target_pairs={{0,32},{4,12},{8,40},{12,20},{16,48},{20,28},{24,56},{28,4},{32,64... | collective-permute-start | bytes 786440 | tf_op jit(solution)/shard_map/ppermute | solution.py:540
  125.2 9.3 %collective-permute-start.22 = (bf16[4,128,256]{2,1,0:T(8,128)(2,1)S(1)}, bf16[4,128,256]{2,1,0:T(8,128)(2,1)S(1)}, u32[]{:S(2)}, u32[]{:S(2)}) collective-permute-start(bf16[4,128,256]{2,1,0:T(8,128)(2,1)S(1)} %get-tuple-element.74), channel_id=1, source_target_pairs={{0,96},{4,28},{8,104},{12,4},{16,112},{20,12},{24,120},{28,20},{32... | collective-permute-start | bytes 786440 | tf_op jit(solution)/shard_map/ppermute | solution.py:540
  132.1 8.1 %collective-permute-start.24 = (bf16[4,128,256]{2,1,0:T(8,128)(2,1)S(1)}, bf16[4,128,256]{2,1,0:T(8,128)(2,1)S(1)}, u32[]{:S(2)}, u32[]{:S(2)}) collective-permute-start(bf16[4,128,256]{2,1,0:T(8,128)(2,1)S(1)} %get-tuple-element.76), channel_id=1, source_target_pairs={{0,12},{4,32},{8,20},{12,40},{16,28},{20,48},{24,4},{28,56},{32,44... | collective-permute-start | bytes 786440 | tf_op jit(solution)/shard_map/ppermute | solution.py:540
  151.5 9.2 %collective-permute-start.30 = (bf16[256,256]{1,0:T(8,128)(2,1)S(1)}, bf16[256,256]{1,0:T(8,128)(2,1)S(1)}, u32[]{:S(2)}, u32[]{:S(2)}) collective-permute-start(bf16[256,256]{1,0:T(8,128)(2,1)S(1)} %coarse_means.1.refs_0_), channel_id=1, source_target_pairs={{2,0},{3,1},{0,2},{1,3},{6,4},{7,5},{4,6},{5,7},{10,8},{11,9},{8,1... | collective-permute-start | bytes 393224 | tf_op jit(solution)/shard_map/ppermute | solution.py:605
  (35 other events, 200.5 us)

commit v6 on v5

--- a/solution.py
+++ b/solution.py
@@ -193,10 +193,12 @@
     size = onehot.shape[0]
     group = size // LANES
     fine_dev = digits * LANES
+    stride = crosses[1] - crosses[0] if len(crosses) > 1 else 1
 
     def one(i):
+        cross = crosses[0] + i * stride
         for s in range(sources):
-            slot = arrived[s].at[crosses[0] - lowest[s] + i]
+            slot = arrived[s].at[cross - lowest[s]]
             tail = slot[capacity:, :].astype(F32)
             data[s * capacity : (s + 1) * capacity, :] = slot[:capacity, :]
             for part in range(capacity // LANES):
@@ -216,7 +218,7 @@
             preferred_element_type=F32,
         )
         if had_counts is not None:
-            counts = counts + had_counts[crosses[0] - had_lowest + i]
+            counts = counts + had_counts[cross - had_lowest]
         if sent:
             tens = jnp.floor(counts / 64.0)
             out[fine_dev:, :] = jnp.concatenate([tens, counts - 64.0 * tens], axis=1).astype(BF16)
@@ -232,7 +234,7 @@
             total = jnp.dot(onehot[...], data[...], preferred_element_type=F32)
             rows = slice(part * size, (part + 1) * size)
             if had_acc is not None:
-                total = total + had_acc[crosses[0] - had_lowest + i, rows, :]
+                total = total + had_acc[cross - had_lowest, rows, :]
             if sent:
                 out[rows, :] = total.astype(BF16)
             else:
@@ -249,7 +251,7 @@
     tall = capacity + TAIL
     sources = len(arrived)
     digits = fine_dev // LANES
-    size = fine_dev // 2
+    size = fine_dev // 4
     many = len(crosses)
     operands = [a for a, _ in arrived]
     had_lowest = None
@@ -545,7 +547,7 @@
 
     kept = []
     for part, group in (("far", order[:1]), ("near", order[1:])):
-        limit = 61 * MIB
+        limit = 61 * MIB if part == "far" else None
         keep = pack([(True, s, sent) for s in group], *rows, limit=limit)
         for s, a in zip(group, keep):
             kept.append(along(a, s, True))
@@ -565,14 +567,19 @@
     given = [along(a, s, False) for s, a in zip(order, more[11:])]
     near = [(more[4], 0), (swapped, 0)]
     had = line_sums(near + [(kept[0], 1)], capacity, fine_dev, sent)
-    had = line_sums([(a, 1) for a in kept[1:]], capacity, fine_dev, sent, (*had, 1))
     kept_own = [along(a, s, True) for s, a in zip(order, more[5:8])]
     given_own = [along(a, s, False) for s, a in zip(order, more[8:11])]
+    close = [(a, 1) for a in kept[1:]]
     got = {}
     for cross in order:
-        source = [(a, 2) for a in far_given] if cross == 2 else [(a, (cross + 1) // 2) for a in given]
-        part = line_sums(source, capacity, fine_dev, (cross,), (*had, 1), send=True)
+        source = [(a, (cross + 1) // 2) for a in given]
+        before = (*had, (cross + 1) // 2)
+        if cross == 2:
+            source, before = close + [(a, 2) for a in far_given], (*had, 1)
+        part = line_sums(source, capacity, fine_dev, (cross,), before, send=True)
         got[cross] = lax.ppermute(part, "rows", cross_pairs(cross))
+        if cross == 2:
+            had = line_sums(close, capacity, fine_dev, (1, 3), (*had, 1))
     acc, counts = line_sums(near + [(a, 0) for a in kept_own + given_own], capacity, fine_dev, own)
     hot, digits = tag_hot(
         [more[4], swapped] + kept_own + given_own, capacity, capacity_two, coarse_dev

time: 162 us -> 161 us (level)
  Pallas kernels: 44.8 us -> 41.6 us
  local copies, waits for them, and re-layouts: 13.1 us -> 15.3 us
    unnamed x54 -> x66, local copies, waits for them, and re-layouts: 13.1 us -> 15.3 us
    pallas_call x3, Pallas kernels: 14 us -> 12.2 us  [pack(): pl.pallas_call(functools.partial(pack_body, slots, capacity, tags is not...]
  transfers between devices with their start and end apart: 32 -> 32, of which waited for: 12 -> 13; matrix products, arithmetic and copies ran while one was open for 0% -> 0% of each run, Pallas kernels for 20% -> 18%
where the time goes in v6:
time: 161 us
  starting transfers between devices  53.1 us (33%)
  waiting for transfers between devices  49.8 us (31%)
  Pallas kernels  41.6 us (26%)
  local copies, waits for them, and re-layouts  15.3 us (10%)
    ppermute x23, waiting for transfers between devices, along(): return lax.ppermute(slots, 'rows', line_pairs(step, same_class))  42.1 us
    ppermute x23, starting transfers between devices, along(): return lax.ppermute(slots, 'rows', line_pairs(step, same_class))  37.5 us
    pallas_call x6, Pallas kernels, line_sums(): pl.pallas_call(body, out_shape=out_shape, scratch_shapes=[pltpu.VMEM((LAN...  20.1 us
    unnamed x66, local copies, waits for them, and re-layouts  15.3 us
    pallas_call x3, Pallas kernels, pack(): pl.pallas_call(functools.partial(pack_body, slots, capacity, tags is not...  12.2 us
    ppermute x3, starting transfers between devices, level_step(): pieces.append(lax.ppermute(means, 'grp', back))  6.58 us
    ppermute x3, starting transfers between devices, level_step(): got.append(lax.ppermute(part, 'rows', cross_pairs(cross)))  5.27 us
    ppermute x3, waiting for transfers between devices, level_step(): pieces.append(lax.ppermute(means, 'grp', back))  4.65 us
  transfers between devices with their start and end apart: 32, of which 13 were waited for; matrix products, arithmetic and copies ran while one was open for 0% of the time, Pallas kernels for 18%

profile of v6, /device:TPU:0, one launch (start us, length us, event | category | flops | bytes accessed | tf_op | source)
XLA Modules:
  0.0 160.8 jit_solution(17076418024557877924)
XLA Ops:
  5.5 6.6 %pack_rows.3 = (bf16[1,520,256]{2,1,0:T(8,128)(2,1)S(1)}, bf16[1,520,256]{2,1,0:T(8,128)(2,1)S(1)}, bf16[1,520,256]{2,1,0:T(8,128)(2,1)S(1)}, bf16[4,520,256]{2,...) custom-call(s32[1,32]{1,0:T(1,128)S(1)} %copy-done.7, ...), custom_call_target="tpu_custom_call" | custom-call | bytes 12247040 | tf_op jit(solution)/shard_map/pack_rows/pallas_call | solution.py:152
  20.8 3.6 %pack_rows.5 = bf16[3,520,256]{2,1,0:T(8,128)(2,1)} custom-call(s32[1,32]{1,0:T(1,128)} %counts.5, bf16[8192,256]{1,0:T(8,128)(2,1)} %emb.5, s32[64,128]{1,0:T(8,128)} %bitcast.3), custom_call_target="tpu_custom_call" | custom-call | bytes 1597440 | tf_op jit(solution)/shard_map/pack_rows/pallas_call | solution.py:152
  24.5 3.2 %collective-permute-start.12 = (bf16[3,520,256]{2,1,0:T(8,128)(2,1)}, bf16[3,520,256]{2,1,0:T(8,128)(2,1)S(1)}, u32[]{:S(2)}, u32[]{:S(2)}) collective-permute-start(bf16[3,520,256]{2,1,0:T(8,128)(2,1)} %pack_rows.5), channel_id=1, source_target_pairs={{0,64},{4,20},{8,72},{12,28},{16,80},{20,4},{24,88},{28,12},{32,96... | collective-permute-start | bytes 2396168 | tf_op jit(solution)/shard_map/ppermute | solution.py:542
  32.5 2.6 %collective-permute-start.11 = (bf16[3,520,256]{2,1,0:T(8,128)(2,1)S(1)}, bf16[3,520,256]{2,1,0:T(8,128)(2,1)S(1)}, u32[]{:S(2)}, u32[]{:S(2)}) collective-permute-start(bf16[3,520,256]{2,1,0:T(8,128)(2,1)S(1)} %get-tuple-element.60), channel_id=1, source_target_pairs={{0,96},{4,28},{8,104},{12,4},{16,112},{20,12},{24,120},{28,20},{32... | collective-permute-start | bytes 2396168 | tf_op jit(solution)/shard_map/ppermute | solution.py:542
  35.2 4.8 %collective-permute-done.12.refs_2_ = bf16[3,520,256]{2,1,0:T(8,128)(2,1)S(1)} collective-permute-done((bf16[3,520,256]{2,1,0:T(8,128)(2,1)}, bf16[3,520,256]{2,1,0:T(8,128)(2,1)S(1)}, u32[]{:S(2)}, u32[]{:S(2)}) %collective-permute-start.12) | collective-permute-done | bytes 798752 | tf_op jit(solution)/shard_map/ppermute | solution.py:542
  39.9 3.9 %collective-permute-start.9 = (bf16[2,520,256]{2,1,0:T(8,128)(2,1)S(1)}, bf16[2,520,256]{2,1,0:T(8,128)(2,1)S(1)}, u32[]{:S(2)}, u32[]{:S(2)}) collective-permute-start(bf16[2,520,256]{2,1,0:T(8,128)(2,1)S(1)} %copy-done.10), channel_id=1, source_target_pairs={{0,28},{4,96},{8,4},{12,104},{16,12},{20,112},{24,20},{28,120},{32... | collective-permute-start | bytes 1597448 | tf_op jit(solution)/shard_map/ppermute | solution.py:542
  43.8 5.7 %line_sums.7 = (f32[3,2048,256]{2,1,0:T(8,128)S(1)}, f32[3,16,128]{2,1,0:T(8,128)S(1)}) custom-call(bf16[4,520,256]{2,1,0:T(8,128)(2,1)S(1)} %get-tuple-element.44.refs_0_, bf16[4,520,256]{2,1,0:T(8,128)(2,1)S(1)} %collective-permute-done.refs_1_, bf16[3,520,256]{2,1,0:T(8,128)(2,1)S(1)} %collective-permute-done.12.refs_2_), custom_call_target="tpu_custom_call" | custom-call | flops 4831838208 | bytes 14979072 | tf_op jit(solution)/shard_map/line_sums/pallas_call | solution.py:271
  49.5 8.1 %collective-permute-done.10.refs_0_ = bf16[3,520,256]{2,1,0:T(8,128)(2,1)S(1)} collective-permute-done((bf16[3,520,256]{2,1,0:T(8,128)(2,1)S(1)}, bf16[3,520,256]{2,1,0:T(8,128)(2,1)S(1)}, u32[]{:S(2)}, u32[]{:S(2)}) %collective-permute-start.10) | collective-permute-done | bytes 798752 | tf_op jit(solution)/shard_map/ppermute | solution.py:542
  57.7 3.8 %collective-permute-start.1 = (bf16[1,520,256]{2,1,0:T(8,128)(2,1)S(1)}, bf16[1,520,256]{2,1,0:T(8,128)(2,1)S(1)}, u32[]{:S(2)}, u32[]{:S(2)}) collective-permute-start(bf16[1,520,256]{2,1,0:T(8,128)(2,1)S(1)} %copy-done.26), channel_id=1, source_target_pairs={{0,64},{4,20},{8,72},{12,28},{16,80},{20,4},{24,88},{28,12},{32,96... | collective-permute-start | bytes 798728 | tf_op jit(solution)/shard_map/ppermute | solution.py:542
  61.5 2.7 %line_sums.8 = (f32[2,2048,256]{2,1,0:T(8,128)S(1)}, f32[2,16,128]{2,1,0:T(8,128)S(1)}) custom-call(bf16[3,520,256]{2,1,0:T(8,128)(2,1)S(1)} %collective-permute-done.10.refs_0_, bf16[3,520,256]{2,1,0:T(8,128)(2,1)S(1)} %collective-permute-done.11.refs_1_, f32[3,2048,256]{2,1,0:T(8,128)S(1)} %get-tuple-element.61.refs_2_.refs_5_, ...), custom_call_target="tpu_custom_call" | custom-call | flops 2147483648 | bytes 9453568 | tf_op jit(solution)/shard_map/line_sums/pallas_call | solution.py:271
  64.7 3.1 %collective-permute-start.15 = (bf16[1,520,256]{2,1,0:T(8,128)(2,1)S(1)}, bf16[1,520,256]{2,1,0:T(8,128)(2,1)S(1)}, u32[]{:S(2)}, u32[]{:S(2)}) collective-permute-start(bf16[1,520,256]{2,1,0:T(8,128)(2,1)S(1)} %copy-done.30), channel_id=1, source_target_pairs={{0,12},{4,32},{8,20},{12,40},{16,28},{20,48},{24,4},{28,56},{32,44... | collective-permute-start | bytes 798728 | tf_op jit(solution)/shard_map/ppermute | solution.py:542
  74.8 3.0 %collective-permute-start.18 = (bf16[2064,256]{1,0:T(8,128)(2,1)S(1)}, bf16[2064,256]{1,0:T(8,128)(2,1)S(1)}, u32[]{:S(2)}, u32[]{:S(2)}) collective-permute-start(bf16[2064,256]{1,0:T(8,128)(2,1)S(1)} %line_sums.11), channel_id=1, source_target_pairs={{0,24},{4,100},{8,0},{12,108},{16,8},{20,116},{24,16},{28,124},{32... | collective-permute-start | bytes 3170312 | tf_op jit(solution)/shard_map/ppermute | solution.py:580
  77.8 3.1 %line_sums.10 = bf16[2064,256]{1,0:T(8,128)(2,1)S(1)} custom-call(bf16[3,520,256]{2,1,0:T(8,128)(2,1)S(1)} %collective-permute-done.10.refs_0_, bf16[3,520,256]{2,1,0:T(8,128)(2,1)S(1)} %collective-permute-done.11.refs_1_, bf16[1,520,256]{2,1,0:T(8,128)(2,1)S(1)} %collective-permute-done.14.refs_2_, ...), custom_call_target="tpu_custom_call" | custom-call | flops 2684354560 | bytes 5525504 | tf_op jit(solution)/shard_map/line_sums/pallas_call | solution.py:271
  84.1 6.8 %collective-permute-done.3.refs_4_ = bf16[1,520,256]{2,1,0:T(8,128)(2,1)S(1)} collective-permute-done((bf16[1,520,256]{2,1,0:T(8,128)(2,1)S(1)}, bf16[1,520,256]{2,1,0:T(8,128)(2,1)S(1)}, u32[]{:S(2)}, u32[]{:S(2)}) %collective-permute-start.3) | collective-permute-done | bytes 266272 | tf_op jit(solution)/shard_map/ppermute | solution.py:542
  90.9 11.7 %collective-permute-done.4.refs_5_ = bf16[1,520,256]{2,1,0:T(8,128)(2,1)S(1)} collective-permute-done((bf16[1,520,256]{2,1,0:T(8,128)(2,1)S(1)}, bf16[1,520,256]{2,1,0:T(8,128)(2,1)S(1)}, u32[]{:S(2)}, u32[]{:S(2)}) %collective-permute-start.4) | collective-permute-done | bytes 266272 | tf_op jit(solution)/shard_map/ppermute | solution.py:542
  102.7 6.3 %collective-permute-start.6 = (bf16[1,520,256]{2,1,0:T(8,128)(2,1)S(1)}, bf16[1,520,256]{2,1,0:T(8,128)(2,1)S(1)}, u32[]{:S(2)}, u32[]{:S(2)}) collective-permute-start(bf16[1,520,256]{2,1,0:T(8,128)(2,1)S(1)} %copy-done.16), channel_id=1, source_target_pairs={{0,28},{4,96},{8,4},{12,104},{16,12},{20,112},{24,20},{28,120},{32... | collective-permute-start | bytes 798728 | tf_op jit(solution)/shard_map/ppermute | solution.py:542
  109.0 3.9 %collective-permute-done.6.refs_7_ = bf16[1,520,256]{2,1,0:T(8,128)(2,1)S(1)} collective-permute-done((bf16[1,520,256]{2,1,0:T(8,128)(2,1)S(1)}, bf16[1,520,256]{2,1,0:T(8,128)(2,1)S(1)}, u32[]{:S(2)}, u32[]{:S(2)}) %collective-permute-start.6) | collective-permute-done | bytes 266272 | tf_op jit(solution)/shard_map/ppermute | solution.py:542
  112.9 4.8 %line_sums.6 = (f32[1,2048,256]{2,1,0:T(8,128)S(1)}, f32[1,16,128]{2,1,0:T(8,128)S(1)}) custom-call(bf16[4,520,256]{2,1,0:T(8,128)(2,1)S(1)} %get-tuple-element.44.refs_0_, bf16[4,520,256]{2,1,0:T(8,128)(2,1)S(1)} %collective-permute-done.refs_1_, bf16[1,520,256]{2,1,0:T(8,128)(2,1)S(1)} %collective-permute-done.1.refs_2_, ...), custom_call_target="tpu_custom_call" | custom-call | flops 4294967296 | bytes 6324224 | tf_op jit(solution)/shard_map/line_sums/pallas_call | solution.py:271
  117.7 2.8 %new_fine.1 = (bf16[2048,256]{1,0:T(8,128)(2,1)}, bf16[2048,256]{1,0:T(8,128)(2,1)S(1)}, bf16[4,128,256]{2,1,0:T(8,128)(2,1)S(1)}, bf16[4,128,256]{2,1,0:T(8,128)(2,1)S(1)}, bf16[4,128,256]{2,1,0:T(8,128)(2,1)S(1)}) custom-call(f32[1,2048,256]{2,1,0:T(8,128)S(1)} %get-tuple-element.52.acc, f32[1,16,128]{2,1,0:T(8,128)S(1)} %get-tuple-element.53.counts, ...), custom_call_target="tpu_custom_call" | custom-call | tf_op jit(solution)/shard_map/new_fine/pallas_call | solution.py:319
  133.9 2.5 %collective-permute-done.23.refs_5_ = bf16[4,128,256]{2,1,0:T(8,128)(2,1)S(1)} collective-permute-done((bf16[4,128,256]{2,1,0:T(8,128)(2,1)S(1)}, bf16[4,128,256]{2,1,0:T(8,128)(2,1)S(1)}, u32[]{:S(2)}, u32[]{:S(2)}) %collective-permute-start.23) | collective-permute-done | bytes 262176 | tf_op jit(solution)/shard_map/ppermute | solution.py:542
  136.4 2.7 %collective-permute-done.24.refs_6_ = bf16[4,128,256]{2,1,0:T(8,128)(2,1)S(1)} collective-permute-done((bf16[4,128,256]{2,1,0:T(8,128)(2,1)S(1)}, bf16[4,128,256]{2,1,0:T(8,128)(2,1)S(1)}, u32[]{:S(2)}, u32[]{:S(2)}) %collective-permute-start.24) | collective-permute-done | bytes 262176 | tf_op jit(solution)/shard_map/ppermute | solution.py:542
  142.1 3.0 %collective-permute-start.28 = (bf16[272,256]{1,0:T(8,128)(2,1)S(1)}, bf16[272,256]{1,0:T(8,128)(2,1)S(1)}, u32[]{:S(2)}, u32[]{:S(2)}) collective-permute-start(bf16[272,256]{1,0:T(8,128)(2,1)S(1)} %get-tuple-element.83), channel_id=1, source_target_pairs={{0,24},{4,100},{8,0},{12,108},{16,8},{20,116},{24,16},{28,124},{32... | collective-permute-start | bytes 417800 | tf_op jit(solution)/shard_map/ppermute | solution.py:607
  150.4 3.6 %collective-permute-start.30 = (bf16[256,256]{1,0:T(8,128)(2,1)S(1)}, bf16[256,256]{1,0:T(8,128)(2,1)S(1)}, u32[]{:S(2)}, u32[]{:S(2)}) collective-permute-start(bf16[256,256]{1,0:T(8,128)(2,1)S(1)} %coarse_means.1.refs_0_), channel_id=1, source_target_pairs={{2,0},{3,1},{0,2},{1,3},{6,4},{7,5},{4,6},{5,7},{10,8},{11,9},{8,1... | collective-permute-start | bytes 393224 | tf_op jit(solution)/shard_map/ppermute | solution.py:612
  156.0 3.7 %collective-permute-done.30.refs_2_ = bf16[256,256]{1,0:T(8,128)(2,1)S(1)} collective-permute-done((bf16[256,256]{1,0:T(8,128)(2,1)S(1)}, bf16[256,256]{1,0:T(8,128)(2,1)S(1)}, u32[]{:S(2)}, u32[]{:S(2)}) %collective-permute-start.30) | collective-permute-done | bytes 131104 | tf_op jit(solution)/shard_map/ppermute | solution.py:612
  (123 shorter events, 53.8 us)
Async XLA Ops:
  20.8 19.1 %collective-permute-start = (bf16[4,520,256]{2,1,0:T(8,128)(2,1)}, bf16[4,520,256]{2,1,0:T(8,128)(2,1)S(1)}, u32[]{:S(2)}, u32[]{:S(2)}) collective-permute-start(bf16[4,520,256]{2,1,0:T(8,128)(2,1)} %get-tuple-element.45), channel_id=1, source_target_pairs={{0,4},{4,0},{8,12},{12,8},{16,20},{20,16},{24,28},{28,24},{32,36},... | collective-permute-start | bytes 3194888 | tf_op jit(solution)/shard_map/ppermute | solution.py:542
  24.5 15.5 %collective-permute-start.12 = (bf16[3,520,256]{2,1,0:T(8,128)(2,1)}, bf16[3,520,256]{2,1,0:T(8,128)(2,1)S(1)}, u32[]{:S(2)}, u32[]{:S(2)}) collective-permute-start(bf16[3,520,256]{2,1,0:T(8,128)(2,1)} %pack_rows.5), channel_id=1, source_target_pairs={{0,64},{4,20},{8,72},{12,28},{16,80},{20,4},{24,88},{28,12},{32,96... | collective-permute-start | bytes 2396168 | tf_op jit(solution)/shard_map/ppermute | solution.py:542
  31.8 25.8 %collective-permute-start.10 = (bf16[3,520,256]{2,1,0:T(8,128)(2,1)S(1)}, bf16[3,520,256]{2,1,0:T(8,128)(2,1)S(1)}, u32[]{:S(2)}, u32[]{:S(2)}) collective-permute-start(bf16[3,520,256]{2,1,0:T(8,128)(2,1)S(1)} %get-tuple-element.59), channel_id=1, source_target_pairs={{0,32},{4,12},{8,40},{12,20},{16,48},{20,28},{24,56},{28,4},{32,64... | collective-permute-start | bytes 2396168 | tf_op jit(solution)/shard_map/ppermute | solution.py:542
  32.5 29.0 %collective-permute-start.11 = (bf16[3,520,256]{2,1,0:T(8,128)(2,1)S(1)}, bf16[3,520,256]{2,1,0:T(8,128)(2,1)S(1)}, u32[]{:S(2)}, u32[]{:S(2)}) collective-permute-start(bf16[3,520,256]{2,1,0:T(8,128)(2,1)S(1)} %get-tuple-element.60), channel_id=1, source_target_pairs={{0,96},{4,28},{8,104},{12,4},{16,112},{20,12},{24,120},{28,20},{32... | collective-permute-start | bytes 2396168 | tf_op jit(solution)/shard_map/ppermute | solution.py:542
  35.2 29.1 %collective-permute-start.7 = (bf16[2,520,256]{2,1,0:T(8,128)(2,1)S(1)}, bf16[2,520,256]{2,1,0:T(8,128)(2,1)S(1)}, u32[]{:S(2)}, u32[]{:S(2)}) collective-permute-start(bf16[2,520,256]{2,1,0:T(8,128)(2,1)S(1)} %copy-done.14), channel_id=1, source_target_pairs={{0,20},{4,64},{8,28},{12,72},{16,4},{20,80},{24,12},{28,88},{32,52... | collective-permute-start | bytes 1597448 | tf_op jit(solution)/shard_map/ppermute | solution.py:542
  39.9 24.8 %collective-permute-start.8 = (bf16[2,520,256]{2,1,0:T(8,128)(2,1)S(1)}, bf16[2,520,256]{2,1,0:T(8,128)(2,1)S(1)}, u32[]{:S(2)}, u32[]{:S(2)}) collective-permute-start(bf16[2,520,256]{2,1,0:T(8,128)(2,1)S(1)} %copy-done.12), channel_id=1, source_target_pairs={{0,12},{4,32},{8,20},{12,40},{16,28},{20,48},{24,4},{28,56},{32,44... | collective-permute-start | bytes 1597448 | tf_op jit(solution)/shard_map/ppermute | solution.py:542
  39.9 27.9 %collective-permute-start.9 = (bf16[2,520,256]{2,1,0:T(8,128)(2,1)S(1)}, bf16[2,520,256]{2,1,0:T(8,128)(2,1)S(1)}, u32[]{:S(2)}, u32[]{:S(2)}) collective-permute-start(bf16[2,520,256]{2,1,0:T(8,128)(2,1)S(1)} %copy-done.10), channel_id=1, source_target_pairs={{0,28},{4,96},{8,4},{12,104},{16,12},{20,112},{24,20},{28,120},{32... | collective-permute-start | bytes 1597448 | tf_op jit(solution)/shard_map/ppermute | solution.py:542
  57.7 24.0 %collective-permute-start.1 = (bf16[1,520,256]{2,1,0:T(8,128)(2,1)S(1)}, bf16[1,520,256]{2,1,0:T(8,128)(2,1)S(1)}, u32[]{:S(2)}, u32[]{:S(2)}) collective-permute-start(bf16[1,520,256]{2,1,0:T(8,128)(2,1)S(1)} %copy-done.26), channel_id=1, source_target_pairs={{0,64},{4,20},{8,72},{12,28},{16,80},{20,4},{24,88},{28,12},{32,96... | collective-permute-start | bytes 798728 | tf_op jit(solution)/shard_map/ppermute | solution.py:542
  61.5 22.6 %collective-permute-start.2 = (bf16[1,520,256]{2,1,0:T(8,128)(2,1)S(1)}, bf16[1,520,256]{2,1,0:T(8,128)(2,1)S(1)}, u32[]{:S(2)}, u32[]{:S(2)}) collective-permute-start(bf16[1,520,256]{2,1,0:T(8,128)(2,1)S(1)} %copy-done.24), channel_id=1, source_target_pairs={{0,32},{4,12},{8,40},{12,20},{16,48},{20,28},{24,56},{28,4},{32,64... | collective-permute-start | bytes 798728 | tf_op jit(solution)/shard_map/ppermute | solution.py:542
  64.2 9.1 %collective-permute-start.14 = (bf16[1,520,256]{2,1,0:T(8,128)(2,1)S(1)}, bf16[1,520,256]{2,1,0:T(8,128)(2,1)S(1)}, u32[]{:S(2)}, u32[]{:S(2)}) collective-permute-start(bf16[1,520,256]{2,1,0:T(8,128)(2,1)S(1)} %copy-done.32), channel_id=1, source_target_pairs={{0,20},{4,64},{8,28},{12,72},{16,4},{20,80},{24,12},{28,88},{32,52... | collective-permute-start | bytes 798728 | tf_op jit(solution)/shard_map/ppermute | solution.py:542
  64.7 10.1 %collective-permute-start.15 = (bf16[1,520,256]{2,1,0:T(8,128)(2,1)S(1)}, bf16[1,520,256]{2,1,0:T(8,128)(2,1)S(1)}, u32[]{:S(2)}, u32[]{:S(2)}) collective-permute-start(bf16[1,520,256]{2,1,0:T(8,128)(2,1)S(1)} %copy-done.30), channel_id=1, source_target_pairs={{0,12},{4,32},{8,20},{12,40},{16,28},{20,48},{24,4},{28,56},{32,44... | collective-permute-start | bytes 798728 | tf_op jit(solution)/shard_map/ppermute | solution.py:542
  67.8 10.0 %collective-permute-start.16 = (bf16[1,520,256]{2,1,0:T(8,128)(2,1)S(1)}, bf16[1,520,256]{2,1,0:T(8,128)(2,1)S(1)}, u32[]{:S(2)}, u32[]{:S(2)}) collective-permute-start(bf16[1,520,256]{2,1,0:T(8,128)(2,1)S(1)} %copy-done.28), channel_id=1, source_target_pairs={{0,28},{4,96},{8,4},{12,104},{16,12},{20,112},{24,20},{28,120},{32... | collective-permute-start | bytes 798728 | tf_op jit(solution)/shard_map/ppermute | solution.py:542
  73.4 44.3 %collective-permute-start.13 = (bf16[2064,256]{1,0:T(8,128)(2,1)S(1)}, bf16[2064,256]{1,0:T(8,128)(2,1)S(1)}, u32[]{:S(2)}, u32[]{:S(2)}) collective-permute-start(bf16[2064,256]{1,0:T(8,128)(2,1)S(1)} %line_sums.9), channel_id=1, source_target_pairs={{0,8},{4,36},{8,16},{12,44},{16,24},{20,52},{24,0},{28,60},{32,40}... | collective-permute-start | bytes 3170312 | tf_op jit(solution)/shard_map/ppermute | solution.py:580
  74.8 42.9 %collective-permute-start.18 = (bf16[2064,256]{1,0:T(8,128)(2,1)S(1)}, bf16[2064,256]{1,0:T(8,128)(2,1)S(1)}, u32[]{:S(2)}, u32[]{:S(2)}) collective-permute-start(bf16[2064,256]{1,0:T(8,128)(2,1)S(1)} %line_sums.11), channel_id=1, source_target_pairs={{0,24},{4,100},{8,0},{12,108},{16,8},{20,116},{24,16},{28,124},{32... | collective-permute-start | bytes 3170312 | tf_op jit(solution)/shard_map/ppermute | solution.py:580
  80.9 36.7 %collective-permute-start.17 = (bf16[2064,256]{1,0:T(8,128)(2,1)S(1)}, bf16[2064,256]{1,0:T(8,128)(2,1)S(1)}, u32[]{:S(2)}, u32[]{:S(2)}) collective-permute-start(bf16[2064,256]{1,0:T(8,128)(2,1)S(1)} %line_sums.10), channel_id=1, source_target_pairs={{0,16},{4,68},{8,24},{12,76},{16,0},{20,84},{24,8},{28,92},{32,48}... | collective-permute-start | bytes 3170312 | tf_op jit(solution)/shard_map/ppermute | solution.py:580
  81.7 9.3 %collective-permute-start.3 = (bf16[1,520,256]{2,1,0:T(8,128)(2,1)S(1)}, bf16[1,520,256]{2,1,0:T(8,128)(2,1)S(1)}, u32[]{:S(2)}, u32[]{:S(2)}) collective-permute-start(bf16[1,520,256]{2,1,0:T(8,128)(2,1)S(1)} %copy-done.22), channel_id=1, source_target_pairs={{0,96},{4,28},{8,104},{12,4},{16,112},{20,12},{24,120},{28,20},{32... | collective-permute-start | bytes 798728 | tf_op jit(solution)/shard_map/ppermute | solution.py:542
  84.1 18.6 %collective-permute-start.4 = (bf16[1,520,256]{2,1,0:T(8,128)(2,1)S(1)}, bf16[1,520,256]{2,1,0:T(8,128)(2,1)S(1)}, u32[]{:S(2)}, u32[]{:S(2)}) collective-permute-start(bf16[1,520,256]{2,1,0:T(8,128)(2,1)S(1)} %copy-done.20), channel_id=1, source_target_pairs={{0,20},{4,64},{8,28},{12,72},{16,4},{20,80},{24,12},{28,88},{32,52... | collective-permute-start | bytes 798728 | tf_op jit(solution)/shard_map/ppermute | solution.py:542
  90.9 18.0 %collective-permute-start.5 = (bf16[1,520,256]{2,1,0:T(8,128)(2,1)S(1)}, bf16[1,520,256]{2,1,0:T(8,128)(2,1)S(1)}, u32[]{:S(2)}, u32[]{:S(2)}) collective-permute-start(bf16[1,520,256]{2,1,0:T(8,128)(2,1)S(1)} %copy-done.18), channel_id=1, source_target_pairs={{0,12},{4,32},{8,20},{12,40},{16,28},{20,48},{24,4},{28,56},{32,44... | collective-permute-start | bytes 798728 | tf_op jit(solution)/shard_map/ppermute | solution.py:542
  102.7 10.2 %collective-permute-start.6 = (bf16[1,520,256]{2,1,0:T(8,128)(2,1)S(1)}, bf16[1,520,256]{2,1,0:T(8,128)(2,1)S(1)}, u32[]{:S(2)}, u32[]{:S(2)}) collective-permute-start(bf16[1,520,256]{2,1,0:T(8,128)(2,1)S(1)} %copy-done.16), channel_id=1, source_target_pairs={{0,28},{4,96},{8,4},{12,104},{16,12},{20,112},{24,20},{28,120},{32... | collective-permute-start | bytes 798728 | tf_op jit(solution)/shard_map/ppermute | solution.py:542
  120.5 10.5 %collective-permute-start.20 = (bf16[4,128,256]{2,1,0:T(8,128)(2,1)S(1)}, bf16[4,128,256]{2,1,0:T(8,128)(2,1)S(1)}, u32[]{:S(2)}, u32[]{:S(2)}) collective-permute-start(bf16[4,128,256]{2,1,0:T(8,128)(2,1)S(1)} %get-tuple-element.72), channel_id=1, source_target_pairs={{0,64},{4,20},{8,72},{12,28},{16,80},{20,4},{24,88},{28,12},{32,96... | collective-permute-start | bytes 786440 | tf_op jit(solution)/shard_map/ppermute | solution.py:542
  122.5 8.7 %collective-permute-start.21 = (bf16[4,128,256]{2,1,0:T(8,128)(2,1)S(1)}, bf16[4,128,256]{2,1,0:T(8,128)(2,1)S(1)}, u32[]{:S(2)}, u32[]{:S(2)}) collective-permute-start(bf16[4,128,256]{2,1,0:T(8,128)(2,1)S(1)} %get-tuple-element.73), channel_id=1, source_target_pairs={{0,32},{4,12},{8,40},{12,20},{16,48},{20,28},{24,56},{28,4},{32,64... | collective-permute-start | bytes 786440 | tf_op jit(solution)/shard_map/ppermute | solution.py:542
  124.6 9.2 %collective-permute-start.22 = (bf16[4,128,256]{2,1,0:T(8,128)(2,1)S(1)}, bf16[4,128,256]{2,1,0:T(8,128)(2,1)S(1)}, u32[]{:S(2)}, u32[]{:S(2)}) collective-permute-start(bf16[4,128,256]{2,1,0:T(8,128)(2,1)S(1)} %get-tuple-element.74), channel_id=1, source_target_pairs={{0,96},{4,28},{8,104},{12,4},{16,112},{20,12},{24,120},{28,20},{32... | collective-permute-start | bytes 786440 | tf_op jit(solution)/shard_map/ppermute | solution.py:542
  131.0 8.0 %collective-permute-start.24 = (bf16[4,128,256]{2,1,0:T(8,128)(2,1)S(1)}, bf16[4,128,256]{2,1,0:T(8,128)(2,1)S(1)}, u32[]{:S(2)}, u32[]{:S(2)}) collective-permute-start(bf16[4,128,256]{2,1,0:T(8,128)(2,1)S(1)} %get-tuple-element.76), channel_id=1, source_target_pairs={{0,12},{4,32},{8,20},{12,40},{16,28},{20,48},{24,4},{28,56},{32,44... | collective-permute-start | bytes 786440 | tf_op jit(solution)/shard_map/ppermute | solution.py:542
  150.4 9.2 %collective-permute-start.30 = (bf16[256,256]{1,0:T(8,128)(2,1)S(1)}, bf16[256,256]{1,0:T(8,128)(2,1)S(1)}, u32[]{:S(2)}, u32[]{:S(2)}) collective-permute-start(bf16[256,256]{1,0:T(8,128)(2,1)S(1)} %coarse_means.1.refs_0_), channel_id=1, source_target_pairs={{2,0},{3,1},{0,2},{1,3},{6,4},{7,5},{4,6},{5,7},{10,8},{11,9},{8,1... | collective-permute-start | bytes 393224 | tf_op jit(solution)/shard_map/ppermute | solution.py:612
  (41 other events, 242.5 us)
